TPU v7x, 512 devices: a whole 4x8x8 slice. The times are simulated.
512 devices in a mesh: row: 64 (over x, z, core), blk: 8 (over y).
Axes of the slice: x: 4, y: 8, z: 8, core: 2. Of those that a mesh axis runs over, the one named last changes fastest.
Arguments:
- factor_panel: bfloat16 [131072, 2, 2048], P('row', None, 'blk'), may hold values from -0.09375 to 0.09375
- right_side: float32 [256, 131072], P('blk', 'row'), may hold values from -6 to 6
- block_inverse: float32 [2, 2048, 2048], P(None, 'row', 'blk'), may hold values from -2 to 2, as said below
Outputs:
- solved: float32 [2, 256, 2048], P(None, 'blk', 'row')
- reduced_side: float32 [256, 131072], P('blk', 'row')
Inputs may be any that keep to these rules, and one draw needn't show every extreme that they name: block_inverse[k] is lower triangular with diagonal entries between 1 and 2.
All inputs are finite; a program needn't handle non-finite values.
Results may differ from a plain program's by a relative error of at most 0.015.
Values may be sent and summed in bfloat16 or wider, within the bound.
No kernel may reach another device: no remote copies, remote signals or barrier semaphores. Data moves between devices by JAX's collectives and lax.ppermute only.
A program may use at most 64 MiB of HBM per device.

v0:
```python
import jax
import jax.numpy as jnp
from jax import lax
from jax.sharding import Mesh, PartitionSpec as P


STEPS = 2
NX, NZ, NC = 4, 8, 2
HALF = jnp.bfloat16
WIDE = jnp.float32


def swap_blocks(array, axis):
    return lax.all_to_all(array, axis, split_axis=0, concat_axis=0, tiled=True)


def gather_by_swap(array, axis, count):
    return swap_blocks(jnp.broadcast_to(array[None], (count, *array.shape)), axis)


def product(left, right):
    return lax.dot_general(left, right, (((1,), (1,)), ((), ())), preferred_element_type=WIDE)


def scatter_sum(partial, blocks):
    t, wide = partial.shape
    split = partial.astype(HALF).reshape(t, blocks, wide // blocks).transpose(1, 0, 2)
    return jnp.sum(swap_blocks(split, "blk").astype(WIDE), axis=0)


def local(factor_panel, right_side, block_inverse):
    x = lax.axis_index("x")
    z = lax.axis_index("z")
    core = lax.axis_index("core")
    blk = lax.axis_index("blk")
    row = (x * NZ + z) * NC + core
    n_blk = right_side.shape[1] // factor_panel.shape[2]
    pixels, _, width = factor_panel.shape
    dates_local = right_side.shape[0]
    dates_x = dates_local // NX
    t = dates_x * n_blk
    rows_local = block_inverse.shape[1]
    per_blk = width // rows_local
    half = width // NC

    pivot = right_side.astype(HALF).reshape(NX, dates_x, pixels)
    mine = jnp.where(x == 0, pivot[0], jnp.zeros_like(pivot[0]))
    for k in range(1, NX):
        mine = mine + lax.ppermute(pivot[k], ("x", "z"), [(0, k * NZ)])

    inverse = gather_by_swap(block_inverse.astype(HALF), "x", NX)
    planes = [inverse] + [lax.ppermute(inverse, "z", [(k, 0)]) for k in range(1, NZ)]
    inverse = jnp.stack(planes).transpose(2, 1, 0, 3, 4)
    inverse = inverse.reshape(STEPS, NX * NZ * rows_local, width)

    pivot = swap_blocks(mine.reshape(dates_x, n_blk, width).transpose(1, 0, 2), "blk")
    pivot = lax.all_gather(pivot.reshape(t, width), "core", axis=0, tiled=False)

    panels = factor_panel.transpose(1, 0, 2)
    halves = panels[0].reshape(n_blk, NC, half, width)
    sent = lax.ppermute(halves[:, 0], ("x", "z", "core"), [(1, 0)])
    lower = jnp.where(core == 1, halves[:, 1], sent)
    cross = jnp.where((x == 0) & (z == 0), lower, jnp.zeros_like(lower))
    for k in range(1, NX):
        cross = cross + lax.ppermute(lower, ("x", "z"), [(0, k * NZ)])
    cross = cross.reshape(n_blk * half, width)

    place = jnp.arange(width)
    c_of, q_of, i_of = place // half, place % half // rows_local, place % rows_local
    natural = (q_of * NC + c_of) * rows_local + i_of
    order = (natural[:, None] == place[None, :]).astype(HALF)

    def ordered(value):
        return jnp.dot(value, order, preferred_element_type=WIDE).astype(HALF)

    def both_cores(value):
        pair = lax.all_gather(value, "core", axis=0, tiled=False)
        return jnp.concatenate([pair[0], pair[1]], axis=-1)

    first = scatter_sum(product(pivot[0], inverse[0]), n_blk).astype(HALF)
    first, panels = lax.optimization_barrier((first, panels))
    update = scatter_sum(product(ordered(both_cores(first)), cross), n_blk)
    reduced = pivot[1].astype(WIDE) - both_cores(update)
    second = scatter_sum(product(reduced.astype(HALF), inverse[1]), n_blk).astype(HALF)

    solved = jnp.stack([first, second])
    spread = jnp.where(z == 0, solved, jnp.zeros_like(solved))
    for k in range(1, NZ):
        spread = spread + lax.ppermute(solved, "z", [(0, k)])
    spread = ordered(both_cores(gather_by_swap(spread, "x", NX)))
    spread = spread.reshape(NX, STEPS, n_blk, dates_x, width).transpose(2, 0, 3, 1, 4)
    spread = spread.reshape(dates_local * n_blk, STEPS * width)

    panel = jnp.concatenate(
        [
            jnp.where(row > k, panels[k], jnp.zeros((), HALF))
            for k in range(STEPS)
        ],
        axis=1,
    )
    extra = 128
    pick = jnp.arange(extra)
    at = pick // rows_local * width + row % per_blk * rows_local + pick % rows_local
    wanted = (pick < STEPS * rows_local) & (row // per_blk == blk)
    select = wanted[:, None] & (at[:, None] == jnp.arange(STEPS * width)[None, :])
    panel = jnp.concatenate([panel, select.astype(HALF)], axis=0)

    total = product(spread, panel).astype(HALF)
    lanes, rows8 = 128, 8
    total = total.reshape(n_blk * dates_local // rows8, rows8, -1, lanes).transpose(0, 2, 1, 3)
    total = swap_blocks(total.reshape(n_blk, -1, lanes), "blk")
    total = jnp.sum(total.astype(WIDE), axis=0)
    total = total.reshape(dates_local // rows8, -1, rows8, lanes).transpose(0, 2, 1, 3)
    total = total.reshape(dates_local, pixels + extra)
    answer = total[:, pixels : pixels + STEPS * rows_local]
    answer = answer.reshape(dates_local, STEPS, rows_local).transpose(1, 0, 2)
    return (answer, right_side - total[:, :pixels])


def solution(mesh):
    shape = (NX, NZ, NC, mesh.shape["blk"])
    fine = Mesh(mesh.devices.reshape(shape), ("x", "z", "core", "blk"))
    row = ("x", "z", "core")
    return jax.shard_map(
        local,
        mesh=fine,
        in_specs=(P(row, None, "blk"), P("blk", row), P(None, row, "blk")),
        out_specs=(P(None, "blk", row), P("blk", row)),
        check_vma=False,
    )
```

profile of v0, /device:TPU:1, one launch (start us, length us, event | category | flops | bytes accessed | tf_op | source)
XLA Modules:
  0.0 178.5 jit_solution(10975864316071418845)
XLA Ops:
  1.6 3.9 %collective-permute-start = (bf16[8,2048]{1,0:T(8,128)(2,1)S(1)}, bf16[8,2048]{1,0:T(8,128)(2,1)S(1)}, u32[]{:S(2)}, u32[]{:S(2)}) collective-permute-start(bf16[8,2048]{1,0:T(8,128)(2,1)S(1)} %get-tuple-element.12), channel_id=1, source_target_pairs={{0,128},{1,129},{2,130},{3,131},{4,132},{5,133},{6,134},{7,135},{8... | collective-permute-start | bytes 98312 | tf_op jit(solution)/shard_map/ppermute | solution.py:49
  5.6 2.2 %collective-permute-start.1 = (bf16[8,2048]{1,0:T(8,128)(2,1)S(1)}, bf16[8,2048]{1,0:T(8,128)(2,1)S(1)}, u32[]{:S(2)}, u32[]{:S(2)}) collective-permute-start(bf16[8,2048]{1,0:T(8,128)(2,1)S(1)} %get-tuple-element.14), channel_id=1, source_target_pairs={{0,256},{1,257},{2,258},{3,259},{4,260},{5,261},{6,262},{7,263},{8... | collective-permute-start | bytes 98312 | tf_op jit(solution)/shard_map/ppermute | solution.py:49
  10.7 6.8 %all-to-all-start = ((bf16[8,8,256]{2,1,0:T(8,128)(2,1)}), bf16[8,8,256]{2,1,0:T(8,128)(2,1)S(1)}, u32[]{:S(2)}, u32[]{:S(2)}) async-start(bf16[8,8,256]{2,1,0:T(8,128)(2,1)} %bitcast.1), calls=%async_computation | async-start | bytes 65536 | tf_op jit(solution)/shard_map/all_to_all | solution.py:14
  18.4 1.9 %copy.47 = bf16[2048,2,256]{2,0,1:T(8,128)(2,1)S(1)} copy(bf16[2048,2,256]{2,1,0:T(2,128)(2,1)} %param.3) | data formatting | bytes 4194304 | tf_op args[0]
  20.3 4.1 %all-to-all-done = bf16[8,8,256]{2,1,0:T(8,128)(2,1)S(1)} async-done(((bf16[8,8,256]{2,1,0:T(8,128)(2,1)}), bf16[8,8,256]{2,1,0:T(8,128)(2,1)S(1)}, u32[]{:S(2)}, u32[]{:S(2)}) %all-to-all-start) | async-done | bytes 32800 | tf_op jit(solution)/shard_map/all_to_all | solution.py:14
  25.1 4.2 %all-to-all-start.1 = ((bf16[4,2,32,256]{3,2,1,0:T(8,128)(2,1)}), bf16[4,2,32,256]{3,2,1,0:T(8,128)(2,1)S(1)}, u32[]{:S(2)}, u32[]{:S(2)}) async-start(bf16[4,2,32,256]{3,2,1,0:T(8,128)(2,1)} %broadcast_in_dim.16), calls=%async_computation.1 | async-start | bytes 262144 | tf_op jit(solution)/shard_map/all_to_all | solution.py:14
  30.1 6.2 %collective-permute-start.10 = (bf16[8,128,256]{2,1,0:T(8,128)(2,1)}, bf16[8,128,256]{2,1,0:T(8,128)(2,1)}, u32[]{:S(2)}, u32[]{:S(2)}) collective-permute-start(bf16[8,128,256]{2,1,0:T(8,128)(2,1)} %slice_bitcast_fusion), channel_id=1, source_target_pairs={{8,0},{9,1},{10,2},{11,3},{12,4},{13,5},{14,6},{15,7}} | collective-permute-start | bytes 1572872 | tf_op jit(solution)/shard_map/ppermute | solution.py:61
  36.4 1.8 %all_gather.19 = bf16[2,64,256]{2,1,0:T(8,128)(2,1)S(1)} all-gather(bf16[1,64,256]{2,1,0:T(8,128)(2,1)S(1)} %bitcast.122), channel_id=1, replica_groups=mesh['x'=4,'z'=8,'core'=2,'blk'=8] {'core'}, dimensions={0}, use_global_device_ids=true | all-gather | bytes 98304 | tf_op jit(solution)/shard_map/all_gather | solution.py:57
  50.4 2.0 %collective-permute-done.6 = bf16[4,2,32,256]{3,2,0,1:T(8,128)(2,1)S(1)} collective-permute-done((bf16[4,2,32,256]{3,2,0,1:T(8,128)(2,1)S(1)}, bf16[4,2,32,256]{3,2,0,1:T(8,128)(2,1)S(1)}, u32[]{:S(2)}, u32[]{:S(2)}) %collective-permute-start.6) | collective-permute-done | bytes 131104 | tf_op jit(solution)/shard_map/ppermute | solution.py:52
  52.4 2.2 %collective-permute-done.7 = bf16[4,2,32,256]{3,2,0,1:T(8,128)(2,1)S(1)} collective-permute-done((bf16[4,2,32,256]{3,2,0,1:T(8,128)(2,1)S(1)}, bf16[4,2,32,256]{3,2,0,1:T(8,128)(2,1)S(1)}, u32[]{:S(2)}, u32[]{:S(2)}) %collective-permute-start.7) | collective-permute-done | bytes 131104 | tf_op jit(solution)/shard_map/ppermute | solution.py:52
  59.2 2.1 %collective-permute-start.11 = (bf16[8,128,256]{2,1,0:T(8,128)(2,1)}, bf16[8,128,256]{2,1,0:T(8,128)(2,1)S(1)}, u32[]{:S(2)}, u32[]{:S(2)}) collective-permute-start(bf16[8,128,256]{2,1,0:T(8,128)(2,1)} %fusion.9), channel_id=1, source_target_pairs={{0,128},{1,129},{2,130},{3,131},{4,132},{5,133},{6,134},{7,135},{8... | collective-permute-start | bytes 1572872 | tf_op jit(solution)/shard_map/ppermute | solution.py:65
  61.2 3.0 %collective-permute-start.12 = (bf16[8,128,256]{2,1,0:T(8,128)(2,1)}, bf16[8,128,256]{2,1,0:T(8,128)(2,1)}, u32[]{:S(2)}, u32[]{:S(2)}) collective-permute-start(bf16[8,128,256]{2,1,0:T(8,128)(2,1)} %fusion.9), channel_id=1, source_target_pairs={{0,256},{1,257},{2,258},{3,259},{4,260},{5,261},{6,262},{7,263},{8... | collective-permute-start | bytes 1572872 | tf_op jit(solution)/shard_map/ppermute | solution.py:65
  64.2 2.1 %collective-permute-start.13 = (bf16[8,128,256]{2,1,0:T(8,128)(2,1)}, bf16[8,128,256]{2,1,0:T(8,128)(2,1)}, u32[]{:S(2)}, u32[]{:S(2)}) collective-permute-start(bf16[8,128,256]{2,1,0:T(8,128)(2,1)} %fusion.9), channel_id=1, source_target_pairs={{0,384},{1,385},{2,386},{3,387},{4,388},{5,389},{6,390},{7,391},{8... | collective-permute-start | bytes 1572872 | tf_op jit(solution)/shard_map/ppermute | solution.py:65
  67.3 3.4 %all-to-all-start.2 = ((bf16[8,64,128]{2,1,0:T(8,128)(2,1)}), bf16[8,64,128]{2,1,0:T(8,128)(2,1)S(1)}, u32[]{:S(2)}, u32[]{:S(2)}) async-start(bf16[8,64,128]{2,1,0:T(8,128)(2,1)} %bitcast.102), calls=%async_computation.2 | async-start | bytes 262144 | tf_op jit(solution)/shard_map/all_to_all | solution.py:14
  70.7 7.8 %all-to-all-done.2 = bf16[8,64,128]{2,1,0:T(8,128)(2,1)S(1)} async-done(((bf16[8,64,128]{2,1,0:T(8,128)(2,1)}), bf16[8,64,128]{2,1,0:T(8,128)(2,1)S(1)}, u32[]{:S(2)}, u32[]{:S(2)}) %all-to-all-start.2) | async-done | bytes 131104 | tf_op jit(solution)/shard_map/all_to_all | solution.py:14
  78.5 10.9 %all-gather = bf16[128,128]{1,0:T(8,128)(2,1)S(1)} all-gather(bf16[64,128]{1,0:T(8,128)(2,1)S(1)} %reduce_sum.42), channel_id=2, replica_groups=mesh['x'=4,'z'=8,'core'=2,'blk'=8] {'core'}, dimensions={0}, use_global_device_ids=true | all-gather | bytes 49152 | tf_op jit(solution)/shard_map/all_gather | solution.py:77
  92.3 10.8 %all_to_all.35 = bf16[8,64,128]{2,1,0:T(8,128)(2,1)S(1)} all-to-all(bf16[8,64,128]{2,1,0:T(8,128)(2,1)S(1)} %bitcast.116), channel_id=1, replica_groups=mesh['x'=4,'z'=8,'core'=2,'blk'=8] {'blk'}, dimensions={0} | all-to-all | bytes 262144 | tf_op jit(solution)/shard_map/all_to_all | solution.py:14
  103.1 3.1 %all-gather.1 = f32[128,128]{1,0:T(8,128)S(1)} all-gather(f32[64,128]{1,0:T(8,128)S(1)} %convert_reduce_fusion.1), channel_id=3, replica_groups=mesh['x'=4,'z'=8,'core'=2,'blk'=8] {'core'}, dimensions={0}, use_global_device_ids=true | all-gather | bytes 98304 | tf_op jit(solution)/shard_map/all_gather | solution.py:77
  107.2 3.4 %all-to-all-start.4 = ((bf16[8,64,128]{2,1,0:T(8,128)(2,1)}), bf16[8,64,128]{2,1,0:T(8,128)(2,1)S(1)}, u32[]{:S(2)}, u32[]{:S(2)}) async-start(bf16[8,64,128]{2,1,0:T(8,128)(2,1)} %bitcast.98), calls=%async_computation.4 | async-start | bytes 262144 | tf_op jit(solution)/shard_map/all_to_all | solution.py:14
  110.7 8.2 %all-to-all-done.4 = bf16[8,64,128]{2,1,0:T(8,128)(2,1)S(1)} async-done(((bf16[8,64,128]{2,1,0:T(8,128)(2,1)}), bf16[8,64,128]{2,1,0:T(8,128)(2,1)S(1)}, u32[]{:S(2)}, u32[]{:S(2)}) %all-to-all-start.4) | async-done | bytes 131104 | tf_op jit(solution)/shard_map/all_to_all | solution.py:14
  129.8 3.3 %all-to-all-start.5 = ((bf16[4,2,64,128]{3,2,1,0:T(8,128)(2,1)}), bf16[4,2,64,128]{3,2,1,0:T(8,128)(2,1)S(1)}, u32[]{:S(2)}, u32[]{:S(2)}) async-start(bf16[4,2,64,128]{3,2,1,0:T(8,128)(2,1)} %broadcast_in_dim.35), calls=%async_computation.5 | async-start | bytes 262144 | tf_op jit(solution)/shard_map/all_to_all | solution.py:14
  134.2 3.7 %all-to-all-done.5 = bf16[4,2,64,128]{3,2,1,0:T(8,128)(2,1)S(1)} async-done(((bf16[4,2,64,128]{3,2,1,0:T(8,128)(2,1)}), bf16[4,2,64,128]{3,2,1,0:T(8,128)(2,1)S(1)}, u32[]{:S(2)}, u32[]{:S(2)}) %all-to-all-start.5) | async-done | bytes 131104 | tf_op jit(solution)/shard_map/all_to_all | solution.py:14
  137.9 5.0 %all-gather.2 = bf16[8,2,64,128]{3,2,1,0:T(8,128)(2,1)S(1)} all-gather(bf16[4,2,64,128]{3,2,1,0:T(8,128)(2,1)S(1)} %all-to-all-done.5), channel_id=4, replica_groups=mesh['x'=4,'z'=8,'core'=2,'blk'=8] {'core'}, dimensions={0}, use_global_device_ids=true | all-gather | bytes 393216 | tf_op jit(solution)/shard_map/all_gather | solution.py:77
  144.4 32.5 %all_to_all.36 = bf16[8,544,128]{2,1,0:T(8,128)(2,1)S(1)} all-to-all(bf16[8,544,128]{2,1,0:T(8,128)(2,1)S(1)} %bitcast.114), channel_id=1, replica_groups=mesh['x'=4,'z'=8,'core'=2,'blk'=8] {'blk'}, dimensions={0} | all-to-all | bytes 2228224 | tf_op jit(solution)/shard_map/all_to_all | solution.py:14
  (91 shorter events, 42.7 us)
Async XLA Ops:
  1.6 7.5 %collective-permute-start = (bf16[8,2048]{1,0:T(8,128)(2,1)S(1)}, bf16[8,2048]{1,0:T(8,128)(2,1)S(1)}, u32[]{:S(2)}, u32[]{:S(2)}) collective-permute-start(bf16[8,2048]{1,0:T(8,128)(2,1)S(1)} %get-tuple-element.12), channel_id=1, source_target_pairs={{0,128},{1,129},{2,130},{3,131},{4,132},{5,133},{6,134},{7,135},{8... | collective-permute-start | bytes 98312 | tf_op jit(solution)/shard_map/ppermute | solution.py:49
  5.6 3.5 %collective-permute-start.1 = (bf16[8,2048]{1,0:T(8,128)(2,1)S(1)}, bf16[8,2048]{1,0:T(8,128)(2,1)S(1)}, u32[]{:S(2)}, u32[]{:S(2)}) collective-permute-start(bf16[8,2048]{1,0:T(8,128)(2,1)S(1)} %get-tuple-element.14), channel_id=1, source_target_pairs={{0,256},{1,257},{2,258},{3,259},{4,260},{5,261},{6,262},{7,263},{8... | collective-permute-start | bytes 98312 | tf_op jit(solution)/shard_map/ppermute | solution.py:49
  10.7 13.7 %all-to-all-start = ((bf16[8,8,256]{2,1,0:T(8,128)(2,1)}), bf16[8,8,256]{2,1,0:T(8,128)(2,1)S(1)}, u32[]{:S(2)}, u32[]{:S(2)}) async-start(bf16[8,8,256]{2,1,0:T(8,128)(2,1)} %bitcast.1), calls=%async_computation | async-start | bytes 65536 | tf_op jit(solution)/shard_map/all_to_all | solution.py:14
  25.1 13.2 %all-to-all-start.1 = ((bf16[4,2,32,256]{3,2,1,0:T(8,128)(2,1)}), bf16[4,2,32,256]{3,2,1,0:T(8,128)(2,1)S(1)}, u32[]{:S(2)}, u32[]{:S(2)}) async-start(bf16[4,2,32,256]{3,2,1,0:T(8,128)(2,1)} %broadcast_in_dim.16), calls=%async_computation.1 | async-start | bytes 262144 | tf_op jit(solution)/shard_map/all_to_all | solution.py:14
  30.1 28.2 %collective-permute-start.10 = (bf16[8,128,256]{2,1,0:T(8,128)(2,1)}, bf16[8,128,256]{2,1,0:T(8,128)(2,1)}, u32[]{:S(2)}, u32[]{:S(2)}) collective-permute-start(bf16[8,128,256]{2,1,0:T(8,128)(2,1)} %slice_bitcast_fusion), channel_id=1, source_target_pairs={{8,0},{9,1},{10,2},{11,3},{12,4},{13,5},{14,6},{15,7}} | collective-permute-start | bytes 1572872 | tf_op jit(solution)/shard_map/ppermute | solution.py:61
  38.2 6.4 %collective-permute-start.3 = (bf16[4,2,32,256]{3,2,0,1:T(8,128)(2,1)S(1)}, bf16[4,2,32,256]{3,2,0,1:T(8,128)(2,1)S(1)}, u32[]{:S(2)}, u32[]{:S(2)}) collective-permute-start(bf16[4,2,32,256]{3,2,0,1:T(8,128)(2,1)S(1)} %copy.20), channel_id=1, source_target_pairs={{16,0},{17,1},{18,2},{19,3},{20,4},{21,5},{22,6},{23,7},{24,8},{25... | collective-permute-start | bytes 393224 | tf_op jit(solution)/shard_map/ppermute | solution.py:52
  39.5 7.4 %collective-permute-start.4 = (bf16[4,2,32,256]{3,2,0,1:T(8,128)(2,1)S(1)}, bf16[4,2,32,256]{3,2,0,1:T(8,128)(2,1)S(1)}, u32[]{:S(2)}, u32[]{:S(2)}) collective-permute-start(bf16[4,2,32,256]{3,2,0,1:T(8,128)(2,1)S(1)} %copy.20), channel_id=1, source_target_pairs={{32,0},{33,1},{34,2},{35,3},{36,4},{37,5},{38,6},{39,7},{40,8},{41... | collective-permute-start | bytes 393224 | tf_op jit(solution)/shard_map/ppermute | solution.py:52
  40.8 8.3 %collective-permute-start.5 = (bf16[4,2,32,256]{3,2,0,1:T(8,128)(2,1)S(1)}, bf16[4,2,32,256]{3,2,0,1:T(8,128)(2,1)S(1)}, u32[]{:S(2)}, u32[]{:S(2)}) collective-permute-start(bf16[4,2,32,256]{3,2,0,1:T(8,128)(2,1)S(1)} %copy.20), channel_id=1, source_target_pairs={{48,0},{49,1},{50,2},{51,3},{52,4},{53,5},{54,6},{55,7},{56,8},{57... | collective-permute-start | bytes 393224 | tf_op jit(solution)/shard_map/ppermute | solution.py:52
  42.1 10.3 %collective-permute-start.6 = (bf16[4,2,32,256]{3,2,0,1:T(8,128)(2,1)S(1)}, bf16[4,2,32,256]{3,2,0,1:T(8,128)(2,1)S(1)}, u32[]{:S(2)}, u32[]{:S(2)}) collective-permute-start(bf16[4,2,32,256]{3,2,0,1:T(8,128)(2,1)S(1)} %copy.20), channel_id=1, source_target_pairs={{64,0},{65,1},{66,2},{67,3},{68,4},{69,5},{70,6},{71,7},{72,8},{73... | collective-permute-start | bytes 393224 | tf_op jit(solution)/shard_map/ppermute | solution.py:52
  44.6 10.1 %collective-permute-start.7 = (bf16[4,2,32,256]{3,2,0,1:T(8,128)(2,1)S(1)}, bf16[4,2,32,256]{3,2,0,1:T(8,128)(2,1)S(1)}, u32[]{:S(2)}, u32[]{:S(2)}) collective-permute-start(bf16[4,2,32,256]{3,2,0,1:T(8,128)(2,1)S(1)} %copy.20), channel_id=1, source_target_pairs={{80,0},{81,1},{82,2},{83,3},{84,4},{85,5},{86,6},{87,7},{88,8},{89... | collective-permute-start | bytes 393224 | tf_op jit(solution)/shard_map/ppermute | solution.py:52
  46.9 9.2 %collective-permute-start.8 = (bf16[4,2,32,256]{3,2,0,1:T(8,128)(2,1)S(1)}, bf16[4,2,32,256]{3,2,0,1:T(8,128)(2,1)S(1)}, u32[]{:S(2)}, u32[]{:S(2)}) collective-permute-start(bf16[4,2,32,256]{3,2,0,1:T(8,128)(2,1)S(1)} %copy.20), channel_id=1, source_target_pairs={{96,0},{97,1},{98,2},{99,3},{100,4},{101,5},{102,6},{103,7},{104,8... | collective-permute-start | bytes 393224 | tf_op jit(solution)/shard_map/ppermute | solution.py:52
  49.1 8.3 %collective-permute-start.9 = (bf16[4,2,32,256]{3,2,0,1:T(8,128)(2,1)S(1)}, bf16[4,2,32,256]{3,2,0,1:T(8,128)(2,1)S(1)}, u32[]{:S(2)}, u32[]{:S(2)}) collective-permute-start(bf16[4,2,32,256]{3,2,0,1:T(8,128)(2,1)S(1)} %copy.20), channel_id=1, source_target_pairs={{112,0},{113,1},{114,2},{115,3},{116,4},{117,5},{118,6},{119,7},{1... | collective-permute-start | bytes 393224 | tf_op jit(solution)/shard_map/ppermute | solution.py:52
  59.2 30.3 %collective-permute-start.11 = (bf16[8,128,256]{2,1,0:T(8,128)(2,1)}, bf16[8,128,256]{2,1,0:T(8,128)(2,1)S(1)}, u32[]{:S(2)}, u32[]{:S(2)}) collective-permute-start(bf16[8,128,256]{2,1,0:T(8,128)(2,1)} %fusion.9), channel_id=1, source_target_pairs={{0,128},{1,129},{2,130},{3,131},{4,132},{5,133},{6,134},{7,135},{8... | collective-permute-start | bytes 1572872 | tf_op jit(solution)/shard_map/ppermute | solution.py:65
  61.2 28.2 %collective-permute-start.12 = (bf16[8,128,256]{2,1,0:T(8,128)(2,1)}, bf16[8,128,256]{2,1,0:T(8,128)(2,1)}, u32[]{:S(2)}, u32[]{:S(2)}) collective-permute-start(bf16[8,128,256]{2,1,0:T(8,128)(2,1)} %fusion.9), channel_id=1, source_target_pairs={{0,256},{1,257},{2,258},{3,259},{4,260},{5,261},{6,262},{7,263},{8... | collective-permute-start | bytes 1572872 | tf_op jit(solution)/shard_map/ppermute | solution.py:65
  64.2 26.0 %collective-permute-start.13 = (bf16[8,128,256]{2,1,0:T(8,128)(2,1)}, bf16[8,128,256]{2,1,0:T(8,128)(2,1)}, u32[]{:S(2)}, u32[]{:S(2)}) collective-permute-start(bf16[8,128,256]{2,1,0:T(8,128)(2,1)} %fusion.9), channel_id=1, source_target_pairs={{0,384},{1,385},{2,386},{3,387},{4,388},{5,389},{6,390},{7,391},{8... | collective-permute-start | bytes 1572872 | tf_op jit(solution)/shard_map/ppermute | solution.py:65
  67.3 11.2 %all-to-all-start.2 = ((bf16[8,64,128]{2,1,0:T(8,128)(2,1)}), bf16[8,64,128]{2,1,0:T(8,128)(2,1)S(1)}, u32[]{:S(2)}, u32[]{:S(2)}) async-start(bf16[8,64,128]{2,1,0:T(8,128)(2,1)} %bitcast.102), calls=%async_computation.2 | async-start | bytes 262144 | tf_op jit(solution)/shard_map/all_to_all | solution.py:14
  107.2 11.6 %all-to-all-start.4 = ((bf16[8,64,128]{2,1,0:T(8,128)(2,1)}), bf16[8,64,128]{2,1,0:T(8,128)(2,1)S(1)}, u32[]{:S(2)}, u32[]{:S(2)}) async-start(bf16[8,64,128]{2,1,0:T(8,128)(2,1)} %bitcast.98), calls=%async_computation.4 | async-start | bytes 262144 | tf_op jit(solution)/shard_map/all_to_all | solution.py:14
  118.9 6.5 %collective-permute-start.14 = (bf16[2,64,128]{2,1,0:T(8,128)(2,1)S(1)}, bf16[2,64,128]{2,1,0:T(8,128)(2,1)S(1)}, u32[]{:S(2)}, u32[]{:S(2)}) collective-permute-start(bf16[2,64,128]{2,1,0:T(8,128)(2,1)S(1)} %pad_maximum_fusion), channel_id=1, source_target_pairs={{0,16},{1,17},{2,18},{3,19},{4,20},{5,21},{6,22},{7,23},{8,24},{9,... | collective-permute-start | bytes 98312 | tf_op jit(solution)/shard_map/ppermute | solution.py:89
  120.2 6.5 %collective-permute-start.15 = (bf16[2,64,128]{2,1,0:T(8,128)(2,1)S(1)}, bf16[2,64,128]{2,1,0:T(8,128)(2,1)S(1)}, u32[]{:S(2)}, u32[]{:S(2)}) collective-permute-start(bf16[2,64,128]{2,1,0:T(8,128)(2,1)S(1)} %pad_maximum_fusion), channel_id=1, source_target_pairs={{0,32},{1,33},{2,34},{3,35},{4,36},{5,37},{6,38},{7,39},{8,40},{9,... | collective-permute-start | bytes 98312 | tf_op jit(solution)/shard_map/ppermute | solution.py:89
  121.5 6.6 %collective-permute-start.16 = (bf16[2,64,128]{2,1,0:T(8,128)(2,1)S(1)}, bf16[2,64,128]{2,1,0:T(8,128)(2,1)S(1)}, u32[]{:S(2)}, u32[]{:S(2)}) collective-permute-start(bf16[2,64,128]{2,1,0:T(8,128)(2,1)S(1)} %pad_maximum_fusion), channel_id=1, source_target_pairs={{0,48},{1,49},{2,50},{3,51},{4,52},{5,53},{6,54},{7,55},{8,56},{9,... | collective-permute-start | bytes 98312 | tf_op jit(solution)/shard_map/ppermute | solution.py:89
  122.8 5.4 %collective-permute-start.17 = (bf16[2,64,128]{2,1,0:T(8,128)(2,1)S(1)}, bf16[2,64,128]{2,1,0:T(8,128)(2,1)S(1)}, u32[]{:S(2)}, u32[]{:S(2)}) collective-permute-start(bf16[2,64,128]{2,1,0:T(8,128)(2,1)S(1)} %pad_maximum_fusion), channel_id=1, source_target_pairs={{0,64},{1,65},{2,66},{3,67},{4,68},{5,69},{6,70},{7,71},{8,72},{9,... | collective-permute-start | bytes 98312 | tf_op jit(solution)/shard_map/ppermute | solution.py:89
  124.1 4.1 %collective-permute-start.18 = (bf16[2,64,128]{2,1,0:T(8,128)(2,1)S(1)}, bf16[2,64,128]{2,1,0:T(8,128)(2,1)S(1)}, u32[]{:S(2)}, u32[]{:S(2)}) collective-permute-start(bf16[2,64,128]{2,1,0:T(8,128)(2,1)S(1)} %pad_maximum_fusion), channel_id=1, source_target_pairs={{0,80},{1,81},{2,82},{3,83},{4,84},{5,85},{6,86},{7,87},{8,88},{9,... | collective-permute-start | bytes 98312 | tf_op jit(solution)/shard_map/ppermute | solution.py:89
  125.5 2.8 %collective-permute-start.19 = (bf16[2,64,128]{2,1,0:T(8,128)(2,1)S(1)}, bf16[2,64,128]{2,1,0:T(8,128)(2,1)S(1)}, u32[]{:S(2)}, u32[]{:S(2)}) collective-permute-start(bf16[2,64,128]{2,1,0:T(8,128)(2,1)S(1)} %pad_maximum_fusion), channel_id=1, source_target_pairs={{0,96},{1,97},{2,98},{3,99},{4,100},{5,101},{6,102},{7,103},{8,104... | collective-permute-start | bytes 98312 | tf_op jit(solution)/shard_map/ppermute | solution.py:89
  129.8 8.1 %all-to-all-start.5 = ((bf16[4,2,64,128]{3,2,1,0:T(8,128)(2,1)}), bf16[4,2,64,128]{3,2,1,0:T(8,128)(2,1)S(1)}, u32[]{:S(2)}, u32[]{:S(2)}) async-start(bf16[4,2,64,128]{3,2,1,0:T(8,128)(2,1)} %broadcast_in_dim.35), calls=%async_computation.5 | async-start | bytes 262144 | tf_op jit(solution)/shard_map/all_to_all | solution.py:14
  (6 other events, 64.3 us)
where the time goes:
time: 180 us; the launch traced here: 179 us
  blocking collectives  64.2 us (36%)
  starting transfers between devices  60 us (33%)
  waiting for transfers between devices  35.6 us (20%)
  local copies, waits for them, and re-layouts  8.36 us (5%)
  other arithmetic  7.18 us (4%)
  matrix products  2.1 us (1%)
    all_to_all x2, blocking collectives, swap_blocks(): return lax.all_to_all(array, axis, split_axis=0, concat_axis=0, tiled=True)  43.3 us
    all_to_all x5, waiting for transfers between devices, swap_blocks(): return lax.all_to_all(array, axis, split_axis=0, concat_axis=0, tiled=True)  23.8 us
    all_to_all x5, starting transfers between devices, swap_blocks(): return lax.all_to_all(array, axis, split_axis=0, concat_axis=0, tiled=True)  21.1 us
    all_gather x3, blocking collectives, both_cores(): pair = lax.all_gather(value, 'core', axis=0, tiled=False)  19.1 us
    ppermute x7, waiting for transfers between devices, local(): lax.ppermute(inverse, 'z', [(k, 0)])  9.95 us
    ppermute x7, starting transfers between devices, local(): spread = spread + lax.ppermute(solved, 'z', [(0, k)])  9.04 us
    ppermute x7, starting transfers between devices, local(): lax.ppermute(inverse, 'z', [(k, 0)])  9.01 us
    ppermute x3, starting transfers between devices, local(): mine = mine + lax.ppermute(pivot[k], ('x', 'z'), [(0, k * NZ)])  7.42 us
  transfers between devices with their start and end apart: 26, of which 13 were waited for; matrix products, arithmetic and copies ran while one was open for 4% of the time, Pallas kernels for 0%

commit v1 on v0

--- a/solution.py
+++ b/solution.py
@@ -1,6 +1,8 @@
 import jax
 import jax.numpy as jnp
 from jax import lax
+from jax.experimental import pallas as pl
+from jax.experimental.pallas import tpu as pltpu
 from jax.sharding import Mesh, PartitionSpec as P
 
 
@@ -22,10 +24,59 @@
     return lax.dot_general(left, right, (((1,), (1,)), ((), ())), preferred_element_type=WIDE)
 
 
-def scatter_sum(partial, blocks):
-    t, wide = partial.shape
-    split = partial.astype(HALF).reshape(t, blocks, wide // blocks).transpose(1, 0, 2)
+def scatter_sum(split):
     return jnp.sum(swap_blocks(split, "blk").astype(WIDE), axis=0)
+
+
+def assemble(planes, whole):
+    for z, plane in enumerate(planes):
+        count, size, _ = plane.shape
+        for x in range(count):
+            at = (x * len(planes) + z) * size
+            whole[at : at + size, :] = plane[x]
+
+
+def write_blocks(value, whole, out):
+    size = out.shape[2]
+    for g in range(out.shape[0]):
+        out[g] = product(value, whole[g * size : (g + 1) * size, :]).astype(out.dtype)
+
+
+def first_kernel(pivot, *refs):
+    planes, (out, whole) = refs[:NZ], refs[NZ:]
+    assemble(planes, whole)
+    write_blocks(pivot[...], whole, out)
+
+
+def cross_kernel(pair, order, own, *refs):
+    others, (out, whole) = refs[: NX - 1], refs[NX - 1 :]
+    value = product(pair[0], order[0])
+    for c in range(1, NC):
+        value = value + product(pair[c], order[c])
+    blocks, size, _ = own.shape
+    for g in range(blocks):
+        whole[g * size : (g + 1) * size, :] = own[g]
+        for other in others:
+            whole[g * size : (g + 1) * size, :] += other[g]
+    write_blocks(value.astype(HALF), whole, out)
+
+
+def second_kernel(pivot, update, *refs):
+    planes, (out, whole, value) = refs[:NZ], refs[NZ:]
+    assemble(planes, whole)
+    half = update.shape[2]
+    for c in range(NC):
+        part = pivot[:, c * half : (c + 1) * half].astype(WIDE) - update[c]
+        value[:, c * half : (c + 1) * half] = part.astype(HALF)
+    write_blocks(value[...], whole, out)
+
+
+def run_kernel(kernel, blocks, t, size, width, scratch, *operands):
+    return pl.pallas_call(
+        kernel,
+        out_shape=jax.ShapeDtypeStruct((blocks, t, size), HALF),
+        scratch_shapes=[pltpu.VMEM((blocks * size, width), HALF), *scratch],
+    )(*operands)
 
 
 def local(factor_panel, right_side, block_inverse):
@@ -49,10 +100,6 @@
         mine = mine + lax.ppermute(pivot[k], ("x", "z"), [(0, k * NZ)])
 
     inverse = gather_by_swap(block_inverse.astype(HALF), "x", NX)
-    planes = [inverse] + [lax.ppermute(inverse, "z", [(k, 0)]) for k in range(1, NZ)]
-    inverse = jnp.stack(planes).transpose(2, 1, 0, 3, 4)
-    inverse = inverse.reshape(STEPS, NX * NZ * rows_local, width)
-
     pivot = swap_blocks(mine.reshape(dates_x, n_blk, width).transpose(1, 0, 2), "blk")
     pivot = lax.all_gather(pivot.reshape(t, width), "core", axis=0, tiled=False)
 
@@ -60,15 +107,19 @@
     halves = panels[0].reshape(n_blk, NC, half, width)
     sent = lax.ppermute(halves[:, 0], ("x", "z", "core"), [(1, 0)])
     lower = jnp.where(core == 1, halves[:, 1], sent)
-    cross = jnp.where((x == 0) & (z == 0), lower, jnp.zeros_like(lower))
-    for k in range(1, NX):
-        cross = cross + lax.ppermute(lower, ("x", "z"), [(0, k * NZ)])
-    cross = cross.reshape(n_blk * half, width)
+    cross = [jnp.where((x == 0) & (z == 0), lower, jnp.zeros_like(lower))]
+    cross += [lax.ppermute(lower, ("x", "z"), [(0, k * NZ)]) for k in range(1, NX)]
 
     place = jnp.arange(width)
     c_of, q_of, i_of = place // half, place % half // rows_local, place % rows_local
     natural = (q_of * NC + c_of) * rows_local + i_of
     order = (natural[:, None] == place[None, :]).astype(HALF)
+    pair_order = order.reshape(NC, half, width).transpose(0, 2, 1)
+    sizes = (n_blk, t, half, width)
+
+    def planes_of(k):
+        mine = inverse[:, k]
+        return [mine] + [lax.ppermute(mine, "z", [(source, 0)]) for source in range(1, NZ)]
 
     def ordered(value):
         return jnp.dot(value, order, preferred_element_type=WIDE).astype(HALF)
@@ -77,11 +128,18 @@
         pair = lax.all_gather(value, "core", axis=0, tiled=False)
         return jnp.concatenate([pair[0], pair[1]], axis=-1)
 
-    first = scatter_sum(product(pivot[0], inverse[0]), n_blk).astype(HALF)
+    planes = planes_of(0)
+    partial = run_kernel(first_kernel, *sizes, (), pivot[0], *planes)
+    first = scatter_sum(partial).astype(HALF)
     first, panels = lax.optimization_barrier((first, panels))
-    update = scatter_sum(product(ordered(both_cores(first)), cross), n_blk)
-    reduced = pivot[1].astype(WIDE) - both_cores(update)
-    second = scatter_sum(product(reduced.astype(HALF), inverse[1]), n_blk).astype(HALF)
+    planes = planes_of(1)
+    pair = lax.all_gather(first, "core", axis=0, tiled=False)
+    partial = run_kernel(cross_kernel, *sizes, (), pair, pair_order, *cross)
+    update = scatter_sum(partial)
+    pair = lax.all_gather(update, "core", axis=0, tiled=False)
+    scratch = (pltpu.VMEM((t, width), HALF),)
+    partial = run_kernel(second_kernel, *sizes, scratch, pivot[1], pair, *planes)
+    second = scatter_sum(partial).astype(HALF)
 
     solved = jnp.stack([first, second])
     spread = jnp.where(z == 0, solved, jnp.zeros_like(solved))
@@ -98,7 +156,7 @@
         ],
         axis=1,
     )
-    extra = 128
+    extra = 512
     pick = jnp.arange(extra)
     at = pick // rows_local * width + row % per_blk * rows_local + pick % rows_local
     wanted = (pick < STEPS * rows_local) & (row // per_blk == blk)

time: 180 us -> 186 us (1.033)
  starting transfers between devices: 60 us -> 71.8 us
  blocking collectives: 64.2 us -> 52.6 us
  Pallas kernels: 0 us -> 6.85 us
    all_gather x3 -> x1, blocking collectives: 19.1 us -> 5.59 us  [both_cores(): pair = lax.all_gather(value, 'core', axis=0, tiled=False)]
    ppermute x10 -> x17, starting transfers between devices: 16.1 us -> 25 us  [the longest x14 18.1 us: planes_of(): lax.ppermute(mine, 'z', [(source, 0)])]
    all_gather x0 -> x2, blocking collectives: none -> 7.81 us  [the longest x1 5.32 us: local(): pair = lax.all_gather(first, 'core', axis=0, tiled=False)]
    pallas_call x0 -> x3, Pallas kernels: none -> 6.85 us  [run_kernel(): pl.pallas_call(kernel, out_shape=jax.ShapeDtypeStruct((blocks, t, size),...]
    all_to_all x2 -> x1, blocking collectives: 43.3 us -> 37.4 us  [swap_blocks(): return lax.all_to_all(array, axis, split_axis=0, concat_axis=0, tiled=True)]
    all_to_all x5 -> x6, waiting for transfers between devices: 23.8 us -> 28.5 us  [swap_blocks(): return lax.all_to_all(array, axis, split_axis=0, concat_axis=0, tiled=True)]
    all_to_all x5 -> x6, starting transfers between devices: 21.1 us -> 24.4 us  [swap_blocks(): return lax.all_to_all(array, axis, split_axis=0, concat_axis=0, tiled=True)]
    ppermute x10 -> x17, waiting for transfers between devices: 9.96 us -> 6.65 us  [the longest x14 6.64 us: planes_of(): lax.ppermute(mine, 'z', [(source, 0)])]
  transfers between devices with their start and end apart: 26 -> 34, of which waited for: 13 -> 11; matrix products, arithmetic and copies ran while one was open for 4% -> 5% of each run, Pallas kernels for 0% -> 1%
where the time goes in v1:
time: 186 us; the launch traced here: 185 us
  starting transfers between devices  71.8 us (39%)
  blocking collectives  52.6 us (28%)
  waiting for transfers between devices  36.1 us (19%)
  local copies, waits for them, and re-layouts  8 us (4%)
  Pallas kernels  6.85 us (4%)
  other arithmetic  6.61 us (4%)
    all_to_all x1, blocking collectives, swap_blocks(): return lax.all_to_all(array, axis, split_axis=0, concat_axis=0, tiled=True)  37.4 us
    all_to_all x6, waiting for transfers between devices, swap_blocks(): return lax.all_to_all(array, axis, split_axis=0, concat_axis=0, tiled=True)  28.5 us
    all_to_all x6, starting transfers between devices, swap_blocks(): return lax.all_to_all(array, axis, split_axis=0, concat_axis=0, tiled=True)  24.4 us
    ppermute x14, starting transfers between devices, planes_of(): lax.ppermute(mine, 'z', [(source, 0)])  18.1 us
    ppermute x7, starting transfers between devices, local(): spread = spread + lax.ppermute(solved, 'z', [(0, k)])  9.03 us
    ppermute x3, starting transfers between devices, local(): mine = mine + lax.ppermute(pivot[k], ('x', 'z'), [(0, k * NZ)])  7.42 us
    ppermute x3, starting transfers between devices, local(): lax.ppermute(lower, ('x', 'z'), [(0, k * NZ)])  6.88 us
    pallas_call x3, Pallas kernels, run_kernel(): pl.pallas_call(kernel, out_shape=jax.ShapeDtypeStruct((blocks, t, size),...  6.85 us
  transfers between devices with their start and end apart: 34, of which 11 were waited for; matrix products, arithmetic and copies ran while one was open for 5% of the time, Pallas kernels for 1%

profile of v1, /device:TPU:1, one launch (start us, length us, event | category | flops | bytes accessed | tf_op | source)
XLA Modules:
  0.0 184.5 jit_solution(17591157278136119133)
XLA Ops:
  1.6 3.9 %collective-permute-start = (bf16[8,2048]{1,0:T(8,128)(2,1)S(1)}, bf16[8,2048]{1,0:T(8,128)(2,1)S(1)}, u32[]{:S(2)}, u32[]{:S(2)}) collective-permute-start(bf16[8,2048]{1,0:T(8,128)(2,1)S(1)} %get-tuple-element.14), channel_id=1, source_target_pairs={{0,128},{1,129},{2,130},{3,131},{4,132},{5,133},{6,134},{7,135},{8... | collective-permute-start | bytes 98312 | tf_op jit(solution)/shard_map/ppermute | solution.py:100
  5.6 2.2 %collective-permute-start.1 = (bf16[8,2048]{1,0:T(8,128)(2,1)S(1)}, bf16[8,2048]{1,0:T(8,128)(2,1)S(1)}, u32[]{:S(2)}, u32[]{:S(2)}) collective-permute-start(bf16[8,2048]{1,0:T(8,128)(2,1)S(1)} %get-tuple-element.16), channel_id=1, source_target_pairs={{0,256},{1,257},{2,258},{3,259},{4,260},{5,261},{6,262},{7,263},{8... | collective-permute-start | bytes 98312 | tf_op jit(solution)/shard_map/ppermute | solution.py:100
  11.9 6.0 %collective-permute-start.10 = (bf16[8,128,256]{2,1,0:T(8,128)(2,1)}, bf16[8,128,256]{2,1,0:T(8,128)(2,1)}, u32[]{:S(2)}, u32[]{:S(2)}) collective-permute-start(bf16[8,128,256]{2,1,0:T(8,128)(2,1)} %slice_bitcast_fusion), channel_id=1, source_target_pairs={{8,0},{9,1},{10,2},{11,3},{12,4},{13,5},{14,6},{15,7}} | collective-permute-start | bytes 1572872 | tf_op jit(solution)/shard_map/ppermute | solution.py:108
  18.5 4.5 %all-to-all-start = ((bf16[8,8,256]{2,1,0:T(8,128)(2,1)}), bf16[8,8,256]{2,1,0:T(8,128)(2,1)S(1)}, u32[]{:S(2)}, u32[]{:S(2)}) async-start(bf16[8,8,256]{2,1,0:T(8,128)(2,1)} %bitcast.1), calls=%async_computation | async-start | bytes 65536 | tf_op jit(solution)/shard_map/all_to_all | solution.py:16
  23.0 6.9 %all-to-all-done = bf16[8,8,256]{2,1,0:T(8,128)(2,1)S(1)} async-done(((bf16[8,8,256]{2,1,0:T(8,128)(2,1)}), bf16[8,8,256]{2,1,0:T(8,128)(2,1)S(1)}, u32[]{:S(2)}, u32[]{:S(2)}) %all-to-all-start) | async-done | bytes 32800 | tf_op jit(solution)/shard_map/all_to_all | solution.py:16
  30.5 3.3 %all-to-all-start.1 = ((bf16[4,2,32,256]{3,2,1,0:T(8,128)(2,1)}), bf16[4,2,32,256]{3,2,1,0:T(8,128)(2,1)S(1)}, u32[]{:S(2)}, u32[]{:S(2)}) async-start(bf16[4,2,32,256]{3,2,1,0:T(8,128)(2,1)} %broadcast_in_dim.16), calls=%async_computation.1 | async-start | bytes 262144 | tf_op jit(solution)/shard_map/all_to_all | solution.py:16
  35.7 3.1 %all-to-all-done.1 = bf16[4,2,32,256]{3,2,1,0:T(8,128)(2,1)S(1)} async-done(((bf16[4,2,32,256]{3,2,1,0:T(8,128)(2,1)}), bf16[4,2,32,256]{3,2,1,0:T(8,128)(2,1)S(1)}, u32[]{:S(2)}, u32[]{:S(2)}) %all-to-all-start.1) | async-done | bytes 131104 | tf_op jit(solution)/shard_map/all_to_all | solution.py:16
  49.1 2.2 %collective-permute-start.11 = (bf16[8,128,256]{2,1,0:T(8,128)(2,1)}, bf16[8,128,256]{2,1,0:T(8,128)(2,1)S(1)}, u32[]{:S(2)}, u32[]{:S(2)}) collective-permute-start(bf16[8,128,256]{2,1,0:T(8,128)(2,1)} %get-tuple-element.7), channel_id=1, source_target_pairs={{0,128},{1,129},{2,130},{3,131},{4,132},{5,133},{6,134},{7,135},{8... | collective-permute-start | bytes 1572872 | tf_op jit(solution)/shard_map/ppermute | solution.py:111
  51.7 2.6 %collective-permute-start.12 = (bf16[8,128,256]{2,1,0:T(8,128)(2,1)}, bf16[8,128,256]{2,1,0:T(8,128)(2,1)S(1)}, u32[]{:S(2)}, u32[]{:S(2)}) collective-permute-start(bf16[8,128,256]{2,1,0:T(8,128)(2,1)} %get-tuple-element.7), channel_id=1, source_target_pairs={{0,256},{1,257},{2,258},{3,259},{4,260},{5,261},{6,262},{7,263},{8... | collective-permute-start | bytes 1572872 | tf_op jit(solution)/shard_map/ppermute | solution.py:111
  54.3 2.1 %collective-permute-start.13 = (bf16[8,128,256]{2,1,0:T(8,128)(2,1)}, bf16[8,128,256]{2,1,0:T(8,128)(2,1)}, u32[]{:S(2)}, u32[]{:S(2)}) collective-permute-start(bf16[8,128,256]{2,1,0:T(8,128)(2,1)} %get-tuple-element.7), channel_id=1, source_target_pairs={{0,384},{1,385},{2,386},{3,387},{4,388},{5,389},{6,390},{7,391},{8... | collective-permute-start | bytes 1572872 | tf_op jit(solution)/shard_map/ppermute | solution.py:111
  59.7 3.4 %all-to-all-start.2 = ((bf16[8,64,128]{2,1,0:T(8,128)(2,1)}), bf16[8,64,128]{2,1,0:T(8,128)(2,1)S(1)}, u32[]{:S(2)}, u32[]{:S(2)}) async-start(bf16[8,64,128]{2,1,0:T(8,128)(2,1)} %shard_map.50), calls=%async_computation.2 | async-start | bytes 262144 | tf_op jit(solution)/shard_map/all_to_all | solution.py:16
  63.8 7.1 %all-to-all-done.2 = bf16[8,64,128]{2,1,0:T(8,128)(2,1)S(1)} async-done(((bf16[8,64,128]{2,1,0:T(8,128)(2,1)}), bf16[8,64,128]{2,1,0:T(8,128)(2,1)S(1)}, u32[]{:S(2)}, u32[]{:S(2)}) %all-to-all-start.2) | async-done | bytes 131104 | tf_op jit(solution)/shard_map/all_to_all | solution.py:16
  71.0 5.3 %all-gather = bf16[128,128]{1,0:T(8,128)(2,1)} all-gather(bf16[64,128]{1,0:T(8,128)(2,1)S(1)} %reduce_sum.42), channel_id=2, replica_groups=mesh['x'=4,'z'=8,'core'=2,'blk'=8] {'core'}, dimensions={0}, use_global_device_ids=true | all-gather | bytes 49152 | tf_op jit(solution)/shard_map/all_gather | solution.py:136
  77.3 2.7 %shard_map.51 = bf16[8,64,128]{2,1,0:T(8,128)(2,1)} custom-call(bf16[2,64,128]{2,1,0:T(8,128)(2,1)} %bitcast.78, bf16[2,256,128]{2,1,0:T(8,128)(2,1)} %fusion.12.order, bf16[8,128,256]{2,1,0:T(8,128)(2,1)} %get-tuple-element.6.own, bf16[8,128,256]{2,1,0:T(8,128)(2,1)} %copy-done.3, bf16[8,128,256]{2,1,0:T(8,128)(2,1)} %copy-done.4, ...), custom_call_target="tpu_custom_call" | custom-call | tf_op jit(solution)/shard_map/pallas_call | solution.py:75
  80.1 3.4 %all-to-all-start.3 = ((bf16[8,64,128]{2,1,0:T(8,128)(2,1)}), bf16[8,64,128]{2,1,0:T(8,128)(2,1)S(1)}, u32[]{:S(2)}, u32[]{:S(2)}) async-start(bf16[8,64,128]{2,1,0:T(8,128)(2,1)} %shard_map.51), calls=%async_computation.3 | async-start | bytes 262144 | tf_op jit(solution)/shard_map/all_to_all | solution.py:16
  92.6 2.5 %all-gather.1 = f32[128,128]{1,0:T(8,128)} all-gather(f32[64,128]{1,0:T(8,128)S(1)} %convert_reduce_fusion.1), channel_id=3, replica_groups=mesh['x'=4,'z'=8,'core'=2,'blk'=8] {'core'}, dimensions={0}, use_global_device_ids=true | all-gather | bytes 98304 | tf_op jit(solution)/shard_map/all_gather | solution.py:139
  96.3 2.3 %collective-permute-done.18.refs_5_ = bf16[4,32,256]{2,1,0:T(8,128)(2,1)S(1)} collective-permute-done((bf16[4,32,256]{2,1,0:T(8,128)(2,1)S(1)}, bf16[4,32,256]{2,1,0:T(8,128)(2,1)S(1)}, u32[]{:S(2)}, u32[]{:S(2)}) %collective-permute-start.18) | collective-permute-done | bytes 65568 | tf_op jit(solution)/shard_map/ppermute | solution.py:122
  102.0 2.1 %shard_map.52 = bf16[8,64,128]{2,1,0:T(8,128)(2,1)} custom-call(bf16[64,256]{1,0:T(8,128)(2,1)} %get-tuple-element.18.pivot, f32[2,64,128]{2,1,0:T(8,128)} %bitcast.72, bf16[4,32,256]{2,1,0:T(8,128)(2,1)} %copy-done.5, bf16[4,32,256]{2,1,0:T(8,128)(2,1)} %copy-done.7, bf16[4,32,256]{2,1,0:T(8,128)(2,1)} %copy-done.8, bf16[4,32,256]{2,1,0:T(8,128)(2,1)} %copy-done.9, ...), custom_call_target="tpu_custom_call" | custom-call | tf_op jit(solution)/shard_map/pallas_call | solution.py:75
  104.1 6.6 %all-to-all-start.4 = ((bf16[8,64,128]{2,1,0:T(8,128)(2,1)}), bf16[8,64,128]{2,1,0:T(8,128)(2,1)S(1)}, u32[]{:S(2)}, u32[]{:S(2)}) async-start(bf16[8,64,128]{2,1,0:T(8,128)(2,1)} %shard_map.52), calls=%async_computation.4 | async-start | bytes 262144 | tf_op jit(solution)/shard_map/all_to_all | solution.py:16
  110.6 7.7 %all-to-all-done.4 = bf16[8,64,128]{2,1,0:T(8,128)(2,1)S(1)} async-done(((bf16[8,64,128]{2,1,0:T(8,128)(2,1)}), bf16[8,64,128]{2,1,0:T(8,128)(2,1)S(1)}, u32[]{:S(2)}, u32[]{:S(2)}) %all-to-all-start.4) | async-done | bytes 131104 | tf_op jit(solution)/shard_map/all_to_all | solution.py:16
  130.3 3.3 %all-to-all-start.5 = ((bf16[4,2,64,128]{3,2,1,0:T(8,128)(2,1)}), bf16[4,2,64,128]{3,2,1,0:T(8,128)(2,1)S(1)}, u32[]{:S(2)}, u32[]{:S(2)}) async-start(bf16[4,2,64,128]{3,2,1,0:T(8,128)(2,1)} %broadcast_in_dim.35), calls=%async_computation.5 | async-start | bytes 262144 | tf_op jit(solution)/shard_map/all_to_all | solution.py:16
  134.7 3.6 %all-to-all-done.5 = bf16[4,2,64,128]{3,2,1,0:T(8,128)(2,1)S(1)} async-done(((bf16[4,2,64,128]{3,2,1,0:T(8,128)(2,1)}), bf16[4,2,64,128]{3,2,1,0:T(8,128)(2,1)S(1)}, u32[]{:S(2)}, u32[]{:S(2)}) %all-to-all-start.5) | async-done | bytes 131104 | tf_op jit(solution)/shard_map/all_to_all | solution.py:16
  138.4 5.6 %all-gather.2 = bf16[8,2,64,128]{3,2,1,0:T(8,128)(2,1)S(1)} all-gather(bf16[4,2,64,128]{3,2,1,0:T(8,128)(2,1)S(1)} %all-to-all-done.5), channel_id=4, replica_groups=mesh['x'=4,'z'=8,'core'=2,'blk'=8] {'core'}, dimensions={0}, use_global_device_ids=true | all-gather | bytes 393216 | tf_op jit(solution)/shard_map/all_gather | solution.py:128
  145.5 37.4 %all_to_all.35 = bf16[8,640,128]{2,1,0:T(8,128)(2,1)S(1)} all-to-all(bf16[8,640,128]{2,1,0:T(8,128)(2,1)S(1)} %bitcast.68), channel_id=1, replica_groups=mesh['x'=4,'z'=8,'core'=2,'blk'=8] {'blk'}, dimensions={0} | all-to-all | bytes 2621440 | tf_op jit(solution)/shard_map/all_to_all | solution.py:16
  (130 shorter events, 53.4 us)
Async XLA Ops:
  1.6 16.3 %collective-permute-start = (bf16[8,2048]{1,0:T(8,128)(2,1)S(1)}, bf16[8,2048]{1,0:T(8,128)(2,1)S(1)}, u32[]{:S(2)}, u32[]{:S(2)}) collective-permute-start(bf16[8,2048]{1,0:T(8,128)(2,1)S(1)} %get-tuple-element.14), channel_id=1, source_target_pairs={{0,128},{1,129},{2,130},{3,131},{4,132},{5,133},{6,134},{7,135},{8... | collective-permute-start | bytes 98312 | tf_op jit(solution)/shard_map/ppermute | solution.py:100
  5.6 12.3 %collective-permute-start.1 = (bf16[8,2048]{1,0:T(8,128)(2,1)S(1)}, bf16[8,2048]{1,0:T(8,128)(2,1)S(1)}, u32[]{:S(2)}, u32[]{:S(2)}) collective-permute-start(bf16[8,2048]{1,0:T(8,128)(2,1)S(1)} %get-tuple-element.16), channel_id=1, source_target_pairs={{0,256},{1,257},{2,258},{3,259},{4,260},{5,261},{6,262},{7,263},{8... | collective-permute-start | bytes 98312 | tf_op jit(solution)/shard_map/ppermute | solution.py:100
  7.8 10.1 %collective-permute-start.2 = (bf16[8,2048]{1,0:T(8,128)(2,1)S(1)}, bf16[8,2048]{1,0:T(8,128)(2,1)S(1)}, u32[]{:S(2)}, u32[]{:S(2)}) collective-permute-start(bf16[8,2048]{1,0:T(8,128)(2,1)S(1)} %get-tuple-element.15), channel_id=1, source_target_pairs={{0,384},{1,385},{2,386},{3,387},{4,388},{5,389},{6,390},{7,391},{8... | collective-permute-start | bytes 98312 | tf_op jit(solution)/shard_map/ppermute | solution.py:100
  11.9 32.2 %collective-permute-start.10 = (bf16[8,128,256]{2,1,0:T(8,128)(2,1)}, bf16[8,128,256]{2,1,0:T(8,128)(2,1)}, u32[]{:S(2)}, u32[]{:S(2)}) collective-permute-start(bf16[8,128,256]{2,1,0:T(8,128)(2,1)} %slice_bitcast_fusion), channel_id=1, source_target_pairs={{8,0},{9,1},{10,2},{11,3},{12,4},{13,5},{14,6},{15,7}} | collective-permute-start | bytes 1572872 | tf_op jit(solution)/shard_map/ppermute | solution.py:108
  18.5 11.4 %all-to-all-start = ((bf16[8,8,256]{2,1,0:T(8,128)(2,1)}), bf16[8,8,256]{2,1,0:T(8,128)(2,1)S(1)}, u32[]{:S(2)}, u32[]{:S(2)}) async-start(bf16[8,8,256]{2,1,0:T(8,128)(2,1)} %bitcast.1), calls=%async_computation | async-start | bytes 65536 | tf_op jit(solution)/shard_map/all_to_all | solution.py:16
  30.5 8.3 %all-to-all-start.1 = ((bf16[4,2,32,256]{3,2,1,0:T(8,128)(2,1)}), bf16[4,2,32,256]{3,2,1,0:T(8,128)(2,1)S(1)}, u32[]{:S(2)}, u32[]{:S(2)}) async-start(bf16[4,2,32,256]{3,2,1,0:T(8,128)(2,1)} %broadcast_in_dim.16), calls=%async_computation.1 | async-start | bytes 262144 | tf_op jit(solution)/shard_map/all_to_all | solution.py:16
  38.9 7.6 %collective-permute-start.3 = (bf16[4,32,256]{2,1,0:T(8,128)(2,1)S(1)}, bf16[4,32,256]{2,1,0:T(8,128)(2,1)S(1)}, u32[]{:S(2)}, u32[]{:S(2)}) collective-permute-start(bf16[4,32,256]{2,1,0:T(8,128)(2,1)S(1)} %get-tuple-element.13.refs_0_), channel_id=1, source_target_pairs={{16,0},{17,1},{18,2},{19,3},{20,4},{21,5},{22,6},{23,7},{24,8},{25... | collective-permute-start | bytes 196616 | tf_op jit(solution)/shard_map/ppermute | solution.py:122
  41.5 7.6 %collective-permute-start.5 = (bf16[4,32,256]{2,1,0:T(8,128)(2,1)S(1)}, bf16[4,32,256]{2,1,0:T(8,128)(2,1)S(1)}, u32[]{:S(2)}, u32[]{:S(2)}) collective-permute-start(bf16[4,32,256]{2,1,0:T(8,128)(2,1)S(1)} %get-tuple-element.13.refs_0_), channel_id=1, source_target_pairs={{48,0},{49,1},{50,2},{51,3},{52,4},{53,5},{54,6},{55,7},{56,8},{57... | collective-permute-start | bytes 196616 | tf_op jit(solution)/shard_map/ppermute | solution.py:122
  42.8 8.9 %collective-permute-start.6 = (bf16[4,32,256]{2,1,0:T(8,128)(2,1)S(1)}, bf16[4,32,256]{2,1,0:T(8,128)(2,1)S(1)}, u32[]{:S(2)}, u32[]{:S(2)}) collective-permute-start(bf16[4,32,256]{2,1,0:T(8,128)(2,1)S(1)} %get-tuple-element.13.refs_0_), channel_id=1, source_target_pairs={{64,0},{65,1},{66,2},{67,3},{68,4},{69,5},{70,6},{71,7},{72,8},{73... | collective-permute-start | bytes 196616 | tf_op jit(solution)/shard_map/ppermute | solution.py:122
  44.1 10.2 %collective-permute-start.7 = (bf16[4,32,256]{2,1,0:T(8,128)(2,1)S(1)}, bf16[4,32,256]{2,1,0:T(8,128)(2,1)S(1)}, u32[]{:S(2)}, u32[]{:S(2)}) collective-permute-start(bf16[4,32,256]{2,1,0:T(8,128)(2,1)S(1)} %get-tuple-element.13.refs_0_), channel_id=1, source_target_pairs={{80,0},{81,1},{82,2},{83,3},{84,4},{85,5},{86,6},{87,7},{88,8},{89... | collective-permute-start | bytes 196616 | tf_op jit(solution)/shard_map/ppermute | solution.py:122
  46.5 10.6 %collective-permute-start.8 = (bf16[4,32,256]{2,1,0:T(8,128)(2,1)S(1)}, bf16[4,32,256]{2,1,0:T(8,128)(2,1)S(1)}, u32[]{:S(2)}, u32[]{:S(2)}) collective-permute-start(bf16[4,32,256]{2,1,0:T(8,128)(2,1)S(1)} %get-tuple-element.13.refs_0_), channel_id=1, source_target_pairs={{96,0},{97,1},{98,2},{99,3},{100,4},{101,5},{102,6},{103,7},{104,8... | collective-permute-start | bytes 196616 | tf_op jit(solution)/shard_map/ppermute | solution.py:122
  47.8 9.3 %collective-permute-start.9 = (bf16[4,32,256]{2,1,0:T(8,128)(2,1)S(1)}, bf16[4,32,256]{2,1,0:T(8,128)(2,1)S(1)}, u32[]{:S(2)}, u32[]{:S(2)}) collective-permute-start(bf16[4,32,256]{2,1,0:T(8,128)(2,1)S(1)} %get-tuple-element.13.refs_0_), channel_id=1, source_target_pairs={{112,0},{113,1},{114,2},{115,3},{116,4},{117,5},{118,6},{119,7},{1... | collective-permute-start | bytes 196616 | tf_op jit(solution)/shard_map/ppermute | solution.py:122
  49.1 27.2 %collective-permute-start.11 = (bf16[8,128,256]{2,1,0:T(8,128)(2,1)}, bf16[8,128,256]{2,1,0:T(8,128)(2,1)S(1)}, u32[]{:S(2)}, u32[]{:S(2)}) collective-permute-start(bf16[8,128,256]{2,1,0:T(8,128)(2,1)} %get-tuple-element.7), channel_id=1, source_target_pairs={{0,128},{1,129},{2,130},{3,131},{4,132},{5,133},{6,134},{7,135},{8... | collective-permute-start | bytes 1572872 | tf_op jit(solution)/shard_map/ppermute | solution.py:111
  51.7 24.6 %collective-permute-start.12 = (bf16[8,128,256]{2,1,0:T(8,128)(2,1)}, bf16[8,128,256]{2,1,0:T(8,128)(2,1)S(1)}, u32[]{:S(2)}, u32[]{:S(2)}) collective-permute-start(bf16[8,128,256]{2,1,0:T(8,128)(2,1)} %get-tuple-element.7), channel_id=1, source_target_pairs={{0,256},{1,257},{2,258},{3,259},{4,260},{5,261},{6,262},{7,263},{8... | collective-permute-start | bytes 1572872 | tf_op jit(solution)/shard_map/ppermute | solution.py:111
  54.3 22.0 %collective-permute-start.13 = (bf16[8,128,256]{2,1,0:T(8,128)(2,1)}, bf16[8,128,256]{2,1,0:T(8,128)(2,1)}, u32[]{:S(2)}, u32[]{:S(2)}) collective-permute-start(bf16[8,128,256]{2,1,0:T(8,128)(2,1)} %get-tuple-element.7), channel_id=1, source_target_pairs={{0,384},{1,385},{2,386},{3,387},{4,388},{5,389},{6,390},{7,391},{8... | collective-permute-start | bytes 1572872 | tf_op jit(solution)/shard_map/ppermute | solution.py:111
  59.7 11.2 %all-to-all-start.2 = ((bf16[8,64,128]{2,1,0:T(8,128)(2,1)}), bf16[8,64,128]{2,1,0:T(8,128)(2,1)S(1)}, u32[]{:S(2)}, u32[]{:S(2)}) async-start(bf16[8,64,128]{2,1,0:T(8,128)(2,1)} %shard_map.50), calls=%async_computation.2 | async-start | bytes 262144 | tf_op jit(solution)/shard_map/all_to_all | solution.py:16
  80.1 12.5 %all-to-all-start.3 = ((bf16[8,64,128]{2,1,0:T(8,128)(2,1)}), bf16[8,64,128]{2,1,0:T(8,128)(2,1)S(1)}, u32[]{:S(2)}, u32[]{:S(2)}) async-start(bf16[8,64,128]{2,1,0:T(8,128)(2,1)} %shard_map.51), calls=%async_computation.3 | async-start | bytes 262144 | tf_op jit(solution)/shard_map/all_to_all | solution.py:16
  86.0 9.1 %collective-permute-start.16 = (bf16[4,32,256]{2,1,0:T(8,128)(2,1)S(1)}, bf16[4,32,256]{2,1,0:T(8,128)(2,1)S(1)}, u32[]{:S(2)}, u32[]{:S(2)}) collective-permute-start(bf16[4,32,256]{2,1,0:T(8,128)(2,1)S(1)} %get-tuple-element.12.refs_0_), channel_id=1, source_target_pairs={{48,0},{49,1},{50,2},{51,3},{52,4},{53,5},{54,6},{55,7},{56,8},{57... | collective-permute-start | bytes 196616 | tf_op jit(solution)/shard_map/ppermute | solution.py:122
  87.3 8.9 %collective-permute-start.17 = (bf16[4,32,256]{2,1,0:T(8,128)(2,1)S(1)}, bf16[4,32,256]{2,1,0:T(8,128)(2,1)S(1)}, u32[]{:S(2)}, u32[]{:S(2)}) collective-permute-start(bf16[4,32,256]{2,1,0:T(8,128)(2,1)S(1)} %get-tuple-element.12.refs_0_), channel_id=1, source_target_pairs={{64,0},{65,1},{66,2},{67,3},{68,4},{69,5},{70,6},{71,7},{72,8},{73... | collective-permute-start | bytes 196616 | tf_op jit(solution)/shard_map/ppermute | solution.py:122
  88.6 10.0 %collective-permute-start.18 = (bf16[4,32,256]{2,1,0:T(8,128)(2,1)S(1)}, bf16[4,32,256]{2,1,0:T(8,128)(2,1)S(1)}, u32[]{:S(2)}, u32[]{:S(2)}) collective-permute-start(bf16[4,32,256]{2,1,0:T(8,128)(2,1)S(1)} %get-tuple-element.12.refs_0_), channel_id=1, source_target_pairs={{80,0},{81,1},{82,2},{83,3},{84,4},{85,5},{86,6},{87,7},{88,8},{89... | collective-permute-start | bytes 196616 | tf_op jit(solution)/shard_map/ppermute | solution.py:122
  90.0 10.1 %collective-permute-start.19 = (bf16[4,32,256]{2,1,0:T(8,128)(2,1)S(1)}, bf16[4,32,256]{2,1,0:T(8,128)(2,1)S(1)}, u32[]{:S(2)}, u32[]{:S(2)}) collective-permute-start(bf16[4,32,256]{2,1,0:T(8,128)(2,1)S(1)} %get-tuple-element.12.refs_0_), channel_id=1, source_target_pairs={{96,0},{97,1},{98,2},{99,3},{100,4},{101,5},{102,6},{103,7},{104,8... | collective-permute-start | bytes 196616 | tf_op jit(solution)/shard_map/ppermute | solution.py:122
  91.3 10.1 %collective-permute-start.20 = (bf16[4,32,256]{2,1,0:T(8,128)(2,1)S(1)}, bf16[4,32,256]{2,1,0:T(8,128)(2,1)S(1)}, u32[]{:S(2)}, u32[]{:S(2)}) collective-permute-start(bf16[4,32,256]{2,1,0:T(8,128)(2,1)S(1)} %get-tuple-element.12.refs_0_), channel_id=1, source_target_pairs={{112,0},{113,1},{114,2},{115,3},{116,4},{117,5},{118,6},{119,7},{1... | collective-permute-start | bytes 196616 | tf_op jit(solution)/shard_map/ppermute | solution.py:122
  104.1 14.3 %all-to-all-start.4 = ((bf16[8,64,128]{2,1,0:T(8,128)(2,1)}), bf16[8,64,128]{2,1,0:T(8,128)(2,1)S(1)}, u32[]{:S(2)}, u32[]{:S(2)}) async-start(bf16[8,64,128]{2,1,0:T(8,128)(2,1)} %shard_map.52), calls=%async_computation.4 | async-start | bytes 262144 | tf_op jit(solution)/shard_map/all_to_all | solution.py:16
  130.3 8.1 %all-to-all-start.5 = ((bf16[4,2,64,128]{3,2,1,0:T(8,128)(2,1)}), bf16[4,2,64,128]{3,2,1,0:T(8,128)(2,1)S(1)}, u32[]{:S(2)}, u32[]{:S(2)}) async-start(bf16[4,2,64,128]{3,2,1,0:T(8,128)(2,1)} %broadcast_in_dim.35), calls=%async_computation.5 | async-start | bytes 262144 | tf_op jit(solution)/shard_map/all_to_all | solution.py:16
  (32 other events, 261.6 us)

commit v2 on v1

--- a/solution.py
+++ b/solution.py
@@ -28,12 +28,12 @@
     return jnp.sum(swap_blocks(split, "blk").astype(WIDE), axis=0)
 
 
-def assemble(planes, whole):
+def assemble(planes, step, whole):
     for z, plane in enumerate(planes):
-        count, size, _ = plane.shape
+        count, _, size, _ = plane.shape
         for x in range(count):
             at = (x * len(planes) + z) * size
-            whole[at : at + size, :] = plane[x]
+            whole[at : at + size, :] = plane[x, step]
 
 
 def write_blocks(value, whole, out):
@@ -44,7 +44,7 @@
 
 def first_kernel(pivot, *refs):
     planes, (out, whole) = refs[:NZ], refs[NZ:]
-    assemble(planes, whole)
+    assemble(planes, 0, whole)
     write_blocks(pivot[...], whole, out)
 
 
@@ -63,7 +63,7 @@
 
 def second_kernel(pivot, update, *refs):
     planes, (out, whole, value) = refs[:NZ], refs[NZ:]
-    assemble(planes, whole)
+    assemble(planes, 1, whole)
     half = update.shape[2]
     for c in range(NC):
         part = pivot[:, c * half : (c + 1) * half].astype(WIDE) - update[c]
@@ -117,9 +117,6 @@
     pair_order = order.reshape(NC, half, width).transpose(0, 2, 1)
     sizes = (n_blk, t, half, width)
 
-    def planes_of(k):
-        mine = inverse[:, k]
-        return [mine] + [lax.ppermute(mine, "z", [(source, 0)]) for source in range(1, NZ)]
 
     def ordered(value):
         return jnp.dot(value, order, preferred_element_type=WIDE).astype(HALF)
@@ -128,11 +125,10 @@
         pair = lax.all_gather(value, "core", axis=0, tiled=False)
         return jnp.concatenate([pair[0], pair[1]], axis=-1)
 
-    planes = planes_of(0)
+    planes = [inverse] + [lax.ppermute(inverse, "z", [(k, 0)]) for k in range(1, NZ)]
     partial = run_kernel(first_kernel, *sizes, (), pivot[0], *planes)
     first = scatter_sum(partial).astype(HALF)
     first, panels = lax.optimization_barrier((first, panels))
-    planes = planes_of(1)
     pair = lax.all_gather(first, "core", axis=0, tiled=False)
     partial = run_kernel(cross_kernel, *sizes, (), pair, pair_order, *cross)
     update = scatter_sum(partial)
@@ -156,7 +152,7 @@
         ],
         axis=1,
     )
-    extra = 512
+    extra = 128
     pick = jnp.arange(extra)
     at = pick // rows_local * width + row % per_blk * rows_local + pick % rows_local
     wanted = (pick < STEPS * rows_local) & (row // per_blk == blk)

time: 186 us -> 173 us (0.930)
  starting transfers between devices: 71.8 us -> 58.6 us
  blocking collectives: 52.6 us -> 59 us
  waiting for transfers between devices: 36.1 us -> 32 us
    ppermute x14 -> x7, starting transfers between devices: 18.1 us -> 9.15 us  [local(): lax.ppermute(inverse, 'z', [(k, 0)])]
    all_to_all x1 -> x2, blocking collectives: 37.4 us -> 44.2 us  [swap_blocks(): return lax.all_to_all(array, axis, split_axis=0, concat_axis=0, tiled=True)]
    all_to_all x6 -> x5, starting transfers between devices: 24.4 us -> 17.9 us  [swap_blocks(): return lax.all_to_all(array, axis, split_axis=0, concat_axis=0, tiled=True)]
    ppermute x14 -> x7, waiting for transfers between devices: 6.64 us -> 2.12 us  [local(): lax.ppermute(inverse, 'z', [(k, 0)])]
    ppermute x3, starting transfers between devices: 6.88 us -> 9.11 us  [local(): lax.ppermute(lower, ('x', 'z'), [(0, k * NZ)])]
    unnamed x46 -> x28, local copies, waits for them, and re-layouts: 4.11 us -> 3.37 us
    all_to_all x6 -> x5, waiting for transfers between devices: 28.5 us -> 29 us  [swap_blocks(): return lax.all_to_all(array, axis, split_axis=0, concat_axis=0, tiled=True)]
  transfers between devices with their start and end apart: 34 -> 26, of which waited for: 11 -> 8; matrix products, arithmetic and copies ran while one was open for 5% -> 4% of each run, Pallas kernels for 1% -> 1%
where the time goes in v2:
time: 173 us; the launch traced here: 172 us
  blocking collectives  59 us (34%)
  starting transfers between devices  58.6 us (34%)
  waiting for transfers between devices  32 us (18%)
  Pallas kernels  7.25 us (4%)
  local copies, waits for them, and re-layouts  7.23 us (4%)
  other arithmetic  5.61 us (3%)
    all_to_all x2, blocking collectives, swap_blocks(): return lax.all_to_all(array, axis, split_axis=0, concat_axis=0, tiled=True)  44.2 us
    all_to_all x5, waiting for transfers between devices, swap_blocks(): return lax.all_to_all(array, axis, split_axis=0, concat_axis=0, tiled=True)  29 us
    all_to_all x5, starting transfers between devices, swap_blocks(): return lax.all_to_all(array, axis, split_axis=0, concat_axis=0, tiled=True)  17.9 us
    ppermute x7, starting transfers between devices, local(): lax.ppermute(inverse, 'z', [(k, 0)])  9.15 us
    ppermute x3, starting transfers between devices, local(): lax.ppermute(lower, ('x', 'z'), [(0, k * NZ)])  9.11 us
    ppermute x7, starting transfers between devices, local(): spread = spread + lax.ppermute(solved, 'z', [(0, k)])  9.04 us
    ppermute x3, starting transfers between devices, local(): mine = mine + lax.ppermute(pivot[k], ('x', 'z'), [(0, k * NZ)])  7.42 us
    pallas_call x3, Pallas kernels, run_kernel(): pl.pallas_call(kernel, out_shape=jax.ShapeDtypeStruct((blocks, t, size),...  7.25 us
  transfers between devices with their start and end apart: 26, of which 8 were waited for; matrix products, arithmetic and copies ran while one was open for 4% of the time, Pallas kernels for 1%

profile of v2, /device:TPU:1, one launch (start us, length us, event | category | flops | bytes accessed | tf_op | source)
XLA Modules:
  0.0 172.1 jit_solution(17675546991469350034)
XLA Ops:
  1.6 3.9 %collective-permute-start = (bf16[8,2048]{1,0:T(8,128)(2,1)S(1)}, bf16[8,2048]{1,0:T(8,128)(2,1)S(1)}, u32[]{:S(2)}, u32[]{:S(2)}) collective-permute-start(bf16[8,2048]{1,0:T(8,128)(2,1)S(1)} %get-tuple-element.12), channel_id=1, source_target_pairs={{0,128},{1,129},{2,130},{3,131},{4,132},{5,133},{6,134},{7,135},{8... | collective-permute-start | bytes 98312 | tf_op jit(solution)/shard_map/ppermute | solution.py:100
  5.6 2.2 %collective-permute-start.1 = (bf16[8,2048]{1,0:T(8,128)(2,1)S(1)}, bf16[8,2048]{1,0:T(8,128)(2,1)S(1)}, u32[]{:S(2)}, u32[]{:S(2)}) collective-permute-start(bf16[8,2048]{1,0:T(8,128)(2,1)S(1)} %get-tuple-element.14), channel_id=1, source_target_pairs={{0,256},{1,257},{2,258},{3,259},{4,260},{5,261},{6,262},{7,263},{8... | collective-permute-start | bytes 98312 | tf_op jit(solution)/shard_map/ppermute | solution.py:100
  11.8 6.0 %collective-permute-start.10 = (bf16[8,128,256]{2,1,0:T(8,128)(2,1)}, bf16[8,128,256]{2,1,0:T(8,128)(2,1)}, u32[]{:S(2)}, u32[]{:S(2)}) collective-permute-start(bf16[8,128,256]{2,1,0:T(8,128)(2,1)} %slice_bitcast_fusion), channel_id=1, source_target_pairs={{8,0},{9,1},{10,2},{11,3},{12,4},{13,5},{14,6},{15,7}} | collective-permute-start | bytes 1572872 | tf_op jit(solution)/shard_map/ppermute | solution.py:108
  18.5 4.5 %all-to-all-start = ((bf16[8,8,256]{2,1,0:T(8,128)(2,1)}), bf16[8,8,256]{2,1,0:T(8,128)(2,1)S(1)}, u32[]{:S(2)}, u32[]{:S(2)}) async-start(bf16[8,8,256]{2,1,0:T(8,128)(2,1)} %bitcast.1), calls=%async_computation | async-start | bytes 65536 | tf_op jit(solution)/shard_map/all_to_all | solution.py:16
  23.0 6.9 %all-to-all-done = bf16[8,8,256]{2,1,0:T(8,128)(2,1)S(1)} async-done(((bf16[8,8,256]{2,1,0:T(8,128)(2,1)}), bf16[8,8,256]{2,1,0:T(8,128)(2,1)S(1)}, u32[]{:S(2)}, u32[]{:S(2)}) %all-to-all-start) | async-done | bytes 32800 | tf_op jit(solution)/shard_map/all_to_all | solution.py:16
  30.5 3.3 %all-to-all-start.1 = ((bf16[4,2,32,256]{3,2,1,0:T(8,128)(2,1)}), bf16[4,2,32,256]{3,2,1,0:T(8,128)(2,1)S(1)}, u32[]{:S(2)}, u32[]{:S(2)}) async-start(bf16[4,2,32,256]{3,2,1,0:T(8,128)(2,1)} %broadcast_in_dim.16), calls=%async_computation.1 | async-start | bytes 262144 | tf_op jit(solution)/shard_map/all_to_all | solution.py:16
  35.8 3.0 %all-to-all-done.1.refs_0_ = bf16[4,2,32,256]{3,2,1,0:T(8,128)(2,1)S(1)} async-done(((bf16[4,2,32,256]{3,2,1,0:T(8,128)(2,1)}), bf16[4,2,32,256]{3,2,1,0:T(8,128)(2,1)S(1)}, u32[]{:S(2)}, u32[]{:S(2)}) %all-to-all-start.1) | async-done | bytes 131104 | tf_op jit(solution)/shard_map/all_to_all | solution.py:16
  49.2 2.2 %collective-permute-start.11 = (bf16[8,128,256]{2,1,0:T(8,128)(2,1)}, bf16[8,128,256]{2,1,0:T(8,128)(2,1)S(1)}, u32[]{:S(2)}, u32[]{:S(2)}) collective-permute-start(bf16[8,128,256]{2,1,0:T(8,128)(2,1)} %get-tuple-element.7), channel_id=1, source_target_pairs={{0,128},{1,129},{2,130},{3,131},{4,132},{5,133},{6,134},{7,135},{8... | collective-permute-start | bytes 1572872 | tf_op jit(solution)/shard_map/ppermute | solution.py:111
  52.6 3.3 %collective-permute-start.12 = (bf16[8,128,256]{2,1,0:T(8,128)(2,1)}, bf16[8,128,256]{2,1,0:T(8,128)(2,1)}, u32[]{:S(2)}, u32[]{:S(2)}) collective-permute-start(bf16[8,128,256]{2,1,0:T(8,128)(2,1)} %get-tuple-element.7), channel_id=1, source_target_pairs={{0,256},{1,257},{2,258},{3,259},{4,260},{5,261},{6,262},{7,263},{8... | collective-permute-start | bytes 1572872 | tf_op jit(solution)/shard_map/ppermute | solution.py:111
  56.8 3.6 %collective-permute-start.13 = (bf16[8,128,256]{2,1,0:T(8,128)(2,1)}, bf16[8,128,256]{2,1,0:T(8,128)(2,1)}, u32[]{:S(2)}, u32[]{:S(2)}) collective-permute-start(bf16[8,128,256]{2,1,0:T(8,128)(2,1)} %get-tuple-element.7), channel_id=1, source_target_pairs={{0,384},{1,385},{2,386},{3,387},{4,388},{5,389},{6,390},{7,391},{8... | collective-permute-start | bytes 1572872 | tf_op jit(solution)/shard_map/ppermute | solution.py:111
  61.7 2.2 %shard_map.50 = bf16[8,64,128]{2,1,0:T(8,128)(2,1)} custom-call(bf16[64,256]{1,0:T(8,128)(2,1)} %get-tuple-element.15.pivot, bf16[4,2,32,256]{3,2,1,0:T(8,128)(2,1)} %copy-done, bf16[4,2,32,256]{3,2,1,0:T(8,128)(2,1)} %copy-done.3, bf16[4,2,32,256]{3,2,1,0:T(8,128)(2,1)} %copy-done.4, bf16[4,2,32,256]{3,2,1,0:T(8,128)(2,1)} %copy-done.5, ...), custom_call_target="tpu_custom_call" | custom-call | tf_op jit(solution)/shard_map/pallas_call | solution.py:75
  63.9 3.4 %all-to-all-start.2 = ((bf16[8,64,128]{2,1,0:T(8,128)(2,1)}), bf16[8,64,128]{2,1,0:T(8,128)(2,1)S(1)}, u32[]{:S(2)}, u32[]{:S(2)}) async-start(bf16[8,64,128]{2,1,0:T(8,128)(2,1)} %shard_map.50), calls=%async_computation.2 | async-start | bytes 262144 | tf_op jit(solution)/shard_map/all_to_all | solution.py:16
  68.0 7.2 %all-to-all-done.2 = bf16[8,64,128]{2,1,0:T(8,128)(2,1)S(1)} async-done(((bf16[8,64,128]{2,1,0:T(8,128)(2,1)}), bf16[8,64,128]{2,1,0:T(8,128)(2,1)S(1)}, u32[]{:S(2)}, u32[]{:S(2)}) %all-to-all-start.2) | async-done | bytes 131104 | tf_op jit(solution)/shard_map/all_to_all | solution.py:16
  75.3 4.6 %all-gather = bf16[128,128]{1,0:T(8,128)(2,1)} all-gather(bf16[64,128]{1,0:T(8,128)(2,1)S(1)} %reduce_sum.42), channel_id=2, replica_groups=mesh['x'=4,'z'=8,'core'=2,'blk'=8] {'core'}, dimensions={0}, use_global_device_ids=true | all-gather | bytes 49152 | tf_op jit(solution)/shard_map/all_gather | solution.py:132
  80.7 2.7 %shard_map.51 = bf16[8,64,128]{2,1,0:T(8,128)(2,1)} custom-call(bf16[2,64,128]{2,1,0:T(8,128)(2,1)} %bitcast.70, bf16[2,256,128]{2,1,0:T(8,128)(2,1)} %fusion.10.order, bf16[8,128,256]{2,1,0:T(8,128)(2,1)} %get-tuple-element.6.own, bf16[8,128,256]{2,1,0:T(8,128)(2,1)} %copy-done.10, bf16[8,128,256]{2,1,0:T(8,128)(2,1)} %collective-permute-done.12.refs_1_, ...), custom_call_target="tpu_custom_call" | custom-call | tf_op jit(solution)/shard_map/pallas_call | solution.py:75
  83.4 11.7 %all_to_all.35 = bf16[8,64,128]{2,1,0:T(8,128)(2,1)S(1)} all-to-all(bf16[8,64,128]{2,1,0:T(8,128)(2,1)} %shard_map.51), channel_id=1, replica_groups=mesh['x'=4,'z'=8,'core'=2,'blk'=8] {'blk'}, dimensions={0} | all-to-all | bytes 262144 | tf_op jit(solution)/shard_map/all_to_all | solution.py:16
  95.1 3.3 %all-gather.1 = f32[128,128]{1,0:T(8,128)} all-gather(f32[64,128]{1,0:T(8,128)S(1)} %convert_reduce_fusion.1), channel_id=3, replica_groups=mesh['x'=4,'z'=8,'core'=2,'blk'=8] {'core'}, dimensions={0}, use_global_device_ids=true | all-gather | bytes 98304 | tf_op jit(solution)/shard_map/all_gather | solution.py:135
  98.4 2.3 %shard_map.52 = bf16[8,64,128]{2,1,0:T(8,128)(2,1)} custom-call(bf16[64,256]{1,0:T(8,128)(2,1)} %get-tuple-element.16.pivot, f32[2,64,128]{2,1,0:T(8,128)} %bitcast.64, bf16[4,2,32,256]{3,2,1,0:T(8,128)(2,1)} %copy-done, bf16[4,2,32,256]{3,2,1,0:T(8,128)(2,1)} %copy-done.3, bf16[4,2,32,256]{3,2,1,0:T(8,128)(2,1)} %copy-done.4, ...), custom_call_target="tpu_custom_call" | custom-call | tf_op jit(solution)/shard_map/pallas_call | solution.py:75
  100.7 3.4 %all-to-all-start.4 = ((bf16[8,64,128]{2,1,0:T(8,128)(2,1)}), bf16[8,64,128]{2,1,0:T(8,128)(2,1)S(1)}, u32[]{:S(2)}, u32[]{:S(2)}) async-start(bf16[8,64,128]{2,1,0:T(8,128)(2,1)} %shard_map.52), calls=%async_computation.4 | async-start | bytes 262144 | tf_op jit(solution)/shard_map/all_to_all | solution.py:16
  104.1 8.2 %all-to-all-done.4 = bf16[8,64,128]{2,1,0:T(8,128)(2,1)S(1)} async-done(((bf16[8,64,128]{2,1,0:T(8,128)(2,1)}), bf16[8,64,128]{2,1,0:T(8,128)(2,1)S(1)}, u32[]{:S(2)}, u32[]{:S(2)}) %all-to-all-start.4) | async-done | bytes 131104 | tf_op jit(solution)/shard_map/all_to_all | solution.py:16
  123.3 3.3 %all-to-all-start.5 = ((bf16[4,2,64,128]{3,2,1,0:T(8,128)(2,1)}), bf16[4,2,64,128]{3,2,1,0:T(8,128)(2,1)S(1)}, u32[]{:S(2)}, u32[]{:S(2)}) async-start(bf16[4,2,64,128]{3,2,1,0:T(8,128)(2,1)} %broadcast_in_dim.35), calls=%async_computation.5 | async-start | bytes 262144 | tf_op jit(solution)/shard_map/all_to_all | solution.py:16
  127.8 3.7 %all-to-all-done.5 = bf16[4,2,64,128]{3,2,1,0:T(8,128)(2,1)S(1)} async-done(((bf16[4,2,64,128]{3,2,1,0:T(8,128)(2,1)}), bf16[4,2,64,128]{3,2,1,0:T(8,128)(2,1)S(1)}, u32[]{:S(2)}, u32[]{:S(2)}) %all-to-all-start.5) | async-done | bytes 131104 | tf_op jit(solution)/shard_map/all_to_all | solution.py:16
  131.4 5.0 %all-gather.2 = bf16[8,2,64,128]{3,2,1,0:T(8,128)(2,1)S(1)} all-gather(bf16[4,2,64,128]{3,2,1,0:T(8,128)(2,1)S(1)} %all-to-all-done.5), channel_id=4, replica_groups=mesh['x'=4,'z'=8,'core'=2,'blk'=8] {'core'}, dimensions={0}, use_global_device_ids=true | all-gather | bytes 393216 | tf_op jit(solution)/shard_map/all_gather | solution.py:125
  137.9 32.5 %all_to_all.36 = bf16[8,544,128]{2,1,0:T(8,128)(2,1)S(1)} all-to-all(bf16[8,544,128]{2,1,0:T(8,128)(2,1)S(1)} %bitcast.62), channel_id=1, replica_groups=mesh['x'=4,'z'=8,'core'=2,'blk'=8] {'blk'}, dimensions={0} | all-to-all | bytes 2228224 | tf_op jit(solution)/shard_map/all_to_all | solution.py:16
  (96 shorter events, 38.5 us)
Async XLA Ops:
  1.6 16.2 %collective-permute-start = (bf16[8,2048]{1,0:T(8,128)(2,1)S(1)}, bf16[8,2048]{1,0:T(8,128)(2,1)S(1)}, u32[]{:S(2)}, u32[]{:S(2)}) collective-permute-start(bf16[8,2048]{1,0:T(8,128)(2,1)S(1)} %get-tuple-element.12), channel_id=1, source_target_pairs={{0,128},{1,129},{2,130},{3,131},{4,132},{5,133},{6,134},{7,135},{8... | collective-permute-start | bytes 98312 | tf_op jit(solution)/shard_map/ppermute | solution.py:100
  5.6 12.3 %collective-permute-start.1 = (bf16[8,2048]{1,0:T(8,128)(2,1)S(1)}, bf16[8,2048]{1,0:T(8,128)(2,1)S(1)}, u32[]{:S(2)}, u32[]{:S(2)}) collective-permute-start(bf16[8,2048]{1,0:T(8,128)(2,1)S(1)} %get-tuple-element.14), channel_id=1, source_target_pairs={{0,256},{1,257},{2,258},{3,259},{4,260},{5,261},{6,262},{7,263},{8... | collective-permute-start | bytes 98312 | tf_op jit(solution)/shard_map/ppermute | solution.py:100
  7.8 10.1 %collective-permute-start.2 = (bf16[8,2048]{1,0:T(8,128)(2,1)S(1)}, bf16[8,2048]{1,0:T(8,128)(2,1)S(1)}, u32[]{:S(2)}, u32[]{:S(2)}) collective-permute-start(bf16[8,2048]{1,0:T(8,128)(2,1)S(1)} %get-tuple-element.13), channel_id=1, source_target_pairs={{0,384},{1,385},{2,386},{3,387},{4,388},{5,389},{6,390},{7,391},{8... | collective-permute-start | bytes 98312 | tf_op jit(solution)/shard_map/ppermute | solution.py:100
  11.8 32.3 %collective-permute-start.10 = (bf16[8,128,256]{2,1,0:T(8,128)(2,1)}, bf16[8,128,256]{2,1,0:T(8,128)(2,1)}, u32[]{:S(2)}, u32[]{:S(2)}) collective-permute-start(bf16[8,128,256]{2,1,0:T(8,128)(2,1)} %slice_bitcast_fusion), channel_id=1, source_target_pairs={{8,0},{9,1},{10,2},{11,3},{12,4},{13,5},{14,6},{15,7}} | collective-permute-start | bytes 1572872 | tf_op jit(solution)/shard_map/ppermute | solution.py:108
  18.5 11.4 %all-to-all-start = ((bf16[8,8,256]{2,1,0:T(8,128)(2,1)}), bf16[8,8,256]{2,1,0:T(8,128)(2,1)S(1)}, u32[]{:S(2)}, u32[]{:S(2)}) async-start(bf16[8,8,256]{2,1,0:T(8,128)(2,1)} %bitcast.1), calls=%async_computation | async-start | bytes 65536 | tf_op jit(solution)/shard_map/all_to_all | solution.py:16
  30.5 8.3 %all-to-all-start.1 = ((bf16[4,2,32,256]{3,2,1,0:T(8,128)(2,1)}), bf16[4,2,32,256]{3,2,1,0:T(8,128)(2,1)S(1)}, u32[]{:S(2)}, u32[]{:S(2)}) async-start(bf16[4,2,32,256]{3,2,1,0:T(8,128)(2,1)} %broadcast_in_dim.16), calls=%async_computation.1 | async-start | bytes 262144 | tf_op jit(solution)/shard_map/all_to_all | solution.py:16
  38.8 7.7 %collective-permute-start.3 = (bf16[4,2,32,256]{3,2,1,0:T(8,128)(2,1)S(1)}, bf16[4,2,32,256]{3,2,1,0:T(8,128)(2,1)S(1)}, u32[]{:S(2)}, u32[]{:S(2)}) collective-permute-start(bf16[4,2,32,256]{3,2,1,0:T(8,128)(2,1)S(1)} %all-to-all-done.1.refs_0_), channel_id=1, source_target_pairs={{16,0},{17,1},{18,2},{19,3},{20,4},{21,5},{22,6},{23,7},{24,8},{25... | collective-permute-start | bytes 393224 | tf_op jit(solution)/shard_map/ppermute | solution.py:128
  40.2 7.6 %collective-permute-start.4 = (bf16[4,2,32,256]{3,2,1,0:T(8,128)(2,1)S(1)}, bf16[4,2,32,256]{3,2,1,0:T(8,128)(2,1)S(1)}, u32[]{:S(2)}, u32[]{:S(2)}) collective-permute-start(bf16[4,2,32,256]{3,2,1,0:T(8,128)(2,1)S(1)} %all-to-all-done.1.refs_0_), channel_id=1, source_target_pairs={{32,0},{33,1},{34,2},{35,3},{36,4},{37,5},{38,6},{39,7},{40,8},{41... | collective-permute-start | bytes 393224 | tf_op jit(solution)/shard_map/ppermute | solution.py:128
  41.5 7.6 %collective-permute-start.5 = (bf16[4,2,32,256]{3,2,1,0:T(8,128)(2,1)S(1)}, bf16[4,2,32,256]{3,2,1,0:T(8,128)(2,1)S(1)}, u32[]{:S(2)}, u32[]{:S(2)}) collective-permute-start(bf16[4,2,32,256]{3,2,1,0:T(8,128)(2,1)S(1)} %all-to-all-done.1.refs_0_), channel_id=1, source_target_pairs={{48,0},{49,1},{50,2},{51,3},{52,4},{53,5},{54,6},{55,7},{56,8},{57... | collective-permute-start | bytes 393224 | tf_op jit(solution)/shard_map/ppermute | solution.py:128
  42.8 9.7 %collective-permute-start.6 = (bf16[4,2,32,256]{3,2,1,0:T(8,128)(2,1)S(1)}, bf16[4,2,32,256]{3,2,1,0:T(8,128)(2,1)S(1)}, u32[]{:S(2)}, u32[]{:S(2)}) collective-permute-start(bf16[4,2,32,256]{3,2,1,0:T(8,128)(2,1)S(1)} %all-to-all-done.1.refs_0_), channel_id=1, source_target_pairs={{64,0},{65,1},{66,2},{67,3},{68,4},{69,5},{70,6},{71,7},{72,8},{73... | collective-permute-start | bytes 393224 | tf_op jit(solution)/shard_map/ppermute | solution.py:128
  44.1 12.6 %collective-permute-start.7 = (bf16[4,2,32,256]{3,2,1,0:T(8,128)(2,1)S(1)}, bf16[4,2,32,256]{3,2,1,0:T(8,128)(2,1)S(1)}, u32[]{:S(2)}, u32[]{:S(2)}) collective-permute-start(bf16[4,2,32,256]{3,2,1,0:T(8,128)(2,1)S(1)} %all-to-all-done.1.refs_0_), channel_id=1, source_target_pairs={{80,0},{81,1},{82,2},{83,3},{84,4},{85,5},{86,6},{87,7},{88,8},{89... | collective-permute-start | bytes 393224 | tf_op jit(solution)/shard_map/ppermute | solution.py:128
  46.5 14.5 %collective-permute-start.8 = (bf16[4,2,32,256]{3,2,1,0:T(8,128)(2,1)S(1)}, bf16[4,2,32,256]{3,2,1,0:T(8,128)(2,1)S(1)}, u32[]{:S(2)}, u32[]{:S(2)}) collective-permute-start(bf16[4,2,32,256]{3,2,1,0:T(8,128)(2,1)S(1)} %all-to-all-done.1.refs_0_), channel_id=1, source_target_pairs={{96,0},{97,1},{98,2},{99,3},{100,4},{101,5},{102,6},{103,7},{104,8... | collective-permute-start | bytes 393224 | tf_op jit(solution)/shard_map/ppermute | solution.py:128
  47.8 13.2 %collective-permute-start.9 = (bf16[4,2,32,256]{3,2,1,0:T(8,128)(2,1)S(1)}, bf16[4,2,32,256]{3,2,1,0:T(8,128)(2,1)S(1)}, u32[]{:S(2)}, u32[]{:S(2)}) collective-permute-start(bf16[4,2,32,256]{3,2,1,0:T(8,128)(2,1)S(1)} %all-to-all-done.1.refs_0_), channel_id=1, source_target_pairs={{112,0},{113,1},{114,2},{115,3},{116,4},{117,5},{118,6},{119,7},{1... | collective-permute-start | bytes 393224 | tf_op jit(solution)/shard_map/ppermute | solution.py:128
  49.2 30.8 %collective-permute-start.11 = (bf16[8,128,256]{2,1,0:T(8,128)(2,1)}, bf16[8,128,256]{2,1,0:T(8,128)(2,1)S(1)}, u32[]{:S(2)}, u32[]{:S(2)}) collective-permute-start(bf16[8,128,256]{2,1,0:T(8,128)(2,1)} %get-tuple-element.7), channel_id=1, source_target_pairs={{0,128},{1,129},{2,130},{3,131},{4,132},{5,133},{6,134},{7,135},{8... | collective-permute-start | bytes 1572872 | tf_op jit(solution)/shard_map/ppermute | solution.py:111
  52.6 27.4 %collective-permute-start.12 = (bf16[8,128,256]{2,1,0:T(8,128)(2,1)}, bf16[8,128,256]{2,1,0:T(8,128)(2,1)}, u32[]{:S(2)}, u32[]{:S(2)}) collective-permute-start(bf16[8,128,256]{2,1,0:T(8,128)(2,1)} %get-tuple-element.7), channel_id=1, source_target_pairs={{0,256},{1,257},{2,258},{3,259},{4,260},{5,261},{6,262},{7,263},{8... | collective-permute-start | bytes 1572872 | tf_op jit(solution)/shard_map/ppermute | solution.py:111
  56.8 23.1 %collective-permute-start.13 = (bf16[8,128,256]{2,1,0:T(8,128)(2,1)}, bf16[8,128,256]{2,1,0:T(8,128)(2,1)}, u32[]{:S(2)}, u32[]{:S(2)}) collective-permute-start(bf16[8,128,256]{2,1,0:T(8,128)(2,1)} %get-tuple-element.7), channel_id=1, source_target_pairs={{0,384},{1,385},{2,386},{3,387},{4,388},{5,389},{6,390},{7,391},{8... | collective-permute-start | bytes 1572872 | tf_op jit(solution)/shard_map/ppermute | solution.py:111
  63.9 11.3 %all-to-all-start.2 = ((bf16[8,64,128]{2,1,0:T(8,128)(2,1)}), bf16[8,64,128]{2,1,0:T(8,128)(2,1)S(1)}, u32[]{:S(2)}, u32[]{:S(2)}) async-start(bf16[8,64,128]{2,1,0:T(8,128)(2,1)} %shard_map.50), calls=%async_computation.2 | async-start | bytes 262144 | tf_op jit(solution)/shard_map/all_to_all | solution.py:16
  100.7 11.7 %all-to-all-start.4 = ((bf16[8,64,128]{2,1,0:T(8,128)(2,1)}), bf16[8,64,128]{2,1,0:T(8,128)(2,1)S(1)}, u32[]{:S(2)}, u32[]{:S(2)}) async-start(bf16[8,64,128]{2,1,0:T(8,128)(2,1)} %shard_map.52), calls=%async_computation.4 | async-start | bytes 262144 | tf_op jit(solution)/shard_map/all_to_all | solution.py:16
  112.4 6.6 %collective-permute-start.14 = (bf16[2,64,128]{2,1,0:T(8,128)(2,1)S(1)}, bf16[2,64,128]{2,1,0:T(8,128)(2,1)S(1)}, u32[]{:S(2)}, u32[]{:S(2)}) collective-permute-start(bf16[2,64,128]{2,1,0:T(8,128)(2,1)S(1)} %pad_maximum_fusion), channel_id=1, source_target_pairs={{0,16},{1,17},{2,18},{3,19},{4,20},{5,21},{6,22},{7,23},{8,24},{9,... | collective-permute-start | bytes 98312 | tf_op jit(solution)/shard_map/ppermute | solution.py:143
  113.7 6.6 %collective-permute-start.15 = (bf16[2,64,128]{2,1,0:T(8,128)(2,1)S(1)}, bf16[2,64,128]{2,1,0:T(8,128)(2,1)S(1)}, u32[]{:S(2)}, u32[]{:S(2)}) collective-permute-start(bf16[2,64,128]{2,1,0:T(8,128)(2,1)S(1)} %pad_maximum_fusion), channel_id=1, source_target_pairs={{0,32},{1,33},{2,34},{3,35},{4,36},{5,37},{6,38},{7,39},{8,40},{9,... | collective-permute-start | bytes 98312 | tf_op jit(solution)/shard_map/ppermute | solution.py:143
  115.1 6.5 %collective-permute-start.16 = (bf16[2,64,128]{2,1,0:T(8,128)(2,1)S(1)}, bf16[2,64,128]{2,1,0:T(8,128)(2,1)S(1)}, u32[]{:S(2)}, u32[]{:S(2)}) collective-permute-start(bf16[2,64,128]{2,1,0:T(8,128)(2,1)S(1)} %pad_maximum_fusion), channel_id=1, source_target_pairs={{0,48},{1,49},{2,50},{3,51},{4,52},{5,53},{6,54},{7,55},{8,56},{9,... | collective-permute-start | bytes 98312 | tf_op jit(solution)/shard_map/ppermute | solution.py:143
  116.4 5.3 %collective-permute-start.17 = (bf16[2,64,128]{2,1,0:T(8,128)(2,1)S(1)}, bf16[2,64,128]{2,1,0:T(8,128)(2,1)S(1)}, u32[]{:S(2)}, u32[]{:S(2)}) collective-permute-start(bf16[2,64,128]{2,1,0:T(8,128)(2,1)S(1)} %pad_maximum_fusion), channel_id=1, source_target_pairs={{0,64},{1,65},{2,66},{3,67},{4,68},{5,69},{6,70},{7,71},{8,72},{9,... | collective-permute-start | bytes 98312 | tf_op jit(solution)/shard_map/ppermute | solution.py:143
  117.7 4.0 %collective-permute-start.18 = (bf16[2,64,128]{2,1,0:T(8,128)(2,1)S(1)}, bf16[2,64,128]{2,1,0:T(8,128)(2,1)S(1)}, u32[]{:S(2)}, u32[]{:S(2)}) collective-permute-start(bf16[2,64,128]{2,1,0:T(8,128)(2,1)S(1)} %pad_maximum_fusion), channel_id=1, source_target_pairs={{0,80},{1,81},{2,82},{3,83},{4,84},{5,85},{6,86},{7,87},{8,88},{9,... | collective-permute-start | bytes 98312 | tf_op jit(solution)/shard_map/ppermute | solution.py:143
  123.3 8.1 %all-to-all-start.5 = ((bf16[4,2,64,128]{3,2,1,0:T(8,128)(2,1)}), bf16[4,2,64,128]{3,2,1,0:T(8,128)(2,1)S(1)}, u32[]{:S(2)}, u32[]{:S(2)}) async-start(bf16[4,2,64,128]{3,2,1,0:T(8,128)(2,1)} %broadcast_in_dim.35), calls=%async_computation.5 | async-start | bytes 262144 | tf_op jit(solution)/shard_map/all_to_all | solution.py:16
  (15 other events, 157.2 us)

commit v3 on v2

--- a/solution.py
+++ b/solution.py
@@ -48,16 +48,26 @@
     write_blocks(pivot[...], whole, out)
 
 
-def cross_kernel(pair, order, own, *refs):
+def cross_kernel(owner, pair, order, own, *refs):
     others, (out, whole) = refs[: NX - 1], refs[NX - 1 :]
     value = product(pair[0], order[0])
     for c in range(1, NC):
         value = value + product(pair[c], order[c])
     blocks, size, _ = own.shape
-    for g in range(blocks):
-        whole[g * size : (g + 1) * size, :] = own[g]
-        for other in others:
-            whole[g * size : (g + 1) * size, :] += other[g]
+
+    @pl.when(owner[0] == 1)
+    def _():
+        for g in range(blocks):
+            whole[g * size : (g + 1) * size, :] = own[g]
+
+    @pl.when(owner[0] == 0)
+    def _():
+        for g in range(blocks):
+            part = others[0][g]
+            for other in others[1:]:
+                part = part + other[g]
+            whole[g * size : (g + 1) * size, :] = part
+
     write_blocks(value.astype(HALF), whole, out)
 
 
@@ -72,8 +82,10 @@
 
 
 def run_kernel(kernel, blocks, t, size, width, scratch, *operands):
+    spaces = [pltpu.SMEM if item.dtype == jnp.int32 else pltpu.VMEM for item in operands]
     return pl.pallas_call(
         kernel,
+        in_specs=[pl.BlockSpec(memory_space=space) for space in spaces],
         out_shape=jax.ShapeDtypeStruct((blocks, t, size), HALF),
         scratch_shapes=[pltpu.VMEM((blocks * size, width), HALF), *scratch],
     )(*operands)
@@ -107,8 +119,8 @@
     halves = panels[0].reshape(n_blk, NC, half, width)
     sent = lax.ppermute(halves[:, 0], ("x", "z", "core"), [(1, 0)])
     lower = jnp.where(core == 1, halves[:, 1], sent)
-    cross = [jnp.where((x == 0) & (z == 0), lower, jnp.zeros_like(lower))]
-    cross += [lax.ppermute(lower, ("x", "z"), [(0, k * NZ)]) for k in range(1, NX)]
+    owner = ((x == 0) & (z == 0)).astype(jnp.int32).reshape(1)
+    cross = [lower] + [lax.ppermute(lower, ("x", "z"), [(0, k * NZ)]) for k in range(1, NX)]
 
     place = jnp.arange(width)
     c_of, q_of, i_of = place // half, place % half // rows_local, place % rows_local
@@ -125,12 +137,20 @@
         pair = lax.all_gather(value, "core", axis=0, tiled=False)
         return jnp.concatenate([pair[0], pair[1]], axis=-1)
 
+    extra = 128
+    pick = jnp.arange(extra)
+    at = pick // rows_local * width + row % per_blk * rows_local + pick % rows_local
+    wanted = (pick < STEPS * rows_local) & (row // per_blk == blk)
+    select = wanted[:, None] & (at[:, None] == jnp.arange(STEPS * width)[None, :])
+    select = select.astype(HALF)
+    pivot, pair_order, order, select = lax.optimization_barrier((pivot, pair_order, order, select))
+
     planes = [inverse] + [lax.ppermute(inverse, "z", [(k, 0)]) for k in range(1, NZ)]
     partial = run_kernel(first_kernel, *sizes, (), pivot[0], *planes)
     first = scatter_sum(partial).astype(HALF)
     first, panels = lax.optimization_barrier((first, panels))
     pair = lax.all_gather(first, "core", axis=0, tiled=False)
-    partial = run_kernel(cross_kernel, *sizes, (), pair, pair_order, *cross)
+    partial = run_kernel(cross_kernel, *sizes, (), owner, pair, pair_order, *cross)
     update = scatter_sum(partial)
     pair = lax.all_gather(update, "core", axis=0, tiled=False)
     scratch = (pltpu.VMEM((t, width), HALF),)
@@ -152,12 +172,7 @@
         ],
         axis=1,
     )
-    extra = 128
-    pick = jnp.arange(extra)
-    at = pick // rows_local * width + row % per_blk * rows_local + pick % rows_local
-    wanted = (pick < STEPS * rows_local) & (row // per_blk == blk)
-    select = wanted[:, None] & (at[:, None] == jnp.arange(STEPS * width)[None, :])
-    panel = jnp.concatenate([panel, select.astype(HALF)], axis=0)
+    panel = jnp.concatenate([panel, select], axis=0)
 
     total = product(spread, panel).astype(HALF)
     lanes, rows8 = 128, 8

time: 173 us -> 181 us (1.046)
  blocking collectives: 59 us -> 72.5 us
  waiting for transfers between devices: 32 us -> 26.5 us
  starting transfers between devices: 58.6 us -> 55.4 us
  other arithmetic: 5.61 us -> 7.66 us
    all_to_all x5 -> x4, waiting for transfers between devices: 29 us -> 11.4 us  [swap_blocks(): return lax.all_to_all(array, axis, split_axis=0, concat_axis=0, tiled=True)]
    ppermute x7, waiting for transfers between devices: 2.12 us -> 14.1 us  [local(): lax.ppermute(inverse, 'z', [(k, 0)])]
    all_to_all x2 -> x3, blocking collectives: 44.2 us -> 55.9 us  [swap_blocks(): return lax.all_to_all(array, axis, split_axis=0, concat_axis=0, tiled=True)]
    ppermute x3, starting transfers between devices: 9.11 us -> 5.52 us  [local(): lax.ppermute(lower, ('x', 'z'), [(0, k * NZ)])]
    all_gather x1, blocking collectives: 1.99 us -> 4.24 us  [local(): pivot = lax.all_gather(pivot.reshape(t, width), 'core', axis=0, tiled=False)]
    unnamed x28 -> x24, local copies, waits for them, and re-layouts: 3.37 us -> 4 us
    all_to_all x5 -> x4, starting transfers between devices: 17.9 us -> 18.4 us  [swap_blocks(): return lax.all_to_all(array, axis, split_axis=0, concat_axis=0, tiled=True)]
  transfers between devices with their start and end apart: 26 -> 25, of which waited for: 8 -> 6; matrix products, arithmetic and copies ran while one was open for 4% -> 5% of each run, Pallas kernels for 1% -> 1%
where the time goes in v3:
time: 181 us; the launch traced here: 180 us
  blocking collectives  72.5 us (40%)
  starting transfers between devices  55.4 us (31%)
  waiting for transfers between devices  26.5 us (15%)
  local copies, waits for them, and re-layouts  8.52 us (5%)
  other arithmetic  7.66 us (4%)
  Pallas kernels  7.35 us (4%)
    all_to_all x3, blocking collectives, swap_blocks(): return lax.all_to_all(array, axis, split_axis=0, concat_axis=0, tiled=True)  55.9 us
    all_to_all x4, starting transfers between devices, swap_blocks(): return lax.all_to_all(array, axis, split_axis=0, concat_axis=0, tiled=True)  18.4 us
    ppermute x7, waiting for transfers between devices, local(): lax.ppermute(inverse, 'z', [(k, 0)])  14.1 us
    all_to_all x4, waiting for transfers between devices, swap_blocks(): return lax.all_to_all(array, axis, split_axis=0, concat_axis=0, tiled=True)  11.4 us
    ppermute x7, starting transfers between devices, local(): spread = spread + lax.ppermute(solved, 'z', [(0, k)])  9.04 us
    ppermute x7, starting transfers between devices, local(): lax.ppermute(inverse, 'z', [(k, 0)])  9.02 us
    ppermute x3, starting transfers between devices, local(): mine = mine + lax.ppermute(pivot[k], ('x', 'z'), [(0, k * NZ)])  7.77 us
    pallas_call x3, Pallas kernels, run_kernel(): pl.pallas_call(kernel, in_specs=[pl.BlockSpec(memory_space=space) for spa...  7.35 us
  transfers between devices with their start and end apart: 25, of which 6 were waited for; matrix products, arithmetic and copies ran while one was open for 5% of the time, Pallas kernels for 1%

profile of v3, /device:TPU:1, one launch (start us, length us, event | category | flops | bytes accessed | tf_op | source)
XLA Modules:
  0.0 180.0 jit_solution(11161040845567988426)
XLA Ops:
  2.2 5.2 %collective-permute-start.2 = (bf16[8,2048]{1,0:T(8,128)(2,1)}, bf16[8,2048]{1,0:T(8,128)(2,1)S(1)}, u32[]{:S(2)}, u32[]{:S(2)}) collective-permute-start(bf16[8,2048]{1,0:T(8,128)(2,1)} %get-tuple-element.19), channel_id=1, source_target_pairs={{0,384},{1,385},{2,386},{3,387},{4,388},{5,389},{6,390},{7,391},{8... | collective-permute-start | bytes 98312 | tf_op jit(solution)/shard_map/ppermute | solution.py:112
  11.5 3.3 %all-to-all-start.1 = ((bf16[4,2,32,256]{3,2,1,0:T(8,128)(2,1)}), bf16[4,2,32,256]{3,2,1,0:T(8,128)(2,1)S(1)}, u32[]{:S(2)}, u32[]{:S(2)}) async-start(bf16[4,2,32,256]{3,2,1,0:T(8,128)(2,1)} %broadcast_in_dim.13), calls=%async_computation.1 | async-start | bytes 262144 | tf_op jit(solution)/shard_map/all_to_all | solution.py:16
  14.9 1.9 %copy.24 = bf16[2048,2,256]{2,0,1:T(8,128)(2,1)S(1)} copy(bf16[2048,2,256]{2,1,0:T(2,128)(2,1)} %param.3) | data formatting | bytes 4194304 | tf_op args[0]
  17.7 5.6 %collective-permute-start.10 = (bf16[8,128,256]{2,1,0:T(8,128)(2,1)}, bf16[8,128,256]{2,1,0:T(8,128)(2,1)}, u32[]{:S(2)}, u32[]{:S(2)}) collective-permute-start(bf16[8,128,256]{2,1,0:T(8,128)(2,1)} %slice_bitcast_fusion), channel_id=1, source_target_pairs={{8,0},{9,1},{10,2},{11,3},{12,4},{13,5},{14,6},{15,7}} | collective-permute-start | bytes 1572872 | tf_op jit(solution)/shard_map/ppermute | solution.py:120
  25.5 4.8 %all-to-all-start = ((bf16[8,8,256]{2,1,0:T(8,128)(2,1)}), bf16[8,8,256]{2,1,0:T(8,128)(2,1)}, u32[]{:S(2)}, u32[]{:S(2)}) async-start(bf16[8,8,256]{2,1,0:T(8,128)(2,1)} %bitcast.1), calls=%async_computation | async-start | bytes 65536 | tf_op jit(solution)/shard_map/all_to_all | solution.py:16
  37.7 5.1 %collective-permute-done.3.refs_1_ = bf16[4,2,32,256]{3,2,1,0:T(8,128)(2,1)S(1)} collective-permute-done((bf16[4,2,32,256]{3,2,1,0:T(8,128)(2,1)S(1)}, bf16[4,2,32,256]{3,2,1,0:T(8,128)(2,1)S(1)}, u32[]{:S(2)}, u32[]{:S(2)}) %collective-permute-start.3) | collective-permute-done | bytes 131104 | tf_op jit(solution)/shard_map/ppermute | solution.py:148
  44.1 2.1 %collective-permute-start.12 = (bf16[8,128,256]{2,1,0:T(8,128)(2,1)}, bf16[8,128,256]{2,1,0:T(8,128)(2,1)}, u32[]{:S(2)}, u32[]{:S(2)}) collective-permute-start(bf16[8,128,256]{2,1,0:T(8,128)(2,1)} %fusion.6.own), channel_id=1, source_target_pairs={{0,256},{1,257},{2,258},{3,259},{4,260},{5,261},{6,262},{7,263},{8... | collective-permute-start | bytes 1572872 | tf_op jit(solution)/shard_map/ppermute | solution.py:123
  46.9 2.1 %collective-permute-start.13 = (bf16[8,128,256]{2,1,0:T(8,128)(2,1)}, bf16[8,128,256]{2,1,0:T(8,128)(2,1)}, u32[]{:S(2)}, u32[]{:S(2)}) collective-permute-start(bf16[8,128,256]{2,1,0:T(8,128)(2,1)} %fusion.6.own), channel_id=1, source_target_pairs={{0,384},{1,385},{2,386},{3,387},{4,388},{5,389},{6,390},{7,391},{8... | collective-permute-start | bytes 1572872 | tf_op jit(solution)/shard_map/ppermute | solution.py:123
  49.8 4.2 %all_gather.19 = bf16[2,64,256]{2,1,0:T(8,128)(2,1)S(1)} all-gather(bf16[1,64,256]{2,1,0:T(8,128)(2,1)} %bitcast.2), channel_id=1, replica_groups=mesh['x'=4,'z'=8,'core'=2,'blk'=8] {'core'}, dimensions={0}, use_global_device_ids=true | all-gather | bytes 98304 | tf_op jit(solution)/shard_map/all_gather | solution.py:116
  57.2 5.5 %collective-permute-done.8.refs_6_ = bf16[4,2,32,256]{3,2,1,0:T(8,128)(2,1)S(1)} collective-permute-done((bf16[4,2,32,256]{3,2,1,0:T(8,128)(2,1)S(1)}, bf16[4,2,32,256]{3,2,1,0:T(8,128)(2,1)S(1)}, u32[]{:S(2)}, u32[]{:S(2)}) %collective-permute-start.8) | collective-permute-done | bytes 131104 | tf_op jit(solution)/shard_map/ppermute | solution.py:148
  62.7 3.5 %collective-permute-done.9.refs_7_ = bf16[4,2,32,256]{3,2,1,0:T(8,128)(2,1)S(1)} collective-permute-done((bf16[4,2,32,256]{3,2,1,0:T(8,128)(2,1)S(1)}, bf16[4,2,32,256]{3,2,1,0:T(8,128)(2,1)S(1)}, u32[]{:S(2)}, u32[]{:S(2)}) %collective-permute-start.9) | collective-permute-done | bytes 131104 | tf_op jit(solution)/shard_map/ppermute | solution.py:148
  66.9 2.3 %shard_map.50 = bf16[8,64,128]{2,1,0:T(8,128)(2,1)} custom-call(bf16[64,256]{1,0:T(8,128)(2,1)} %get-tuple-element.21.pivot, bf16[4,2,32,256]{3,2,1,0:T(8,128)(2,1)} %copy-done, bf16[4,2,32,256]{3,2,1,0:T(8,128)(2,1)} %copy-done.3, bf16[4,2,32,256]{3,2,1,0:T(8,128)(2,1)} %copy-done.4, bf16[4,2,32,256]{3,2,1,0:T(8,128)(2,1)} %copy-done.5, ...), custom_call_target="tpu_custom_call" | custom-call | tf_op jit(solution)/shard_map/pallas_call | solution.py:86
  69.2 6.9 %all-to-all-start.2 = ((bf16[8,64,128]{2,1,0:T(8,128)(2,1)}), bf16[8,64,128]{2,1,0:T(8,128)(2,1)S(1)}, u32[]{:S(2)}, u32[]{:S(2)}) async-start(bf16[8,64,128]{2,1,0:T(8,128)(2,1)} %shard_map.50), calls=%async_computation.2 | async-start | bytes 262144 | tf_op jit(solution)/shard_map/all_to_all | solution.py:16
  76.0 7.8 %all-to-all-done.2 = bf16[8,64,128]{2,1,0:T(8,128)(2,1)S(1)} async-done(((bf16[8,64,128]{2,1,0:T(8,128)(2,1)}), bf16[8,64,128]{2,1,0:T(8,128)(2,1)S(1)}, u32[]{:S(2)}, u32[]{:S(2)}) %all-to-all-start.2) | async-done | bytes 131104 | tf_op jit(solution)/shard_map/all_to_all | solution.py:16
  83.8 3.9 %all-gather = bf16[128,128]{1,0:T(8,128)(2,1)} all-gather(bf16[64,128]{1,0:T(8,128)(2,1)S(1)} %reduce_sum.42), channel_id=2, replica_groups=mesh['x'=4,'z'=8,'core'=2,'blk'=8] {'core'}, dimensions={0}, use_global_device_ids=true | all-gather | bytes 49152 | tf_op jit(solution)/shard_map/all_gather | solution.py:152
  88.5 2.8 %shard_map.51 = bf16[8,64,128]{2,1,0:T(8,128)(2,1)} custom-call(s32[1]{0:T(128)} %bitcast.7.owner, bf16[2,64,128]{2,1,0:T(8,128)(2,1)} %bitcast.70, bf16[2,256,128]{2,1,0:T(8,128)(2,1)} %fusion.10.order, bf16[8,128,256]{2,1,0:T(8,128)(2,1)} %fusion.6.own, bf16[8,128,256]{2,1,0:T(8,128)(2,1)} %copy-done.9, ...), custom_call_target="tpu_custom_call" | custom-call | tf_op jit(solution)/shard_map/pallas_call | solution.py:86
  91.3 11.7 %all_to_all.35 = bf16[8,64,128]{2,1,0:T(8,128)(2,1)S(1)} all-to-all(bf16[8,64,128]{2,1,0:T(8,128)(2,1)} %shard_map.51), channel_id=1, replica_groups=mesh['x'=4,'z'=8,'core'=2,'blk'=8] {'blk'}, dimensions={0} | all-to-all | bytes 262144 | tf_op jit(solution)/shard_map/all_to_all | solution.py:16
  103.0 3.3 %all-gather.1 = f32[128,128]{1,0:T(8,128)} all-gather(f32[64,128]{1,0:T(8,128)S(1)} %convert_reduce_fusion.1), channel_id=3, replica_groups=mesh['x'=4,'z'=8,'core'=2,'blk'=8] {'core'}, dimensions={0}, use_global_device_ids=true | all-gather | bytes 98304 | tf_op jit(solution)/shard_map/all_gather | solution.py:155
  106.2 2.3 %shard_map.52 = bf16[8,64,128]{2,1,0:T(8,128)(2,1)} custom-call(bf16[64,256]{1,0:T(8,128)(2,1)} %get-tuple-element.22.pivot, f32[2,64,128]{2,1,0:T(8,128)} %bitcast.64, bf16[4,2,32,256]{3,2,1,0:T(8,128)(2,1)} %copy-done, bf16[4,2,32,256]{3,2,1,0:T(8,128)(2,1)} %copy-done.3, bf16[4,2,32,256]{3,2,1,0:T(8,128)(2,1)} %copy-done.4, ...), custom_call_target="tpu_custom_call" | custom-call | tf_op jit(solution)/shard_map/pallas_call | solution.py:86
  108.5 11.7 %all_to_all.36 = bf16[8,64,128]{2,1,0:T(8,128)(2,1)S(1)} all-to-all(bf16[8,64,128]{2,1,0:T(8,128)(2,1)} %shard_map.52), channel_id=1, replica_groups=mesh['x'=4,'z'=8,'core'=2,'blk'=8] {'blk'}, dimensions={0} | all-to-all | bytes 262144 | tf_op jit(solution)/shard_map/all_to_all | solution.py:16
  131.1 3.3 %all-to-all-start.5 = ((bf16[4,2,64,128]{3,2,1,0:T(8,128)(2,1)}), bf16[4,2,64,128]{3,2,1,0:T(8,128)(2,1)S(1)}, u32[]{:S(2)}, u32[]{:S(2)}) async-start(bf16[4,2,64,128]{3,2,1,0:T(8,128)(2,1)} %broadcast_in_dim.15), calls=%async_computation.5 | async-start | bytes 262144 | tf_op jit(solution)/shard_map/all_to_all | solution.py:16
  135.5 3.7 %all-to-all-done.5 = bf16[4,2,64,128]{3,2,1,0:T(8,128)(2,1)S(1)} async-done(((bf16[4,2,64,128]{3,2,1,0:T(8,128)(2,1)}), bf16[4,2,64,128]{3,2,1,0:T(8,128)(2,1)S(1)}, u32[]{:S(2)}, u32[]{:S(2)}) %all-to-all-start.5) | async-done | bytes 131104 | tf_op jit(solution)/shard_map/all_to_all | solution.py:16
  139.2 5.2 %all-gather.2 = bf16[8,2,64,128]{3,2,1,0:T(8,128)(2,1)S(1)} all-gather(bf16[4,2,64,128]{3,2,1,0:T(8,128)(2,1)S(1)} %all-to-all-done.5), channel_id=4, replica_groups=mesh['x'=4,'z'=8,'core'=2,'blk'=8] {'core'}, dimensions={0}, use_global_device_ids=true | all-gather | bytes 393216 | tf_op jit(solution)/shard_map/all_gather | solution.py:137
  145.8 32.6 %all_to_all.37 = bf16[8,544,128]{2,1,0:T(8,128)(2,1)S(1)} all-to-all(bf16[8,544,128]{2,1,0:T(8,128)(2,1)S(1)} %bitcast.62), channel_id=1, replica_groups=mesh['x'=4,'z'=8,'core'=2,'blk'=8] {'blk'}, dimensions={0} | all-to-all | bytes 2228224 | tf_op jit(solution)/shard_map/all_to_all | solution.py:16
  (92 shorter events, 38.3 us)
Async XLA Ops:
  2.2 22.6 %collective-permute-start.2 = (bf16[8,2048]{1,0:T(8,128)(2,1)}, bf16[8,2048]{1,0:T(8,128)(2,1)S(1)}, u32[]{:S(2)}, u32[]{:S(2)}) collective-permute-start(bf16[8,2048]{1,0:T(8,128)(2,1)} %get-tuple-element.19), channel_id=1, source_target_pairs={{0,384},{1,385},{2,386},{3,387},{4,388},{5,389},{6,390},{7,391},{8... | collective-permute-start | bytes 98312 | tf_op jit(solution)/shard_map/ppermute | solution.py:112
  7.4 17.4 %collective-permute-start.1 = (bf16[8,2048]{1,0:T(8,128)(2,1)}, bf16[8,2048]{1,0:T(8,128)(2,1)S(1)}, u32[]{:S(2)}, u32[]{:S(2)}) collective-permute-start(bf16[8,2048]{1,0:T(8,128)(2,1)} %get-tuple-element.20), channel_id=1, source_target_pairs={{0,256},{1,257},{2,258},{3,259},{4,260},{5,261},{6,262},{7,263},{8... | collective-permute-start | bytes 98312 | tf_op jit(solution)/shard_map/ppermute | solution.py:112
  8.7 16.1 %collective-permute-start = (bf16[8,2048]{1,0:T(8,128)(2,1)S(1)}, bf16[8,2048]{1,0:T(8,128)(2,1)S(1)}, u32[]{:S(2)}, u32[]{:S(2)}) collective-permute-start(bf16[8,2048]{1,0:T(8,128)(2,1)S(1)} %get-tuple-element.18), channel_id=1, source_target_pairs={{0,128},{1,129},{2,130},{3,131},{4,132},{5,133},{6,134},{7,135},{8... | collective-permute-start | bytes 98312 | tf_op jit(solution)/shard_map/ppermute | solution.py:112
  11.5 13.9 %all-to-all-start.1 = ((bf16[4,2,32,256]{3,2,1,0:T(8,128)(2,1)}), bf16[4,2,32,256]{3,2,1,0:T(8,128)(2,1)S(1)}, u32[]{:S(2)}, u32[]{:S(2)}) async-start(bf16[4,2,32,256]{3,2,1,0:T(8,128)(2,1)} %broadcast_in_dim.13), calls=%async_computation.1 | async-start | bytes 262144 | tf_op jit(solution)/shard_map/all_to_all | solution.py:16
  17.7 17.9 %collective-permute-start.10 = (bf16[8,128,256]{2,1,0:T(8,128)(2,1)}, bf16[8,128,256]{2,1,0:T(8,128)(2,1)}, u32[]{:S(2)}, u32[]{:S(2)}) collective-permute-start(bf16[8,128,256]{2,1,0:T(8,128)(2,1)} %slice_bitcast_fusion), channel_id=1, source_target_pairs={{8,0},{9,1},{10,2},{11,3},{12,4},{13,5},{14,6},{15,7}} | collective-permute-start | bytes 1572872 | tf_op jit(solution)/shard_map/ppermute | solution.py:120
  25.5 24.3 %all-to-all-start = ((bf16[8,8,256]{2,1,0:T(8,128)(2,1)}), bf16[8,8,256]{2,1,0:T(8,128)(2,1)}, u32[]{:S(2)}, u32[]{:S(2)}) async-start(bf16[8,8,256]{2,1,0:T(8,128)(2,1)} %bitcast.1), calls=%async_computation | async-start | bytes 65536 | tf_op jit(solution)/shard_map/all_to_all | solution.py:16
  30.3 12.4 %collective-permute-start.3 = (bf16[4,2,32,256]{3,2,1,0:T(8,128)(2,1)S(1)}, bf16[4,2,32,256]{3,2,1,0:T(8,128)(2,1)S(1)}, u32[]{:S(2)}, u32[]{:S(2)}) collective-permute-start(bf16[4,2,32,256]{3,2,1,0:T(8,128)(2,1)S(1)} %all-to-all-done.1.refs_0_), channel_id=1, source_target_pairs={{16,0},{17,1},{18,2},{19,3},{20,4},{21,5},{22,6},{23,7},{24,8},{25... | collective-permute-start | bytes 393224 | tf_op jit(solution)/shard_map/ppermute | solution.py:148
  31.6 12.5 %collective-permute-start.4 = (bf16[4,2,32,256]{3,2,1,0:T(8,128)(2,1)S(1)}, bf16[4,2,32,256]{3,2,1,0:T(8,128)(2,1)S(1)}, u32[]{:S(2)}, u32[]{:S(2)}) collective-permute-start(bf16[4,2,32,256]{3,2,1,0:T(8,128)(2,1)S(1)} %all-to-all-done.1.refs_0_), channel_id=1, source_target_pairs={{32,0},{33,1},{34,2},{35,3},{36,4},{37,5},{38,6},{39,7},{40,8},{41... | collective-permute-start | bytes 393224 | tf_op jit(solution)/shard_map/ppermute | solution.py:148
  32.9 13.3 %collective-permute-start.5 = (bf16[4,2,32,256]{3,2,1,0:T(8,128)(2,1)S(1)}, bf16[4,2,32,256]{3,2,1,0:T(8,128)(2,1)S(1)}, u32[]{:S(2)}, u32[]{:S(2)}) collective-permute-start(bf16[4,2,32,256]{3,2,1,0:T(8,128)(2,1)S(1)} %all-to-all-done.1.refs_0_), channel_id=1, source_target_pairs={{48,0},{49,1},{50,2},{51,3},{52,4},{53,5},{54,6},{55,7},{56,8},{57... | collective-permute-start | bytes 393224 | tf_op jit(solution)/shard_map/ppermute | solution.py:148
  34.2 19.8 %collective-permute-start.6 = (bf16[4,2,32,256]{3,2,1,0:T(8,128)(2,1)S(1)}, bf16[4,2,32,256]{3,2,1,0:T(8,128)(2,1)}, u32[]{:S(2)}, u32[]{:S(2)}) collective-permute-start(bf16[4,2,32,256]{3,2,1,0:T(8,128)(2,1)S(1)} %all-to-all-done.1.refs_0_), channel_id=1, source_target_pairs={{64,0},{65,1},{66,2},{67,3},{68,4},{69,5},{70,6},{71,7},{72,8},{73... | collective-permute-start | bytes 393224 | tf_op jit(solution)/shard_map/ppermute | solution.py:148
  35.5 19.8 %collective-permute-start.7 = (bf16[4,2,32,256]{3,2,1,0:T(8,128)(2,1)S(1)}, bf16[4,2,32,256]{3,2,1,0:T(8,128)(2,1)}, u32[]{:S(2)}, u32[]{:S(2)}) collective-permute-start(bf16[4,2,32,256]{3,2,1,0:T(8,128)(2,1)S(1)} %all-to-all-done.1.refs_0_), channel_id=1, source_target_pairs={{80,0},{81,1},{82,2},{83,3},{84,4},{85,5},{86,6},{87,7},{88,8},{89... | collective-permute-start | bytes 393224 | tf_op jit(solution)/shard_map/ppermute | solution.py:148
  42.8 44.9 %collective-permute-start.11 = (bf16[8,128,256]{2,1,0:T(8,128)(2,1)}, bf16[8,128,256]{2,1,0:T(8,128)(2,1)S(1)}, u32[]{:S(2)}, u32[]{:S(2)}) collective-permute-start(bf16[8,128,256]{2,1,0:T(8,128)(2,1)} %fusion.6.own), channel_id=1, source_target_pairs={{0,128},{1,129},{2,130},{3,131},{4,132},{5,133},{6,134},{7,135},{8... | collective-permute-start | bytes 1572872 | tf_op jit(solution)/shard_map/ppermute | solution.py:123
  44.1 43.6 %collective-permute-start.12 = (bf16[8,128,256]{2,1,0:T(8,128)(2,1)}, bf16[8,128,256]{2,1,0:T(8,128)(2,1)}, u32[]{:S(2)}, u32[]{:S(2)}) collective-permute-start(bf16[8,128,256]{2,1,0:T(8,128)(2,1)} %fusion.6.own), channel_id=1, source_target_pairs={{0,256},{1,257},{2,258},{3,259},{4,260},{5,261},{6,262},{7,263},{8... | collective-permute-start | bytes 1572872 | tf_op jit(solution)/shard_map/ppermute | solution.py:123
  46.9 40.8 %collective-permute-start.13 = (bf16[8,128,256]{2,1,0:T(8,128)(2,1)}, bf16[8,128,256]{2,1,0:T(8,128)(2,1)}, u32[]{:S(2)}, u32[]{:S(2)}) collective-permute-start(bf16[8,128,256]{2,1,0:T(8,128)(2,1)} %fusion.6.own), channel_id=1, source_target_pairs={{0,384},{1,385},{2,386},{3,387},{4,388},{5,389},{6,390},{7,391},{8... | collective-permute-start | bytes 1572872 | tf_op jit(solution)/shard_map/ppermute | solution.py:123
  54.0 8.7 %collective-permute-start.8 = (bf16[4,2,32,256]{3,2,1,0:T(8,128)(2,1)S(1)}, bf16[4,2,32,256]{3,2,1,0:T(8,128)(2,1)S(1)}, u32[]{:S(2)}, u32[]{:S(2)}) collective-permute-start(bf16[4,2,32,256]{3,2,1,0:T(8,128)(2,1)S(1)} %all-to-all-done.1.refs_0_), channel_id=1, source_target_pairs={{96,0},{97,1},{98,2},{99,3},{100,4},{101,5},{102,6},{103,7},{104,8... | collective-permute-start | bytes 393224 | tf_op jit(solution)/shard_map/ppermute | solution.py:148
  55.3 10.9 %collective-permute-start.9 = (bf16[4,2,32,256]{3,2,1,0:T(8,128)(2,1)S(1)}, bf16[4,2,32,256]{3,2,1,0:T(8,128)(2,1)S(1)}, u32[]{:S(2)}, u32[]{:S(2)}) collective-permute-start(bf16[4,2,32,256]{3,2,1,0:T(8,128)(2,1)S(1)} %all-to-all-done.1.refs_0_), channel_id=1, source_target_pairs={{112,0},{113,1},{114,2},{115,3},{116,4},{117,5},{118,6},{119,7},{1... | collective-permute-start | bytes 393224 | tf_op jit(solution)/shard_map/ppermute | solution.py:148
  69.2 14.6 %all-to-all-start.2 = ((bf16[8,64,128]{2,1,0:T(8,128)(2,1)}), bf16[8,64,128]{2,1,0:T(8,128)(2,1)S(1)}, u32[]{:S(2)}, u32[]{:S(2)}) async-start(bf16[8,64,128]{2,1,0:T(8,128)(2,1)} %shard_map.50), calls=%async_computation.2 | async-start | bytes 262144 | tf_op jit(solution)/shard_map/all_to_all | solution.py:16
  120.2 6.5 %collective-permute-start.20 = (bf16[2,64,128]{2,1,0:T(8,128)(2,1)S(1)}, bf16[2,64,128]{2,1,0:T(8,128)(2,1)S(1)}, u32[]{:S(2)}, u32[]{:S(2)}) collective-permute-start(bf16[2,64,128]{2,1,0:T(8,128)(2,1)S(1)} %pad_maximum_fusion), channel_id=1, source_target_pairs={{0,112},{1,113},{2,114},{3,115},{4,116},{5,117},{6,118},{7,119},{8... | collective-permute-start | bytes 98312 | tf_op jit(solution)/shard_map/ppermute | solution.py:163
  121.5 6.5 %collective-permute-start.19 = (bf16[2,64,128]{2,1,0:T(8,128)(2,1)S(1)}, bf16[2,64,128]{2,1,0:T(8,128)(2,1)S(1)}, u32[]{:S(2)}, u32[]{:S(2)}) collective-permute-start(bf16[2,64,128]{2,1,0:T(8,128)(2,1)S(1)} %pad_maximum_fusion), channel_id=1, source_target_pairs={{0,96},{1,97},{2,98},{3,99},{4,100},{5,101},{6,102},{7,103},{8,104... | collective-permute-start | bytes 98312 | tf_op jit(solution)/shard_map/ppermute | solution.py:163
  122.8 6.5 %collective-permute-start.18 = (bf16[2,64,128]{2,1,0:T(8,128)(2,1)S(1)}, bf16[2,64,128]{2,1,0:T(8,128)(2,1)S(1)}, u32[]{:S(2)}, u32[]{:S(2)}) collective-permute-start(bf16[2,64,128]{2,1,0:T(8,128)(2,1)S(1)} %pad_maximum_fusion), channel_id=1, source_target_pairs={{0,80},{1,81},{2,82},{3,83},{4,84},{5,85},{6,86},{7,87},{8,88},{9,... | collective-permute-start | bytes 98312 | tf_op jit(solution)/shard_map/ppermute | solution.py:163
  124.1 5.2 %collective-permute-start.17 = (bf16[2,64,128]{2,1,0:T(8,128)(2,1)S(1)}, bf16[2,64,128]{2,1,0:T(8,128)(2,1)S(1)}, u32[]{:S(2)}, u32[]{:S(2)}) collective-permute-start(bf16[2,64,128]{2,1,0:T(8,128)(2,1)S(1)} %pad_maximum_fusion), channel_id=1, source_target_pairs={{0,64},{1,65},{2,66},{3,67},{4,68},{5,69},{6,70},{7,71},{8,72},{9,... | collective-permute-start | bytes 98312 | tf_op jit(solution)/shard_map/ppermute | solution.py:163
  125.4 4.0 %collective-permute-start.16 = (bf16[2,64,128]{2,1,0:T(8,128)(2,1)S(1)}, bf16[2,64,128]{2,1,0:T(8,128)(2,1)S(1)}, u32[]{:S(2)}, u32[]{:S(2)}) collective-permute-start(bf16[2,64,128]{2,1,0:T(8,128)(2,1)S(1)} %pad_maximum_fusion), channel_id=1, source_target_pairs={{0,48},{1,49},{2,50},{3,51},{4,52},{5,53},{6,54},{7,55},{8,56},{9,... | collective-permute-start | bytes 98312 | tf_op jit(solution)/shard_map/ppermute | solution.py:163
  126.7 2.7 %collective-permute-start.15 = (bf16[2,64,128]{2,1,0:T(8,128)(2,1)S(1)}, bf16[2,64,128]{2,1,0:T(8,128)(2,1)S(1)}, u32[]{:S(2)}, u32[]{:S(2)}) collective-permute-start(bf16[2,64,128]{2,1,0:T(8,128)(2,1)S(1)} %pad_maximum_fusion), channel_id=1, source_target_pairs={{0,32},{1,33},{2,34},{3,35},{4,36},{5,37},{6,38},{7,39},{8,40},{9,... | collective-permute-start | bytes 98312 | tf_op jit(solution)/shard_map/ppermute | solution.py:163
  131.1 8.1 %all-to-all-start.5 = ((bf16[4,2,64,128]{3,2,1,0:T(8,128)(2,1)}), bf16[4,2,64,128]{3,2,1,0:T(8,128)(2,1)S(1)}, u32[]{:S(2)}, u32[]{:S(2)}) async-start(bf16[4,2,64,128]{3,2,1,0:T(8,128)(2,1)} %broadcast_in_dim.15), calls=%async_computation.5 | async-start | bytes 262144 | tf_op jit(solution)/shard_map/all_to_all | solution.py:16
  (12 other events, 156.0 us)

commit v4 on v3

--- a/solution.py
+++ b/solution.py
@@ -38,8 +38,9 @@
 
 def write_blocks(value, whole, out):
     size = out.shape[2]
+    total = product(value, whole[...]).astype(out.dtype)
     for g in range(out.shape[0]):
-        out[g] = product(value, whole[g * size : (g + 1) * size, :]).astype(out.dtype)
+        out[g] = total[:, g * size : (g + 1) * size]
 
 
 def first_kernel(pivot, *refs):
@@ -106,13 +107,15 @@
     per_blk = width // rows_local
     half = width // NC
 
-    pivot = right_side.astype(HALF).reshape(NX, dates_x, pixels)
-    mine = jnp.where(x == 0, pivot[0], jnp.zeros_like(pivot[0]))
-    for k in range(1, NX):
-        mine = mine + lax.ppermute(pivot[k], ("x", "z"), [(0, k * NZ)])
-
-    inverse = gather_by_swap(block_inverse.astype(HALF), "x", NX)
-    pivot = swap_blocks(mine.reshape(dates_x, n_blk, width).transpose(1, 0, 2), "blk")
+    copies = block_inverse.astype(HALF).reshape(1, STEPS * rows_local, width)
+    copies = jnp.broadcast_to(copies, (NX, *copies.shape[1:]))
+    pivot = right_side.astype(HALF).reshape(NX, dates_x, n_blk, width)
+    pivot = pivot.transpose(0, 2, 1, 3).reshape(NX, n_blk * dates_x, width)
+    both = swap_blocks(jnp.concatenate([copies, pivot], axis=1), "x")
+    inverse = both[:, : STEPS * rows_local].reshape(NX, STEPS, rows_local, width)
+    mine = both[0, STEPS * rows_local :].reshape(n_blk, dates_x, width)
+
+    pivot = swap_blocks(mine, "blk")
     pivot = lax.all_gather(pivot.reshape(t, width), "core", axis=0, tiled=False)
 
     panels = factor_panel.transpose(1, 0, 2)
@@ -143,7 +146,6 @@
     wanted = (pick < STEPS * rows_local) & (row // per_blk == blk)
     select = wanted[:, None] & (at[:, None] == jnp.arange(STEPS * width)[None, :])
     select = select.astype(HALF)
-    pivot, pair_order, order, select = lax.optimization_barrier((pivot, pair_order, order, select))
 
     planes = [inverse] + [lax.ppermute(inverse, "z", [(k, 0)]) for k in range(1, NZ)]
     partial = run_kernel(first_kernel, *sizes, (), pivot[0], *planes)

time: 181 us -> 169 us (0.934)
  blocking collectives: 72.5 us -> 67.4 us
  starting transfers between devices: 55.4 us -> 51.1 us
  other arithmetic: 7.66 us -> 4.55 us
    ppermute x7, waiting for transfers between devices: 14.1 us -> 5.4 us  [local(): lax.ppermute(inverse, 'z', [(k, 0)])]
    all_to_all x4, waiting for transfers between devices: 11.4 us -> 19.7 us  [swap_blocks(): return lax.all_to_all(array, axis, split_axis=0, concat_axis=0, tiled=True)]
    ppermute x3 -> x0, starting transfers between devices: 7.77 us -> none  [local(): mine = mine + lax.ppermute(pivot[k], ('x', 'z'), [(0, k * NZ)])]
    ppermute x1, starting transfers between devices: 5.64 us -> 9.55 us  [local(): sent = lax.ppermute(halves[:, 0], ('x', 'z', 'core'), [(1, 0)])]
    all_to_all x3, blocking collectives: 55.9 us -> 52.5 us  [swap_blocks(): return lax.all_to_all(array, axis, split_axis=0, concat_axis=0, tiled=True)]
    all_to_all x4, starting transfers between devices: 18.4 us -> 15.6 us  [swap_blocks(): return lax.all_to_all(array, axis, split_axis=0, concat_axis=0, tiled=True)]
    ppermute x3, starting transfers between devices: 5.52 us -> 7.93 us  [local(): lax.ppermute(lower, ('x', 'z'), [(0, k * NZ)])]
    unnamed x24 -> x22, local copies, waits for them, and re-layouts: 4 us -> 4.04 us
  transfers between devices with their start and end apart: 25 -> 22, of which waited for: 6 -> 8; matrix products, arithmetic and copies ran while one was open for 5% -> 3% of each run, Pallas kernels for 1% -> 1%
where the time goes in v4:
time: 169 us; the launch traced here: 167 us
  blocking collectives  67.4 us (40%)
  starting transfers between devices  51.1 us (30%)
  waiting for transfers between devices  26.1 us (15%)
  local copies, waits for them, and re-layouts  8.79 us (5%)
  Pallas kernels  7.22 us (4%)
  other arithmetic  4.55 us (3%)
    all_to_all x3, blocking collectives, swap_blocks(): return lax.all_to_all(array, axis, split_axis=0, concat_axis=0, tiled=True)  52.5 us
    all_to_all x4, waiting for transfers between devices, swap_blocks(): return lax.all_to_all(array, axis, split_axis=0, concat_axis=0, tiled=True)  19.7 us
    all_to_all x4, starting transfers between devices, swap_blocks(): return lax.all_to_all(array, axis, split_axis=0, concat_axis=0, tiled=True)  15.6 us
    ppermute x1, starting transfers between devices, local(): sent = lax.ppermute(halves[:, 0], ('x', 'z', 'core'), [(1, 0)])  9.55 us
    ppermute x7, starting transfers between devices, local(): spread = spread + lax.ppermute(solved, 'z', [(0, k)])  9.03 us
    ppermute x7, starting transfers between devices, local(): lax.ppermute(inverse, 'z', [(k, 0)])  9.02 us
    ppermute x3, starting transfers between devices, local(): lax.ppermute(lower, ('x', 'z'), [(0, k * NZ)])  7.93 us
    pallas_call x3, Pallas kernels, run_kernel(): pl.pallas_call(kernel, in_specs=[pl.BlockSpec(memory_space=space) for spa...  7.22 us
  transfers between devices with their start and end apart: 22, of which 8 were waited for; matrix products, arithmetic and copies ran while one was open for 3% of the time, Pallas kernels for 1%

profile of v4, /device:TPU:1, one launch (start us, length us, event | category | flops | bytes accessed | tf_op | source)
XLA Modules:
  0.0 167.4 jit_solution(4646322762615199825)
XLA Ops:
  0.6 1.9 %copy.24 = bf16[2048,2,256]{2,0,1:T(8,128)(2,1)S(1)} copy(bf16[2048,2,256]{2,1,0:T(2,128)(2,1)} %param.3) | data formatting | bytes 4194304 | tf_op args[0]
  3.4 9.5 %collective-permute-start.7 = (bf16[8,128,256]{2,1,0:T(8,128)(2,1)}, bf16[8,128,256]{2,1,0:T(8,128)(2,1)}, u32[]{:S(2)}, u32[]{:S(2)}) collective-permute-start(bf16[8,128,256]{2,1,0:T(8,128)(2,1)} %slice_bitcast_fusion), channel_id=1, source_target_pairs={{8,0},{9,1},{10,2},{11,3},{12,4},{13,5},{14,6},{15,7}} | collective-permute-start | bytes 1572872 | tf_op jit(solution)/shard_map/ppermute | solution.py:123
  13.1 8.4 %all_to_all.35 = bf16[4,128,256]{2,1,0:T(8,128)(2,1)S(1)} all-to-all(bf16[4,128,256]{2,1,0:T(8,128)(2,1)S(1)} %pad_maximum_fusion), channel_id=1, replica_groups=mesh['x'=4,'z'=8,'core'=2,'blk'=8] {'x'}, dimensions={0} | all-to-all | bytes 524288 | tf_op jit(solution)/shard_map/all_to_all | solution.py:16
  22.8 4.0 %all-to-all-start.1 = ((bf16[8,8,256]{2,1,0:T(8,128)(2,1)}), bf16[8,8,256]{2,1,0:T(8,128)(2,1)}, u32[]{:S(2)}, u32[]{:S(2)}) async-start(bf16[8,8,256]{2,1,0:T(8,128)(2,1)} %slice_bitcast_fusion.4), calls=%async_computation.1 | async-start | bytes 65536 | tf_op jit(solution)/shard_map/all_to_all | solution.py:16
  33.7 2.6 %all_gather.19 = bf16[2,64,256]{2,1,0:T(8,128)(2,1)S(1)} all-gather(bf16[1,64,256]{2,1,0:T(8,128)(2,1)} %bitcast.5), channel_id=1, replica_groups=mesh['x'=4,'z'=8,'core'=2,'blk'=8] {'core'}, dimensions={0}, use_global_device_ids=true | all-gather | bytes 98304 | tf_op jit(solution)/shard_map/all_gather | solution.py:119
  38.5 2.1 %collective-permute-done.refs_1_ = bf16[4,2,32,256]{3,2,1,0:T(8,128)(2,1)} collective-permute-done((bf16[4,2,32,256]{3,2,1,0:T(8,128)(2,1)S(1)}, bf16[4,2,32,256]{3,2,1,0:T(8,128)(2,1)}, u32[]{:S(2)}, u32[]{:S(2)}) %collective-permute-start) | collective-permute-done | bytes 131104 | tf_op jit(solution)/shard_map/ppermute | solution.py:150
  43.2 2.2 %collective-permute-start.8 = (bf16[8,128,256]{2,1,0:T(8,128)(2,1)}, bf16[8,128,256]{2,1,0:T(8,128)(2,1)S(1)}, u32[]{:S(2)}, u32[]{:S(2)}) collective-permute-start(bf16[8,128,256]{2,1,0:T(8,128)(2,1)} %fusion.6.own), channel_id=1, source_target_pairs={{0,128},{1,129},{2,130},{3,131},{4,132},{5,133},{6,134},{7,135},{8... | collective-permute-start | bytes 1572872 | tf_op jit(solution)/shard_map/ppermute | solution.py:126
  45.5 2.1 %collective-permute-start.9 = (bf16[8,128,256]{2,1,0:T(8,128)(2,1)}, bf16[8,128,256]{2,1,0:T(8,128)(2,1)}, u32[]{:S(2)}, u32[]{:S(2)}) collective-permute-start(bf16[8,128,256]{2,1,0:T(8,128)(2,1)} %fusion.6.own), channel_id=1, source_target_pairs={{0,256},{1,257},{2,258},{3,259},{4,260},{5,261},{6,262},{7,263},{8... | collective-permute-start | bytes 1572872 | tf_op jit(solution)/shard_map/ppermute | solution.py:126
  49.1 3.6 %collective-permute-start.10 = (bf16[8,128,256]{2,1,0:T(8,128)(2,1)}, bf16[8,128,256]{2,1,0:T(8,128)(2,1)}, u32[]{:S(2)}, u32[]{:S(2)}) collective-permute-start(bf16[8,128,256]{2,1,0:T(8,128)(2,1)} %fusion.6.own), channel_id=1, source_target_pairs={{0,384},{1,385},{2,386},{3,387},{4,388},{5,389},{6,390},{7,391},{8... | collective-permute-start | bytes 1572872 | tf_op jit(solution)/shard_map/ppermute | solution.py:126
  53.3 1.8 %collective-permute-done.6.refs_7_ = bf16[4,2,32,256]{3,2,1,0:T(8,128)(2,1)S(1)} collective-permute-done((bf16[4,2,32,256]{3,2,1,0:T(8,128)(2,1)S(1)}, bf16[4,2,32,256]{3,2,1,0:T(8,128)(2,1)S(1)}, u32[]{:S(2)}, u32[]{:S(2)}) %collective-permute-start.6) | collective-permute-done | bytes 131104 | tf_op jit(solution)/shard_map/ppermute | solution.py:150
  55.8 2.2 %shard_map.50 = bf16[8,64,128]{2,1,0:T(8,128)(2,1)} custom-call(bf16[64,256]{1,0:T(8,128)(2,1)} %get-tuple-element.10.pivot, bf16[4,2,32,256]{3,2,1,0:T(8,128)(2,1)} %bitcast.73, bf16[4,2,32,256]{3,2,1,0:T(8,128)(2,1)} %collective-permute-done.refs_1_, bf16[4,2,32,256]{3,2,1,0:T(8,128)(2,1)} %collective-permute-done.1.refs_2_, ...), custom_call_target="tpu_custom_call" | custom-call | tf_op jit(solution)/shard_map/pallas_call | solution.py:87
  58.0 4.9 %all-to-all-start.2 = ((bf16[8,64,128]{2,1,0:T(8,128)(2,1)}), bf16[8,64,128]{2,1,0:T(8,128)(2,1)S(1)}, u32[]{:S(2)}, u32[]{:S(2)}) async-start(bf16[8,64,128]{2,1,0:T(8,128)(2,1)} %shard_map.50), calls=%async_computation.2 | async-start | bytes 262144 | tf_op jit(solution)/shard_map/all_to_all | solution.py:16
  63.7 7.0 %all-to-all-done.2 = bf16[8,64,128]{2,1,0:T(8,128)(2,1)S(1)} async-done(((bf16[8,64,128]{2,1,0:T(8,128)(2,1)}), bf16[8,64,128]{2,1,0:T(8,128)(2,1)S(1)}, u32[]{:S(2)}, u32[]{:S(2)}) %all-to-all-start.2) | async-done | bytes 131104 | tf_op jit(solution)/shard_map/all_to_all | solution.py:16
  70.7 3.9 %all-gather = bf16[128,128]{1,0:T(8,128)(2,1)} all-gather(bf16[64,128]{1,0:T(8,128)(2,1)S(1)} %reduce_sum.42), channel_id=2, replica_groups=mesh['x'=4,'z'=8,'core'=2,'blk'=8] {'core'}, dimensions={0}, use_global_device_ids=true | all-gather | bytes 49152 | tf_op jit(solution)/shard_map/all_gather | solution.py:154
  75.4 2.7 %shard_map.51 = bf16[8,64,128]{2,1,0:T(8,128)(2,1)} custom-call(s32[1]{0:T(128)} %bitcast.11.owner, bf16[2,64,128]{2,1,0:T(8,128)(2,1)} %bitcast.87, bf16[2,256,128]{2,1,0:T(8,128)(2,1)} %fusion.10.order, bf16[8,128,256]{2,1,0:T(8,128)(2,1)} %fusion.6.own, bf16[8,128,256]{2,1,0:T(8,128)(2,1)} %copy-done.7, ...), custom_call_target="tpu_custom_call" | custom-call | tf_op jit(solution)/shard_map/pallas_call | solution.py:87
  78.1 11.7 %all_to_all.36 = bf16[8,64,128]{2,1,0:T(8,128)(2,1)S(1)} all-to-all(bf16[8,64,128]{2,1,0:T(8,128)(2,1)} %shard_map.51), channel_id=1, replica_groups=mesh['x'=4,'z'=8,'core'=2,'blk'=8] {'blk'}, dimensions={0} | all-to-all | bytes 262144 | tf_op jit(solution)/shard_map/all_to_all | solution.py:16
  89.8 3.2 %all-gather.1 = f32[128,128]{1,0:T(8,128)} all-gather(f32[64,128]{1,0:T(8,128)S(1)} %convert_reduce_fusion.1), channel_id=3, replica_groups=mesh['x'=4,'z'=8,'core'=2,'blk'=8] {'core'}, dimensions={0}, use_global_device_ids=true | all-gather | bytes 98304 | tf_op jit(solution)/shard_map/all_gather | solution.py:157
  93.1 2.3 %shard_map.52 = bf16[8,64,128]{2,1,0:T(8,128)(2,1)} custom-call(bf16[64,256]{1,0:T(8,128)(2,1)} %get-tuple-element.11.pivot, f32[2,64,128]{2,1,0:T(8,128)} %bitcast.80, bf16[4,2,32,256]{3,2,1,0:T(8,128)(2,1)} %bitcast.74, bf16[4,2,32,256]{3,2,1,0:T(8,128)(2,1)} %collective-permute-done.refs_1_, bf16[4,2,32,256]{3,2,1,0:T(8,128)(2,1)} %collective-permute-done.1.refs_2_, ...), custom_call_target="tpu_custom_call" | custom-call | tf_op jit(solution)/shard_map/pallas_call | solution.py:87
  95.3 3.4 %all-to-all-start.4 = ((bf16[8,64,128]{2,1,0:T(8,128)(2,1)}), bf16[8,64,128]{2,1,0:T(8,128)(2,1)S(1)}, u32[]{:S(2)}, u32[]{:S(2)}) async-start(bf16[8,64,128]{2,1,0:T(8,128)(2,1)} %shard_map.52), calls=%async_computation.4 | async-start | bytes 262144 | tf_op jit(solution)/shard_map/all_to_all | solution.py:16
  98.8 8.2 %all-to-all-done.4 = bf16[8,64,128]{2,1,0:T(8,128)(2,1)S(1)} async-done(((bf16[8,64,128]{2,1,0:T(8,128)(2,1)}), bf16[8,64,128]{2,1,0:T(8,128)(2,1)S(1)}, u32[]{:S(2)}, u32[]{:S(2)}) %all-to-all-start.4) | async-done | bytes 131104 | tf_op jit(solution)/shard_map/all_to_all | solution.py:16
  118.6 3.3 %all-to-all-start.5 = ((bf16[4,2,64,128]{3,2,1,0:T(8,128)(2,1)}), bf16[4,2,64,128]{3,2,1,0:T(8,128)(2,1)S(1)}, u32[]{:S(2)}, u32[]{:S(2)}) async-start(bf16[4,2,64,128]{3,2,1,0:T(8,128)(2,1)} %broadcast_in_dim.29), calls=%async_computation.5 | async-start | bytes 262144 | tf_op jit(solution)/shard_map/all_to_all | solution.py:16
  123.1 3.6 %all-to-all-done.5 = bf16[4,2,64,128]{3,2,1,0:T(8,128)(2,1)S(1)} async-done(((bf16[4,2,64,128]{3,2,1,0:T(8,128)(2,1)}), bf16[4,2,64,128]{3,2,1,0:T(8,128)(2,1)S(1)}, u32[]{:S(2)}, u32[]{:S(2)}) %all-to-all-start.5) | async-done | bytes 131104 | tf_op jit(solution)/shard_map/all_to_all | solution.py:16
  126.7 5.2 %all-gather.2 = bf16[8,2,64,128]{3,2,1,0:T(8,128)(2,1)S(1)} all-gather(bf16[4,2,64,128]{3,2,1,0:T(8,128)(2,1)S(1)} %all-to-all-done.5), channel_id=4, replica_groups=mesh['x'=4,'z'=8,'core'=2,'blk'=8] {'core'}, dimensions={0}, use_global_device_ids=true | all-gather | bytes 393216 | tf_op jit(solution)/shard_map/all_gather | solution.py:140
  133.4 32.4 %all_to_all.37 = bf16[8,544,128]{2,1,0:T(8,128)(2,1)S(1)} all-to-all(bf16[8,544,128]{2,1,0:T(8,128)(2,1)S(1)} %bitcast.77), channel_id=1, replica_groups=mesh['x'=4,'z'=8,'core'=2,'blk'=8] {'blk'}, dimensions={0} | all-to-all | bytes 2228224 | tf_op jit(solution)/shard_map/all_to_all | solution.py:16
  (84 shorter events, 33.9 us)
Async XLA Ops:
  2.5 10.5 %copy-start.9 = (f32[2,32,256]{2,1,0:T(8,128)S(1)}, f32[2,32,256]{2,1,0:T(8,128)}, u32[]{:S(2)}) copy-start(f32[2,32,256]{2,1,0:T(8,128)} %param.5) | copy-start | bytes 196612
  3.4 32.9 %collective-permute-start.7 = (bf16[8,128,256]{2,1,0:T(8,128)(2,1)}, bf16[8,128,256]{2,1,0:T(8,128)(2,1)}, u32[]{:S(2)}, u32[]{:S(2)}) collective-permute-start(bf16[8,128,256]{2,1,0:T(8,128)(2,1)} %slice_bitcast_fusion), channel_id=1, source_target_pairs={{8,0},{9,1},{10,2},{11,3},{12,4},{13,5},{14,6},{15,7}} | collective-permute-start | bytes 1572872 | tf_op jit(solution)/shard_map/ppermute | solution.py:123
  22.8 11.0 %all-to-all-start.1 = ((bf16[8,8,256]{2,1,0:T(8,128)(2,1)}), bf16[8,8,256]{2,1,0:T(8,128)(2,1)}, u32[]{:S(2)}, u32[]{:S(2)}) async-start(bf16[8,8,256]{2,1,0:T(8,128)(2,1)} %slice_bitcast_fusion.4), calls=%async_computation.1 | async-start | bytes 65536 | tf_op jit(solution)/shard_map/all_to_all | solution.py:16
  27.7 27.4 %copy-start = (bf16[4,64,256]{2,1,0:T(8,128)(2,1)}, bf16[4,64,256]{2,1,0:T(8,128)(2,1)S(1)}, u32[]{:S(2)}) copy-start(bf16[4,64,256]{2,1,0:T(8,128)(2,1)S(1)} %slice.56) | copy-start | bytes 393220
  27.7 12.9 %collective-permute-start = (bf16[4,2,32,256]{3,2,1,0:T(8,128)(2,1)S(1)}, bf16[4,2,32,256]{3,2,1,0:T(8,128)(2,1)}, u32[]{:S(2)}, u32[]{:S(2)}) collective-permute-start(bf16[4,2,32,256]{3,2,1,0:T(8,128)(2,1)S(1)} %bitcast.66), channel_id=1, source_target_pairs={{16,0},{17,1},{18,2},{19,3},{20,4},{21,5},{22,6},{23,7},{24,8},{25... | collective-permute-start | bytes 393224 | tf_op jit(solution)/shard_map/ppermute | solution.py:150
  29.0 12.9 %collective-permute-start.1 = (bf16[4,2,32,256]{3,2,1,0:T(8,128)(2,1)S(1)}, bf16[4,2,32,256]{3,2,1,0:T(8,128)(2,1)}, u32[]{:S(2)}, u32[]{:S(2)}) collective-permute-start(bf16[4,2,32,256]{3,2,1,0:T(8,128)(2,1)S(1)} %bitcast.67), channel_id=1, source_target_pairs={{32,0},{33,1},{34,2},{35,3},{36,4},{37,5},{38,6},{39,7},{40,8},{41... | collective-permute-start | bytes 393224 | tf_op jit(solution)/shard_map/ppermute | solution.py:150
  30.3 12.9 %collective-permute-start.2 = (bf16[4,2,32,256]{3,2,1,0:T(8,128)(2,1)S(1)}, bf16[4,2,32,256]{3,2,1,0:T(8,128)(2,1)}, u32[]{:S(2)}, u32[]{:S(2)}) collective-permute-start(bf16[4,2,32,256]{3,2,1,0:T(8,128)(2,1)S(1)} %bitcast.68), channel_id=1, source_target_pairs={{48,0},{49,1},{50,2},{51,3},{52,4},{53,5},{54,6},{55,7},{56,8},{57... | collective-permute-start | bytes 393224 | tf_op jit(solution)/shard_map/ppermute | solution.py:150
  31.6 13.9 %collective-permute-start.3 = (bf16[4,2,32,256]{3,2,1,0:T(8,128)(2,1)S(1)}, bf16[4,2,32,256]{3,2,1,0:T(8,128)(2,1)}, u32[]{:S(2)}, u32[]{:S(2)}) collective-permute-start(bf16[4,2,32,256]{3,2,1,0:T(8,128)(2,1)S(1)} %bitcast.69), channel_id=1, source_target_pairs={{64,0},{65,1},{66,2},{67,3},{68,4},{69,5},{70,6},{71,7},{72,8},{73... | collective-permute-start | bytes 393224 | tf_op jit(solution)/shard_map/ppermute | solution.py:150
  36.4 12.7 %collective-permute-start.4 = (bf16[4,2,32,256]{3,2,1,0:T(8,128)(2,1)S(1)}, bf16[4,2,32,256]{3,2,1,0:T(8,128)(2,1)S(1)}, u32[]{:S(2)}, u32[]{:S(2)}) collective-permute-start(bf16[4,2,32,256]{3,2,1,0:T(8,128)(2,1)S(1)} %bitcast.70), channel_id=1, source_target_pairs={{80,0},{81,1},{82,2},{83,3},{84,4},{85,5},{86,6},{87,7},{88,8},{89... | collective-permute-start | bytes 393224 | tf_op jit(solution)/shard_map/ppermute | solution.py:150
  40.6 12.7 %collective-permute-start.5 = (bf16[4,2,32,256]{3,2,1,0:T(8,128)(2,1)S(1)}, bf16[4,2,32,256]{3,2,1,0:T(8,128)(2,1)S(1)}, u32[]{:S(2)}, u32[]{:S(2)}) collective-permute-start(bf16[4,2,32,256]{3,2,1,0:T(8,128)(2,1)S(1)} %bitcast.71), channel_id=1, source_target_pairs={{96,0},{97,1},{98,2},{99,3},{100,4},{101,5},{102,6},{103,7},{104,8... | collective-permute-start | bytes 393224 | tf_op jit(solution)/shard_map/ppermute | solution.py:150
  41.9 13.2 %collective-permute-start.6 = (bf16[4,2,32,256]{3,2,1,0:T(8,128)(2,1)S(1)}, bf16[4,2,32,256]{3,2,1,0:T(8,128)(2,1)S(1)}, u32[]{:S(2)}, u32[]{:S(2)}) collective-permute-start(bf16[4,2,32,256]{3,2,1,0:T(8,128)(2,1)S(1)} %bitcast.72), channel_id=1, source_target_pairs={{112,0},{113,1},{114,2},{115,3},{116,4},{117,5},{118,6},{119,7},{1... | collective-permute-start | bytes 393224 | tf_op jit(solution)/shard_map/ppermute | solution.py:150
  43.2 31.4 %collective-permute-start.8 = (bf16[8,128,256]{2,1,0:T(8,128)(2,1)}, bf16[8,128,256]{2,1,0:T(8,128)(2,1)S(1)}, u32[]{:S(2)}, u32[]{:S(2)}) collective-permute-start(bf16[8,128,256]{2,1,0:T(8,128)(2,1)} %fusion.6.own), channel_id=1, source_target_pairs={{0,128},{1,129},{2,130},{3,131},{4,132},{5,133},{6,134},{7,135},{8... | collective-permute-start | bytes 1572872 | tf_op jit(solution)/shard_map/ppermute | solution.py:126
  45.5 29.1 %collective-permute-start.9 = (bf16[8,128,256]{2,1,0:T(8,128)(2,1)}, bf16[8,128,256]{2,1,0:T(8,128)(2,1)}, u32[]{:S(2)}, u32[]{:S(2)}) collective-permute-start(bf16[8,128,256]{2,1,0:T(8,128)(2,1)} %fusion.6.own), channel_id=1, source_target_pairs={{0,256},{1,257},{2,258},{3,259},{4,260},{5,261},{6,262},{7,263},{8... | collective-permute-start | bytes 1572872 | tf_op jit(solution)/shard_map/ppermute | solution.py:126
  49.1 25.6 %collective-permute-start.10 = (bf16[8,128,256]{2,1,0:T(8,128)(2,1)}, bf16[8,128,256]{2,1,0:T(8,128)(2,1)}, u32[]{:S(2)}, u32[]{:S(2)}) collective-permute-start(bf16[8,128,256]{2,1,0:T(8,128)(2,1)} %fusion.6.own), channel_id=1, source_target_pairs={{0,384},{1,385},{2,386},{3,387},{4,388},{5,389},{6,390},{7,391},{8... | collective-permute-start | bytes 1572872 | tf_op jit(solution)/shard_map/ppermute | solution.py:126
  58.0 12.7 %all-to-all-start.2 = ((bf16[8,64,128]{2,1,0:T(8,128)(2,1)}), bf16[8,64,128]{2,1,0:T(8,128)(2,1)S(1)}, u32[]{:S(2)}, u32[]{:S(2)}) async-start(bf16[8,64,128]{2,1,0:T(8,128)(2,1)} %shard_map.50), calls=%async_computation.2 | async-start | bytes 262144 | tf_op jit(solution)/shard_map/all_to_all | solution.py:16
  95.3 11.7 %all-to-all-start.4 = ((bf16[8,64,128]{2,1,0:T(8,128)(2,1)}), bf16[8,64,128]{2,1,0:T(8,128)(2,1)S(1)}, u32[]{:S(2)}, u32[]{:S(2)}) async-start(bf16[8,64,128]{2,1,0:T(8,128)(2,1)} %shard_map.52), calls=%async_computation.4 | async-start | bytes 262144 | tf_op jit(solution)/shard_map/all_to_all | solution.py:16
  107.0 7.2 %collective-permute-start.17 = (bf16[2,64,128]{2,1,0:T(8,128)(2,1)S(1)}, bf16[2,64,128]{2,1,0:T(8,128)(2,1)S(1)}, u32[]{:S(2)}, u32[]{:S(2)}) collective-permute-start(bf16[2,64,128]{2,1,0:T(8,128)(2,1)S(1)} %pad_maximum_fusion.1), channel_id=1, source_target_pairs={{0,112},{1,113},{2,114},{3,115},{4,116},{5,117},{6,118},{7,119},{8... | collective-permute-start | bytes 98312 | tf_op jit(solution)/shard_map/ppermute | solution.py:165
  108.3 7.3 %collective-permute-start.16 = (bf16[2,64,128]{2,1,0:T(8,128)(2,1)S(1)}, bf16[2,64,128]{2,1,0:T(8,128)(2,1)S(1)}, u32[]{:S(2)}, u32[]{:S(2)}) collective-permute-start(bf16[2,64,128]{2,1,0:T(8,128)(2,1)S(1)} %pad_maximum_fusion.1), channel_id=1, source_target_pairs={{0,96},{1,97},{2,98},{3,99},{4,100},{5,101},{6,102},{7,103},{8,104... | collective-permute-start | bytes 98312 | tf_op jit(solution)/shard_map/ppermute | solution.py:165
  110.4 6.5 %collective-permute-start.15 = (bf16[2,64,128]{2,1,0:T(8,128)(2,1)S(1)}, bf16[2,64,128]{2,1,0:T(8,128)(2,1)S(1)}, u32[]{:S(2)}, u32[]{:S(2)}) collective-permute-start(bf16[2,64,128]{2,1,0:T(8,128)(2,1)S(1)} %pad_maximum_fusion.1), channel_id=1, source_target_pairs={{0,80},{1,81},{2,82},{3,83},{4,84},{5,85},{6,86},{7,87},{8,88},{9,... | collective-permute-start | bytes 98312 | tf_op jit(solution)/shard_map/ppermute | solution.py:165
  111.7 5.3 %collective-permute-start.14 = (bf16[2,64,128]{2,1,0:T(8,128)(2,1)S(1)}, bf16[2,64,128]{2,1,0:T(8,128)(2,1)S(1)}, u32[]{:S(2)}, u32[]{:S(2)}) collective-permute-start(bf16[2,64,128]{2,1,0:T(8,128)(2,1)S(1)} %pad_maximum_fusion.1), channel_id=1, source_target_pairs={{0,64},{1,65},{2,66},{3,67},{4,68},{5,69},{6,70},{7,71},{8,72},{9,... | collective-permute-start | bytes 98312 | tf_op jit(solution)/shard_map/ppermute | solution.py:165
  113.0 4.0 %collective-permute-start.13 = (bf16[2,64,128]{2,1,0:T(8,128)(2,1)S(1)}, bf16[2,64,128]{2,1,0:T(8,128)(2,1)S(1)}, u32[]{:S(2)}, u32[]{:S(2)}) collective-permute-start(bf16[2,64,128]{2,1,0:T(8,128)(2,1)S(1)} %pad_maximum_fusion.1), channel_id=1, source_target_pairs={{0,48},{1,49},{2,50},{3,51},{4,52},{5,53},{6,54},{7,55},{8,56},{9,... | collective-permute-start | bytes 98312 | tf_op jit(solution)/shard_map/ppermute | solution.py:165
  114.3 2.7 %collective-permute-start.12 = (bf16[2,64,128]{2,1,0:T(8,128)(2,1)S(1)}, bf16[2,64,128]{2,1,0:T(8,128)(2,1)S(1)}, u32[]{:S(2)}, u32[]{:S(2)}) collective-permute-start(bf16[2,64,128]{2,1,0:T(8,128)(2,1)S(1)} %pad_maximum_fusion.1), channel_id=1, source_target_pairs={{0,32},{1,33},{2,34},{3,35},{4,36},{5,37},{6,38},{7,39},{8,40},{9,... | collective-permute-start | bytes 98312 | tf_op jit(solution)/shard_map/ppermute | solution.py:165
  115.6 2.3 %collective-permute-start.11 = (bf16[2,64,128]{2,1,0:T(8,128)(2,1)S(1)}, bf16[2,64,128]{2,1,0:T(8,128)(2,1)S(1)}, u32[]{:S(2)}, u32[]{:S(2)}) collective-permute-start(bf16[2,64,128]{2,1,0:T(8,128)(2,1)S(1)} %pad_maximum_fusion.1), channel_id=1, source_target_pairs={{0,16},{1,17},{2,18},{3,19},{4,20},{5,21},{6,22},{7,23},{8,24},{9,... | collective-permute-start | bytes 98312 | tf_op jit(solution)/shard_map/ppermute | solution.py:165
  118.6 8.1 %all-to-all-start.5 = ((bf16[4,2,64,128]{3,2,1,0:T(8,128)(2,1)}), bf16[4,2,64,128]{3,2,1,0:T(8,128)(2,1)S(1)}, u32[]{:S(2)}, u32[]{:S(2)}) async-start(bf16[4,2,64,128]{3,2,1,0:T(8,128)(2,1)} %broadcast_in_dim.29), calls=%async_computation.5 | async-start | bytes 262144 | tf_op jit(solution)/shard_map/all_to_all | solution.py:16
  (8 other events, 39.5 us)

commit v5 on v4

--- a/solution.py
+++ b/solution.py
@@ -28,12 +28,17 @@
     return jnp.sum(swap_blocks(split, "blk").astype(WIDE), axis=0)
 
 
-def assemble(planes, step, whole):
+def assemble(planes, step, whole, done):
+    copies = []
     for z, plane in enumerate(planes):
         count, _, size, _ = plane.shape
         for x in range(count):
             at = (x * len(planes) + z) * size
-            whole[at : at + size, :] = plane[x, step]
+            target = whole.at[at : at + size, :]
+            copies.append(pltpu.make_async_copy(plane.at[x, step], target, done.at[len(copies)]))
+    for copy in copies:
+        copy.start()
+    return copies
 
 
 def write_blocks(value, whole, out):
@@ -44,52 +49,51 @@
 
 
 def first_kernel(pivot, *refs):
-    planes, (out, whole) = refs[:NZ], refs[NZ:]
-    assemble(planes, 0, whole)
+    planes, (out, whole, done) = refs[:NZ], refs[NZ:]
+    for copy in assemble(planes, 0, whole, done):
+        copy.wait()
     write_blocks(pivot[...], whole, out)
 
 
-def cross_kernel(owner, pair, order, own, *refs):
-    others, (out, whole) = refs[: NX - 1], refs[NX - 1 :]
+def cross_kernel(which, pair, order, *refs):
+    panels, (out, whole, done) = refs[:NX], refs[NX:]
+    for k in range(NX):
+
+        @pl.when(which[0] == k)
+        def _():
+            copy = pltpu.make_async_copy(panels[k], whole, done.at[0])
+            copy.start()
+            copy.wait()
+
     value = product(pair[0], order[0])
     for c in range(1, NC):
         value = value + product(pair[c], order[c])
-    blocks, size, _ = own.shape
-
-    @pl.when(owner[0] == 1)
-    def _():
-        for g in range(blocks):
-            whole[g * size : (g + 1) * size, :] = own[g]
-
-    @pl.when(owner[0] == 0)
-    def _():
-        for g in range(blocks):
-            part = others[0][g]
-            for other in others[1:]:
-                part = part + other[g]
-            whole[g * size : (g + 1) * size, :] = part
-
     write_blocks(value.astype(HALF), whole, out)
 
 
 def second_kernel(pivot, update, *refs):
-    planes, (out, whole, value) = refs[:NZ], refs[NZ:]
-    assemble(planes, 1, whole)
+    planes, (out, whole, done, value) = refs[:NZ], refs[NZ:]
+    copies = assemble(planes, 1, whole, done)
     half = update.shape[2]
     for c in range(NC):
         part = pivot[:, c * half : (c + 1) * half].astype(WIDE) - update[c]
         value[:, c * half : (c + 1) * half] = part.astype(HALF)
+    for copy in copies:
+        copy.wait()
     write_blocks(value[...], whole, out)
 
 
-def run_kernel(kernel, blocks, t, size, width, scratch, *operands):
-    spaces = [pltpu.SMEM if item.dtype == jnp.int32 else pltpu.VMEM for item in operands]
+def run_kernel(kernel, blocks, t, size, width, scratch, near, far):
+    spaces = [pltpu.SMEM if item.dtype == jnp.int32 else pltpu.VMEM for item in near]
+    spaces += [pl.ANY] * len(far)
+    whole = pltpu.VMEM((blocks * size, width), HALF)
+    done = pltpu.SemaphoreType.DMA((NX * NZ,))
     return pl.pallas_call(
         kernel,
         in_specs=[pl.BlockSpec(memory_space=space) for space in spaces],
         out_shape=jax.ShapeDtypeStruct((blocks, t, size), HALF),
-        scratch_shapes=[pltpu.VMEM((blocks * size, width), HALF), *scratch],
-    )(*operands)
+        scratch_shapes=[whole, done, *scratch],
+    )(*near, *far)
 
 
 def local(factor_panel, right_side, block_inverse):
@@ -122,8 +126,9 @@
     halves = panels[0].reshape(n_blk, NC, half, width)
     sent = lax.ppermute(halves[:, 0], ("x", "z", "core"), [(1, 0)])
     lower = jnp.where(core == 1, halves[:, 1], sent)
-    owner = ((x == 0) & (z == 0)).astype(jnp.int32).reshape(1)
-    cross = [lower] + [lax.ppermute(lower, ("x", "z"), [(0, k * NZ)]) for k in range(1, NX)]
+    which = x.astype(jnp.int32).reshape(1)
+    flat = lower.reshape(n_blk * half, width)
+    cross = [flat] + [lax.ppermute(flat, ("x", "z"), [(0, k * NZ)]) for k in range(1, NX)]
 
     place = jnp.arange(width)
     c_of, q_of, i_of = place // half, place % half // rows_local, place % rows_local
@@ -148,21 +153,22 @@
     select = select.astype(HALF)
 
     planes = [inverse] + [lax.ppermute(inverse, "z", [(k, 0)]) for k in range(1, NZ)]
-    partial = run_kernel(first_kernel, *sizes, (), pivot[0], *planes)
+    partial = run_kernel(first_kernel, *sizes, (), (pivot[0],), planes)
     first = scatter_sum(partial).astype(HALF)
     first, panels = lax.optimization_barrier((first, panels))
     pair = lax.all_gather(first, "core", axis=0, tiled=False)
-    partial = run_kernel(cross_kernel, *sizes, (), owner, pair, pair_order, *cross)
+    partial = run_kernel(cross_kernel, *sizes, (), (which, pair, pair_order), cross)
     update = scatter_sum(partial)
     pair = lax.all_gather(update, "core", axis=0, tiled=False)
     scratch = (pltpu.VMEM((t, width), HALF),)
-    partial = run_kernel(second_kernel, *sizes, scratch, pivot[1], pair, *planes)
+    partial = run_kernel(second_kernel, *sizes, scratch, (pivot[1], pair), planes)
     second = scatter_sum(partial).astype(HALF)
 
     solved = jnp.stack([first, second])
     spread = jnp.where(z == 0, solved, jnp.zeros_like(solved))
     for k in range(1, NZ):
-        spread = spread + lax.ppermute(solved, "z", [(0, k)])
+        received = lax.ppermute(solved, "z", [(0, k)])
+        spread = spread + received
     spread = ordered(both_cores(gather_by_swap(spread, "x", NX)))
     spread = spread.reshape(NX, STEPS, n_blk, dates_x, width).transpose(2, 0, 3, 1, 4)
     spread = spread.reshape(dates_local * n_blk, STEPS * width)

time: 169 us -> 171 us (1.012)
  Pallas kernels: 7.22 us -> 9.29 us
    pallas_call x3, Pallas kernels: 7.22 us -> 9.29 us  [run_kernel(): pl.pallas_call(kernel, in_specs=[pl.BlockSpec(memory_space=space) for spa...]
  transfers between devices with their start and end apart: 22 -> 22, of which waited for: 8 -> 8; matrix products, arithmetic and copies ran while one was open for 3% -> 3% of each run, Pallas kernels for 1% -> 2%
where the time goes in v5:
time: 171 us; the launch traced here: 169 us
  blocking collectives  67.4 us (39%)
  starting transfers between devices  51.2 us (30%)
  waiting for transfers between devices  26.1 us (15%)
  Pallas kernels  9.29 us (5%)
  local copies, waits for them, and re-layouts  8.79 us (5%)
  other arithmetic  4.55 us (3%)
    all_to_all x3, blocking collectives, swap_blocks(): return lax.all_to_all(array, axis, split_axis=0, concat_axis=0, tiled=True)  52.5 us
    all_to_all x4, waiting for transfers between devices, swap_blocks(): return lax.all_to_all(array, axis, split_axis=0, concat_axis=0, tiled=True)  19.7 us
    all_to_all x4, starting transfers between devices, swap_blocks(): return lax.all_to_all(array, axis, split_axis=0, concat_axis=0, tiled=True)  15.6 us
    ppermute x1, starting transfers between devices, local(): sent = lax.ppermute(halves[:, 0], ('x', 'z', 'core'), [(1, 0)])  9.55 us
    pallas_call x3, Pallas kernels, run_kernel(): pl.pallas_call(kernel, in_specs=[pl.BlockSpec(memory_space=space) for spa...  9.29 us
    ppermute x7, starting transfers between devices, local(): received = lax.ppermute(solved, 'z', [(0, k)])  9.03 us
    ppermute x7, starting transfers between devices, local(): lax.ppermute(inverse, 'z', [(k, 0)])  9.02 us
    ppermute x3, starting transfers between devices, local(): lax.ppermute(flat, ('x', 'z'), [(0, k * NZ)])  7.93 us
  transfers between devices with their start and end apart: 22, of which 8 were waited for; matrix products, arithmetic and copies ran while one was open for 3% of the time, Pallas kernels for 2%

profile of v5, /device:TPU:1, one launch (start us, length us, event | category | flops | bytes accessed | tf_op | source)
XLA Modules:
  0.0 169.5 jit_solution(5625868106544427872)
XLA Ops:
  0.6 1.9 %copy.23 = bf16[2048,2,256]{2,0,1:T(8,128)(2,1)S(1)} copy(bf16[2048,2,256]{2,1,0:T(2,128)(2,1)} %param.3) | data formatting | bytes 4194304 | tf_op args[0]
  3.4 9.5 %collective-permute-start.7 = (bf16[8,128,256]{2,1,0:T(8,128)(2,1)}, bf16[8,128,256]{2,1,0:T(8,128)(2,1)}, u32[]{:S(2)}, u32[]{:S(2)}) collective-permute-start(bf16[8,128,256]{2,1,0:T(8,128)(2,1)} %slice_bitcast_fusion), channel_id=1, source_target_pairs={{8,0},{9,1},{10,2},{11,3},{12,4},{13,5},{14,6},{15,7}} | collective-permute-start | bytes 1572872 | tf_op jit(solution)/shard_map/ppermute | solution.py:127
  13.1 8.4 %all_to_all.35 = bf16[4,128,256]{2,1,0:T(8,128)(2,1)S(1)} all-to-all(bf16[4,128,256]{2,1,0:T(8,128)(2,1)S(1)} %pad_maximum_fusion), channel_id=1, replica_groups=mesh['x'=4,'z'=8,'core'=2,'blk'=8] {'x'}, dimensions={0} | all-to-all | bytes 524288 | tf_op jit(solution)/shard_map/all_to_all | solution.py:16
  22.8 4.0 %all-to-all-start.1 = ((bf16[8,8,256]{2,1,0:T(8,128)(2,1)}), bf16[8,8,256]{2,1,0:T(8,128)(2,1)}, u32[]{:S(2)}, u32[]{:S(2)}) async-start(bf16[8,8,256]{2,1,0:T(8,128)(2,1)} %slice_bitcast_fusion.4), calls=%async_computation.1 | async-start | bytes 65536 | tf_op jit(solution)/shard_map/all_to_all | solution.py:16
  33.7 2.6 %all_gather.19 = bf16[2,64,256]{2,1,0:T(8,128)(2,1)S(1)} all-gather(bf16[1,64,256]{2,1,0:T(8,128)(2,1)} %bitcast.5), channel_id=1, replica_groups=mesh['x'=4,'z'=8,'core'=2,'blk'=8] {'core'}, dimensions={0}, use_global_device_ids=true | all-gather | bytes 98304 | tf_op jit(solution)/shard_map/all_gather | solution.py:123
  38.5 2.1 %collective-permute-done.refs_1_ = bf16[4,2,32,256]{3,2,1,0:T(8,128)(2,1)} collective-permute-done((bf16[4,2,32,256]{3,2,1,0:T(8,128)(2,1)S(1)}, bf16[4,2,32,256]{3,2,1,0:T(8,128)(2,1)}, u32[]{:S(2)}, u32[]{:S(2)}) %collective-permute-start) | collective-permute-done | bytes 131104 | tf_op jit(solution)/shard_map/ppermute | solution.py:155
  43.2 2.2 %collective-permute-start.8 = (bf16[1024,256]{1,0:T(8,128)(2,1)}, bf16[1024,256]{1,0:T(8,128)(2,1)S(1)}, u32[]{:S(2)}, u32[]{:S(2)}) collective-permute-start(bf16[1024,256]{1,0:T(8,128)(2,1)} %bitcast.16.refs_0_), channel_id=1, source_target_pairs={{0,128},{1,129},{2,130},{3,131},{4,132},{5,133},{6,134},{7,135},{8... | collective-permute-start | bytes 1572872 | tf_op jit(solution)/shard_map/ppermute | solution.py:131
  45.5 2.1 %collective-permute-start.9 = (bf16[1024,256]{1,0:T(8,128)(2,1)}, bf16[1024,256]{1,0:T(8,128)(2,1)}, u32[]{:S(2)}, u32[]{:S(2)}) collective-permute-start(bf16[1024,256]{1,0:T(8,128)(2,1)} %bitcast.16.refs_0_), channel_id=1, source_target_pairs={{0,256},{1,257},{2,258},{3,259},{4,260},{5,261},{6,262},{7,263},{8... | collective-permute-start | bytes 1572872 | tf_op jit(solution)/shard_map/ppermute | solution.py:131
  49.1 3.6 %collective-permute-start.10 = (bf16[1024,256]{1,0:T(8,128)(2,1)}, bf16[1024,256]{1,0:T(8,128)(2,1)}, u32[]{:S(2)}, u32[]{:S(2)}) collective-permute-start(bf16[1024,256]{1,0:T(8,128)(2,1)} %bitcast.16.refs_0_), channel_id=1, source_target_pairs={{0,384},{1,385},{2,386},{3,387},{4,388},{5,389},{6,390},{7,391},{8... | collective-permute-start | bytes 1572872 | tf_op jit(solution)/shard_map/ppermute | solution.py:131
  53.3 1.8 %collective-permute-done.6.refs_7_ = bf16[4,2,32,256]{3,2,1,0:T(8,128)(2,1)S(1)} collective-permute-done((bf16[4,2,32,256]{3,2,1,0:T(8,128)(2,1)S(1)}, bf16[4,2,32,256]{3,2,1,0:T(8,128)(2,1)S(1)}, u32[]{:S(2)}, u32[]{:S(2)}) %collective-permute-start.6) | collective-permute-done | bytes 131104 | tf_op jit(solution)/shard_map/ppermute | solution.py:155
  55.8 3.0 %shard_map.50 = bf16[8,64,128]{2,1,0:T(8,128)(2,1)} custom-call(bf16[64,256]{1,0:T(8,128)(2,1)} %get-tuple-element.10.pivot, bf16[4,2,32,256]{3,2,1,0:T(8,128)(2,1)} %bitcast.72, bf16[4,2,32,256]{3,2,1,0:T(8,128)(2,1)} %collective-permute-done.refs_1_, bf16[4,2,32,256]{3,2,1,0:T(8,128)(2,1)} %collective-permute-done.1.refs_2_, ...), custom_call_target="tpu_custom_call" | custom-call | tf_op jit(solution)/shard_map/pallas_call | solution.py:91
  58.7 5.0 %all-to-all-start.2 = ((bf16[8,64,128]{2,1,0:T(8,128)(2,1)}), bf16[8,64,128]{2,1,0:T(8,128)(2,1)S(1)}, u32[]{:S(2)}, u32[]{:S(2)}) async-start(bf16[8,64,128]{2,1,0:T(8,128)(2,1)} %shard_map.50), calls=%async_computation.2 | async-start | bytes 262144 | tf_op jit(solution)/shard_map/all_to_all | solution.py:16
  64.4 7.0 %all-to-all-done.2 = bf16[8,64,128]{2,1,0:T(8,128)(2,1)S(1)} async-done(((bf16[8,64,128]{2,1,0:T(8,128)(2,1)}), bf16[8,64,128]{2,1,0:T(8,128)(2,1)S(1)}, u32[]{:S(2)}, u32[]{:S(2)}) %all-to-all-start.2) | async-done | bytes 131104 | tf_op jit(solution)/shard_map/all_to_all | solution.py:16
  71.5 3.9 %all-gather = bf16[128,128]{1,0:T(8,128)(2,1)} all-gather(bf16[64,128]{1,0:T(8,128)(2,1)S(1)} %reduce_sum.42), channel_id=2, replica_groups=mesh['x'=4,'z'=8,'core'=2,'blk'=8] {'core'}, dimensions={0}, use_global_device_ids=true | all-gather | bytes 49152 | tf_op jit(solution)/shard_map/all_gather | solution.py:159
  76.1 3.3 %shard_map.51 = bf16[8,64,128]{2,1,0:T(8,128)(2,1)} custom-call(s32[1]{0:T(128)} %bitcast.11.which, bf16[2,64,128]{2,1,0:T(8,128)(2,1)} %bitcast.86, bf16[2,256,128]{2,1,0:T(8,128)(2,1)} %fusion.10.order, bf16[1024,256]{1,0:T(8,128)(2,1)} %bitcast.16.refs_0_, bf16[1024,256]{1,0:T(8,128)(2,1)} %copy-done.7, bf16[1024,256]{1,0:T(8,128)(2,1)} %collective-permute-done.9.refs_2_, ...), custom_call_target="tpu_custom_call" | custom-call | tf_op jit(solution)/shard_map/pallas_call | solution.py:91
  79.4 11.7 %all_to_all.36 = bf16[8,64,128]{2,1,0:T(8,128)(2,1)S(1)} all-to-all(bf16[8,64,128]{2,1,0:T(8,128)(2,1)} %shard_map.51), channel_id=1, replica_groups=mesh['x'=4,'z'=8,'core'=2,'blk'=8] {'blk'}, dimensions={0} | all-to-all | bytes 262144 | tf_op jit(solution)/shard_map/all_to_all | solution.py:16
  91.1 3.2 %all-gather.1 = f32[128,128]{1,0:T(8,128)} all-gather(f32[64,128]{1,0:T(8,128)S(1)} %convert_reduce_fusion.1), channel_id=3, replica_groups=mesh['x'=4,'z'=8,'core'=2,'blk'=8] {'core'}, dimensions={0}, use_global_device_ids=true | all-gather | bytes 98304 | tf_op jit(solution)/shard_map/all_gather | solution.py:162
  94.4 3.1 %shard_map.52 = bf16[8,64,128]{2,1,0:T(8,128)(2,1)} custom-call(bf16[64,256]{1,0:T(8,128)(2,1)} %get-tuple-element.11.pivot, f32[2,64,128]{2,1,0:T(8,128)} %bitcast.79, bf16[4,2,32,256]{3,2,1,0:T(8,128)(2,1)} %bitcast.73, bf16[4,2,32,256]{3,2,1,0:T(8,128)(2,1)} %collective-permute-done.refs_1_, bf16[4,2,32,256]{3,2,1,0:T(8,128)(2,1)} %collective-permute-done.1.refs_2_, ...), custom_call_target="tpu_custom_call" | custom-call | tf_op jit(solution)/shard_map/pallas_call | solution.py:91
  97.5 3.4 %all-to-all-start.4 = ((bf16[8,64,128]{2,1,0:T(8,128)(2,1)}), bf16[8,64,128]{2,1,0:T(8,128)(2,1)S(1)}, u32[]{:S(2)}, u32[]{:S(2)}) async-start(bf16[8,64,128]{2,1,0:T(8,128)(2,1)} %shard_map.52), calls=%async_computation.4 | async-start | bytes 262144 | tf_op jit(solution)/shard_map/all_to_all | solution.py:16
  100.9 8.2 %all-to-all-done.4 = bf16[8,64,128]{2,1,0:T(8,128)(2,1)S(1)} async-done(((bf16[8,64,128]{2,1,0:T(8,128)(2,1)}), bf16[8,64,128]{2,1,0:T(8,128)(2,1)S(1)}, u32[]{:S(2)}, u32[]{:S(2)}) %all-to-all-start.4) | async-done | bytes 131104 | tf_op jit(solution)/shard_map/all_to_all | solution.py:16
  120.7 3.3 %all-to-all-start.5 = ((bf16[4,2,64,128]{3,2,1,0:T(8,128)(2,1)}), bf16[4,2,64,128]{3,2,1,0:T(8,128)(2,1)S(1)}, u32[]{:S(2)}, u32[]{:S(2)}) async-start(bf16[4,2,64,128]{3,2,1,0:T(8,128)(2,1)} %broadcast_in_dim.29), calls=%async_computation.5 | async-start | bytes 262144 | tf_op jit(solution)/shard_map/all_to_all | solution.py:16
  125.2 3.6 %all-to-all-done.5 = bf16[4,2,64,128]{3,2,1,0:T(8,128)(2,1)S(1)} async-done(((bf16[4,2,64,128]{3,2,1,0:T(8,128)(2,1)}), bf16[4,2,64,128]{3,2,1,0:T(8,128)(2,1)S(1)}, u32[]{:S(2)}, u32[]{:S(2)}) %all-to-all-start.5) | async-done | bytes 131104 | tf_op jit(solution)/shard_map/all_to_all | solution.py:16
  128.9 5.1 %all-gather.2 = bf16[8,2,64,128]{3,2,1,0:T(8,128)(2,1)S(1)} all-gather(bf16[4,2,64,128]{3,2,1,0:T(8,128)(2,1)S(1)} %all-to-all-done.5), channel_id=4, replica_groups=mesh['x'=4,'z'=8,'core'=2,'blk'=8] {'core'}, dimensions={0}, use_global_device_ids=true | all-gather | bytes 393216 | tf_op jit(solution)/shard_map/all_gather | solution.py:145
  135.5 32.4 %all_to_all.37 = bf16[8,544,128]{2,1,0:T(8,128)(2,1)S(1)} all-to-all(bf16[8,544,128]{2,1,0:T(8,128)(2,1)S(1)} %bitcast.76), channel_id=1, replica_groups=mesh['x'=4,'z'=8,'core'=2,'blk'=8] {'blk'}, dimensions={0} | all-to-all | bytes 2228224 | tf_op jit(solution)/shard_map/all_to_all | solution.py:16
  (84 shorter events, 33.9 us)
Async XLA Ops:
  2.5 10.5 %copy-start.9 = (f32[2,32,256]{2,1,0:T(8,128)S(1)}, f32[2,32,256]{2,1,0:T(8,128)}, u32[]{:S(2)}) copy-start(f32[2,32,256]{2,1,0:T(8,128)} %param.5) | copy-start | bytes 196612
  3.4 32.9 %collective-permute-start.7 = (bf16[8,128,256]{2,1,0:T(8,128)(2,1)}, bf16[8,128,256]{2,1,0:T(8,128)(2,1)}, u32[]{:S(2)}, u32[]{:S(2)}) collective-permute-start(bf16[8,128,256]{2,1,0:T(8,128)(2,1)} %slice_bitcast_fusion), channel_id=1, source_target_pairs={{8,0},{9,1},{10,2},{11,3},{12,4},{13,5},{14,6},{15,7}} | collective-permute-start | bytes 1572872 | tf_op jit(solution)/shard_map/ppermute | solution.py:127
  22.8 11.0 %all-to-all-start.1 = ((bf16[8,8,256]{2,1,0:T(8,128)(2,1)}), bf16[8,8,256]{2,1,0:T(8,128)(2,1)}, u32[]{:S(2)}, u32[]{:S(2)}) async-start(bf16[8,8,256]{2,1,0:T(8,128)(2,1)} %slice_bitcast_fusion.4), calls=%async_computation.1 | async-start | bytes 65536 | tf_op jit(solution)/shard_map/all_to_all | solution.py:16
  27.7 27.4 %copy-start = (bf16[4,64,256]{2,1,0:T(8,128)(2,1)}, bf16[4,64,256]{2,1,0:T(8,128)(2,1)S(1)}, u32[]{:S(2)}) copy-start(bf16[4,64,256]{2,1,0:T(8,128)(2,1)S(1)} %slice.56) | copy-start | bytes 393220
  27.7 12.9 %collective-permute-start = (bf16[4,2,32,256]{3,2,1,0:T(8,128)(2,1)S(1)}, bf16[4,2,32,256]{3,2,1,0:T(8,128)(2,1)}, u32[]{:S(2)}, u32[]{:S(2)}) collective-permute-start(bf16[4,2,32,256]{3,2,1,0:T(8,128)(2,1)S(1)} %bitcast.65), channel_id=1, source_target_pairs={{16,0},{17,1},{18,2},{19,3},{20,4},{21,5},{22,6},{23,7},{24,8},{25... | collective-permute-start | bytes 393224 | tf_op jit(solution)/shard_map/ppermute | solution.py:155
  29.0 12.9 %collective-permute-start.1 = (bf16[4,2,32,256]{3,2,1,0:T(8,128)(2,1)S(1)}, bf16[4,2,32,256]{3,2,1,0:T(8,128)(2,1)}, u32[]{:S(2)}, u32[]{:S(2)}) collective-permute-start(bf16[4,2,32,256]{3,2,1,0:T(8,128)(2,1)S(1)} %bitcast.66), channel_id=1, source_target_pairs={{32,0},{33,1},{34,2},{35,3},{36,4},{37,5},{38,6},{39,7},{40,8},{41... | collective-permute-start | bytes 393224 | tf_op jit(solution)/shard_map/ppermute | solution.py:155
  30.3 12.9 %collective-permute-start.2 = (bf16[4,2,32,256]{3,2,1,0:T(8,128)(2,1)S(1)}, bf16[4,2,32,256]{3,2,1,0:T(8,128)(2,1)}, u32[]{:S(2)}, u32[]{:S(2)}) collective-permute-start(bf16[4,2,32,256]{3,2,1,0:T(8,128)(2,1)S(1)} %bitcast.67), channel_id=1, source_target_pairs={{48,0},{49,1},{50,2},{51,3},{52,4},{53,5},{54,6},{55,7},{56,8},{57... | collective-permute-start | bytes 393224 | tf_op jit(solution)/shard_map/ppermute | solution.py:155
  31.6 13.9 %collective-permute-start.3 = (bf16[4,2,32,256]{3,2,1,0:T(8,128)(2,1)S(1)}, bf16[4,2,32,256]{3,2,1,0:T(8,128)(2,1)}, u32[]{:S(2)}, u32[]{:S(2)}) collective-permute-start(bf16[4,2,32,256]{3,2,1,0:T(8,128)(2,1)S(1)} %bitcast.68), channel_id=1, source_target_pairs={{64,0},{65,1},{66,2},{67,3},{68,4},{69,5},{70,6},{71,7},{72,8},{73... | collective-permute-start | bytes 393224 | tf_op jit(solution)/shard_map/ppermute | solution.py:155
  36.4 12.7 %collective-permute-start.4 = (bf16[4,2,32,256]{3,2,1,0:T(8,128)(2,1)S(1)}, bf16[4,2,32,256]{3,2,1,0:T(8,128)(2,1)S(1)}, u32[]{:S(2)}, u32[]{:S(2)}) collective-permute-start(bf16[4,2,32,256]{3,2,1,0:T(8,128)(2,1)S(1)} %bitcast.69), channel_id=1, source_target_pairs={{80,0},{81,1},{82,2},{83,3},{84,4},{85,5},{86,6},{87,7},{88,8},{89... | collective-permute-start | bytes 393224 | tf_op jit(solution)/shard_map/ppermute | solution.py:155
  40.6 12.7 %collective-permute-start.5 = (bf16[4,2,32,256]{3,2,1,0:T(8,128)(2,1)S(1)}, bf16[4,2,32,256]{3,2,1,0:T(8,128)(2,1)S(1)}, u32[]{:S(2)}, u32[]{:S(2)}) collective-permute-start(bf16[4,2,32,256]{3,2,1,0:T(8,128)(2,1)S(1)} %bitcast.70), channel_id=1, source_target_pairs={{96,0},{97,1},{98,2},{99,3},{100,4},{101,5},{102,6},{103,7},{104,8... | collective-permute-start | bytes 393224 | tf_op jit(solution)/shard_map/ppermute | solution.py:155
  41.9 13.2 %collective-permute-start.6 = (bf16[4,2,32,256]{3,2,1,0:T(8,128)(2,1)S(1)}, bf16[4,2,32,256]{3,2,1,0:T(8,128)(2,1)S(1)}, u32[]{:S(2)}, u32[]{:S(2)}) collective-permute-start(bf16[4,2,32,256]{3,2,1,0:T(8,128)(2,1)S(1)} %bitcast.71), channel_id=1, source_target_pairs={{112,0},{113,1},{114,2},{115,3},{116,4},{117,5},{118,6},{119,7},{1... | collective-permute-start | bytes 393224 | tf_op jit(solution)/shard_map/ppermute | solution.py:155
  43.2 32.1 %collective-permute-start.8 = (bf16[1024,256]{1,0:T(8,128)(2,1)}, bf16[1024,256]{1,0:T(8,128)(2,1)S(1)}, u32[]{:S(2)}, u32[]{:S(2)}) collective-permute-start(bf16[1024,256]{1,0:T(8,128)(2,1)} %bitcast.16.refs_0_), channel_id=1, source_target_pairs={{0,128},{1,129},{2,130},{3,131},{4,132},{5,133},{6,134},{7,135},{8... | collective-permute-start | bytes 1572872 | tf_op jit(solution)/shard_map/ppermute | solution.py:131
  45.5 29.9 %collective-permute-start.9 = (bf16[1024,256]{1,0:T(8,128)(2,1)}, bf16[1024,256]{1,0:T(8,128)(2,1)}, u32[]{:S(2)}, u32[]{:S(2)}) collective-permute-start(bf16[1024,256]{1,0:T(8,128)(2,1)} %bitcast.16.refs_0_), channel_id=1, source_target_pairs={{0,256},{1,257},{2,258},{3,259},{4,260},{5,261},{6,262},{7,263},{8... | collective-permute-start | bytes 1572872 | tf_op jit(solution)/shard_map/ppermute | solution.py:131
  49.1 26.3 %collective-permute-start.10 = (bf16[1024,256]{1,0:T(8,128)(2,1)}, bf16[1024,256]{1,0:T(8,128)(2,1)}, u32[]{:S(2)}, u32[]{:S(2)}) collective-permute-start(bf16[1024,256]{1,0:T(8,128)(2,1)} %bitcast.16.refs_0_), channel_id=1, source_target_pairs={{0,384},{1,385},{2,386},{3,387},{4,388},{5,389},{6,390},{7,391},{8... | collective-permute-start | bytes 1572872 | tf_op jit(solution)/shard_map/ppermute | solution.py:131
  58.7 12.7 %all-to-all-start.2 = ((bf16[8,64,128]{2,1,0:T(8,128)(2,1)}), bf16[8,64,128]{2,1,0:T(8,128)(2,1)S(1)}, u32[]{:S(2)}, u32[]{:S(2)}) async-start(bf16[8,64,128]{2,1,0:T(8,128)(2,1)} %shard_map.50), calls=%async_computation.2 | async-start | bytes 262144 | tf_op jit(solution)/shard_map/all_to_all | solution.py:16
  97.5 11.7 %all-to-all-start.4 = ((bf16[8,64,128]{2,1,0:T(8,128)(2,1)}), bf16[8,64,128]{2,1,0:T(8,128)(2,1)S(1)}, u32[]{:S(2)}, u32[]{:S(2)}) async-start(bf16[8,64,128]{2,1,0:T(8,128)(2,1)} %shard_map.52), calls=%async_computation.4 | async-start | bytes 262144 | tf_op jit(solution)/shard_map/all_to_all | solution.py:16
  109.2 7.2 %collective-permute-start.17 = (bf16[2,64,128]{2,1,0:T(8,128)(2,1)S(1)}, bf16[2,64,128]{2,1,0:T(8,128)(2,1)S(1)}, u32[]{:S(2)}, u32[]{:S(2)}) collective-permute-start(bf16[2,64,128]{2,1,0:T(8,128)(2,1)S(1)} %pad_maximum_fusion.1), channel_id=1, source_target_pairs={{0,112},{1,113},{2,114},{3,115},{4,116},{5,117},{6,118},{7,119},{8... | collective-permute-start | bytes 98312 | tf_op jit(solution)/shard_map/ppermute | solution.py:170
  110.5 7.3 %collective-permute-start.16 = (bf16[2,64,128]{2,1,0:T(8,128)(2,1)S(1)}, bf16[2,64,128]{2,1,0:T(8,128)(2,1)S(1)}, u32[]{:S(2)}, u32[]{:S(2)}) collective-permute-start(bf16[2,64,128]{2,1,0:T(8,128)(2,1)S(1)} %pad_maximum_fusion.1), channel_id=1, source_target_pairs={{0,96},{1,97},{2,98},{3,99},{4,100},{5,101},{6,102},{7,103},{8,104... | collective-permute-start | bytes 98312 | tf_op jit(solution)/shard_map/ppermute | solution.py:170
  112.5 6.5 %collective-permute-start.15 = (bf16[2,64,128]{2,1,0:T(8,128)(2,1)S(1)}, bf16[2,64,128]{2,1,0:T(8,128)(2,1)S(1)}, u32[]{:S(2)}, u32[]{:S(2)}) collective-permute-start(bf16[2,64,128]{2,1,0:T(8,128)(2,1)S(1)} %pad_maximum_fusion.1), channel_id=1, source_target_pairs={{0,80},{1,81},{2,82},{3,83},{4,84},{5,85},{6,86},{7,87},{8,88},{9,... | collective-permute-start | bytes 98312 | tf_op jit(solution)/shard_map/ppermute | solution.py:170
  113.8 5.3 %collective-permute-start.14 = (bf16[2,64,128]{2,1,0:T(8,128)(2,1)S(1)}, bf16[2,64,128]{2,1,0:T(8,128)(2,1)S(1)}, u32[]{:S(2)}, u32[]{:S(2)}) collective-permute-start(bf16[2,64,128]{2,1,0:T(8,128)(2,1)S(1)} %pad_maximum_fusion.1), channel_id=1, source_target_pairs={{0,64},{1,65},{2,66},{3,67},{4,68},{5,69},{6,70},{7,71},{8,72},{9,... | collective-permute-start | bytes 98312 | tf_op jit(solution)/shard_map/ppermute | solution.py:170
  115.1 4.0 %collective-permute-start.13 = (bf16[2,64,128]{2,1,0:T(8,128)(2,1)S(1)}, bf16[2,64,128]{2,1,0:T(8,128)(2,1)S(1)}, u32[]{:S(2)}, u32[]{:S(2)}) collective-permute-start(bf16[2,64,128]{2,1,0:T(8,128)(2,1)S(1)} %pad_maximum_fusion.1), channel_id=1, source_target_pairs={{0,48},{1,49},{2,50},{3,51},{4,52},{5,53},{6,54},{7,55},{8,56},{9,... | collective-permute-start | bytes 98312 | tf_op jit(solution)/shard_map/ppermute | solution.py:170
  116.4 2.7 %collective-permute-start.12 = (bf16[2,64,128]{2,1,0:T(8,128)(2,1)S(1)}, bf16[2,64,128]{2,1,0:T(8,128)(2,1)S(1)}, u32[]{:S(2)}, u32[]{:S(2)}) collective-permute-start(bf16[2,64,128]{2,1,0:T(8,128)(2,1)S(1)} %pad_maximum_fusion.1), channel_id=1, source_target_pairs={{0,32},{1,33},{2,34},{3,35},{4,36},{5,37},{6,38},{7,39},{8,40},{9,... | collective-permute-start | bytes 98312 | tf_op jit(solution)/shard_map/ppermute | solution.py:170
  117.7 2.3 %collective-permute-start.11 = (bf16[2,64,128]{2,1,0:T(8,128)(2,1)S(1)}, bf16[2,64,128]{2,1,0:T(8,128)(2,1)S(1)}, u32[]{:S(2)}, u32[]{:S(2)}) collective-permute-start(bf16[2,64,128]{2,1,0:T(8,128)(2,1)S(1)} %pad_maximum_fusion.1), channel_id=1, source_target_pairs={{0,16},{1,17},{2,18},{3,19},{4,20},{5,21},{6,22},{7,23},{8,24},{9,... | collective-permute-start | bytes 98312 | tf_op jit(solution)/shard_map/ppermute | solution.py:170
  120.7 8.1 %all-to-all-start.5 = ((bf16[4,2,64,128]{3,2,1,0:T(8,128)(2,1)}), bf16[4,2,64,128]{3,2,1,0:T(8,128)(2,1)S(1)}, u32[]{:S(2)}, u32[]{:S(2)}) async-start(bf16[4,2,64,128]{3,2,1,0:T(8,128)(2,1)} %broadcast_in_dim.29), calls=%async_computation.5 | async-start | bytes 262144 | tf_op jit(solution)/shard_map/all_to_all | solution.py:16
  (8 other events, 39.4 us)

commit v6 on v4

--- a/solution.py
+++ b/solution.py
@@ -148,21 +148,35 @@
     select = select.astype(HALF)
 
     planes = [inverse] + [lax.ppermute(inverse, "z", [(k, 0)]) for k in range(1, NZ)]
-    partial = run_kernel(first_kernel, *sizes, (), pivot[0], *planes)
-    first = scatter_sum(partial).astype(HALF)
+
+    def first_half(pivot, planes):
+        partial = run_kernel(first_kernel, *sizes, (), pivot, *planes)
+        first = scatter_sum(partial).astype(HALF)
+        return first, lax.all_gather(first, "core", axis=0, tiled=False)
+
+    def second_half(first, pair, pivot, planes, cross):
+        partial = run_kernel(cross_kernel, *sizes, (), owner, pair, pair_order, *cross)
+        pair = lax.all_gather(scatter_sum(partial), "core", axis=0, tiled=False)
+        scratch = (pltpu.VMEM((t, width), HALF),)
+        partial = run_kernel(second_kernel, *sizes, scratch, pivot, pair, *planes)
+        return jnp.stack([first, scatter_sum(partial).astype(HALF)])
+
+    def none_first(pivot, planes):
+        return jnp.zeros((t, half), HALF), jnp.zeros((NC, t, half), HALF)
+
+    def none_second(first, pair, pivot, planes, cross):
+        return jnp.zeros((STEPS, t, half), HALF)
+
+    first, pair = lax.cond(z == 0, first_half, none_first, pivot[0], planes)
     first, panels = lax.optimization_barrier((first, panels))
-    pair = lax.all_gather(first, "core", axis=0, tiled=False)
-    partial = run_kernel(cross_kernel, *sizes, (), owner, pair, pair_order, *cross)
-    update = scatter_sum(partial)
-    pair = lax.all_gather(update, "core", axis=0, tiled=False)
-    scratch = (pltpu.VMEM((t, width), HALF),)
-    partial = run_kernel(second_kernel, *sizes, scratch, pivot[1], pair, *planes)
-    second = scatter_sum(partial).astype(HALF)
-
-    solved = jnp.stack([first, second])
-    spread = jnp.where(z == 0, solved, jnp.zeros_like(solved))
+    solved = lax.cond(
+        z == 0, second_half, none_second, first, pair, pivot[1], planes, cross
+    )
+
+    spread = solved
     for k in range(1, NZ):
-        spread = spread + lax.ppermute(solved, "z", [(0, k)])
+        received = lax.ppermute(solved, "z", [(0, k)])
+        spread = spread + received
     spread = ordered(both_cores(gather_by_swap(spread, "x", NX)))
     spread = spread.reshape(NX, STEPS, n_blk, dates_x, width).transpose(2, 0, 3, 1, 4)
     spread = spread.reshape(dates_local * n_blk, STEPS * width)

time: 169 us -> 175 us (1.036)
  waiting for transfers between devices: 26.1 us -> 30.6 us
  blocking collectives: 67.4 us -> 70.7 us
    all_to_all x4, waiting for transfers between devices: 19.7 us -> 24.1 us  [swap_blocks(): return lax.all_to_all(array, axis, split_axis=0, concat_axis=0, tiled=True)]
    all_to_all x3, blocking collectives: 52.5 us -> 55.7 us  [swap_blocks(): return lax.all_to_all(array, axis, split_axis=0, concat_axis=0, tiled=True)]
    unnamed x22 -> x16, local copies, waits for them, and re-layouts: 4.04 us -> 1.93 us
  transfers between devices with their start and end apart: 22 -> 22, of which waited for: 8 -> 6; matrix products, arithmetic and copies ran while one was open for 3% -> 4% of each run, Pallas kernels for 1% -> 1%
where the time goes in v6:
time: 175 us; the launch traced here: 174 us
  blocking collectives  70.7 us (40%)
  starting transfers between devices  49.5 us (28%)
  waiting for transfers between devices  30.6 us (17%)
  local copies, waits for them, and re-layouts  8.08 us (5%)
  Pallas kernels  6.75 us (4%)
  other arithmetic  5.91 us (3%)
    all_to_all x3, blocking collectives, swap_blocks(): return lax.all_to_all(array, axis, split_axis=0, concat_axis=0, tiled=True)  55.7 us
    all_to_all x4, waiting for transfers between devices, swap_blocks(): return lax.all_to_all(array, axis, split_axis=0, concat_axis=0, tiled=True)  24.1 us
    all_to_all x4, starting transfers between devices, swap_blocks(): return lax.all_to_all(array, axis, split_axis=0, concat_axis=0, tiled=True)  14.1 us
    ppermute x1, starting transfers between devices, local(): sent = lax.ppermute(halves[:, 0], ('x', 'z', 'core'), [(1, 0)])  9.54 us
    ppermute x7, starting transfers between devices, local(): lax.ppermute(inverse, 'z', [(k, 0)])  9.04 us
    ppermute x7, starting transfers between devices, local(): received = lax.ppermute(solved, 'z', [(0, k)])  9.02 us
    ppermute x3, starting transfers between devices, local(): lax.ppermute(lower, ('x', 'z'), [(0, k * NZ)])  7.79 us
    pallas_call x3, Pallas kernels, run_kernel(): pl.pallas_call(kernel, in_specs=[pl.BlockSpec(memory_space=space) for spa...  6.75 us
  transfers between devices with their start and end apart: 22, of which 6 were waited for; matrix products, arithmetic and copies ran while one was open for 4% of the time, Pallas kernels for 1%

profile of v6, /device:TPU:1, one launch (start us, length us, event | category | flops | bytes accessed | tf_op | source)
XLA Modules:
  0.0 173.8 jit_solution(1506954228624996945)
XLA Ops:
  3.5 9.5 %collective-permute-start.7 = (bf16[8,128,256]{2,1,0:T(8,128)(2,1)}, bf16[8,128,256]{2,1,0:T(8,128)(2,1)}, u32[]{:S(2)}, u32[]{:S(2)}) collective-permute-start(bf16[8,128,256]{2,1,0:T(8,128)(2,1)} %slice_bitcast_fusion.2), channel_id=1, source_target_pairs={{8,0},{9,1},{10,2},{11,3},{12,4},{13,5},{14,6},{15,7}} | collective-permute-start | bytes 1572872 | tf_op jit(solution)/shard_map/ppermute | solution.py:123
  13.8 4.0 %all-to-all-start.3 = ((bf16[4,128,256]{2,1,0:T(8,128)(2,1)}), bf16[4,128,256]{2,1,0:T(8,128)(2,1)}, u32[]{:S(2)}, u32[]{:S(2)}) async-start(bf16[4,128,256]{2,1,0:T(8,128)(2,1)} %pad_maximum_fusion.1), calls=%async_computation.3 | async-start | bytes 524288 | tf_op jit(solution)/shard_map/all_to_all | solution.py:16
  17.9 6.0 %all-to-all-done.3 = bf16[4,128,256]{2,1,0:T(8,128)(2,1)} async-done(((bf16[4,128,256]{2,1,0:T(8,128)(2,1)}), bf16[4,128,256]{2,1,0:T(8,128)(2,1)}, u32[]{:S(2)}, u32[]{:S(2)}) %all-to-all-start.3) | async-done | bytes 262176 | tf_op jit(solution)/shard_map/all_to_all | solution.py:16
  32.2 5.5 %collective-permute-done = bf16[4,2,32,256]{3,2,1,0:T(8,128)(2,1)S(1)} collective-permute-done((bf16[4,2,32,256]{3,2,1,0:T(8,128)(2,1)S(1)}, bf16[4,2,32,256]{3,2,1,0:T(8,128)(2,1)S(1)}, u32[]{:S(2)}, u32[]{:S(2)}) %collective-permute-start) | collective-permute-done | bytes 131104 | tf_op jit(solution)/shard_map/ppermute | solution.py:150
  37.7 3.6 %collective-permute-start.10 = (bf16[8,128,256]{2,1,0:T(8,128)(2,1)}, bf16[8,128,256]{2,1,0:T(8,128)(2,1)}, u32[]{:S(2)}, u32[]{:S(2)}) collective-permute-start(bf16[8,128,256]{2,1,0:T(8,128)(2,1)} %fusion.6), channel_id=1, source_target_pairs={{0,384},{1,385},{2,386},{3,387},{4,388},{5,389},{6,390},{7,391},{8... | collective-permute-start | bytes 1572872 | tf_op jit(solution)/shard_map/ppermute | solution.py:126
  41.3 2.1 %collective-permute-start.8 = (bf16[8,128,256]{2,1,0:T(8,128)(2,1)}, bf16[8,128,256]{2,1,0:T(8,128)(2,1)}, u32[]{:S(2)}, u32[]{:S(2)}) collective-permute-start(bf16[8,128,256]{2,1,0:T(8,128)(2,1)} %fusion.6), channel_id=1, source_target_pairs={{0,128},{1,129},{2,130},{3,131},{4,132},{5,133},{6,134},{7,135},{8... | collective-permute-start | bytes 1572872 | tf_op jit(solution)/shard_map/ppermute | solution.py:126
  43.4 2.1 %collective-permute-start.9 = (bf16[8,128,256]{2,1,0:T(8,128)(2,1)}, bf16[8,128,256]{2,1,0:T(8,128)(2,1)}, u32[]{:S(2)}, u32[]{:S(2)}) collective-permute-start(bf16[8,128,256]{2,1,0:T(8,128)(2,1)} %fusion.6), channel_id=1, source_target_pairs={{0,256},{1,257},{2,258},{3,259},{4,260},{5,261},{6,262},{7,263},{8... | collective-permute-start | bytes 1572872 | tf_op jit(solution)/shard_map/ppermute | solution.py:126
  49.6 3.3 %all-to-all-start.4 = ((bf16[8,8,256]{2,1,0:T(8,128)(2,1)}), bf16[8,8,256]{2,1,0:T(8,128)(2,1)S(1)}, u32[]{:S(2)}, u32[]{:S(2)}) async-start(bf16[8,8,256]{2,1,0:T(8,128)(2,1)} %slice_bitcast_fusion.4), calls=%async_computation.4 | async-start | bytes 65536 | tf_op jit(solution)/shard_map/all_to_all | solution.py:16
  53.0 6.8 %all-to-all-done.4 = bf16[8,8,256]{2,1,0:T(8,128)(2,1)S(1)} async-done(((bf16[8,8,256]{2,1,0:T(8,128)(2,1)}), bf16[8,8,256]{2,1,0:T(8,128)(2,1)S(1)}, u32[]{:S(2)}, u32[]{:S(2)}) %all-to-all-start.4) | async-done | bytes 32800 | tf_op jit(solution)/shard_map/all_to_all | solution.py:16
  59.8 3.4 %all_gather.21 = bf16[2,64,256]{2,1,0:T(8,128)(2,1)S(1)} all-gather(bf16[1,64,256]{2,1,0:T(8,128)(2,1)S(1)} %bitcast.81), channel_id=1, replica_groups=mesh['x'=4,'z'=8,'core'=2,'blk'=8] {'core'}, dimensions={0}, use_global_device_ids=true | all-gather | bytes 98304 | tf_op jit(solution)/shard_map/all_gather | solution.py:119
  63.2 18.3 %conditional.2 = (bf16[64,128]{1,0:T(8,128)(2,1)}, bf16[2,64,128]{2,1,0:T(8,128)(2,1)S(1)}) conditional(s32[]{:T(128)} %convert_element_type.37, () %tuple.24, (bf16[2,64,256]{2,1,0:T(8,128)(2,1)S(1)}, bf16[4,2,32,256]{3,2,1,0:T(8,128)(2,1)S(1)}, bf16[4,2,32,256]{3,2,1,0:T(8,128)(2,1)}, bf16[4,2,32,256]{3,2,1,0:T(8,128)(2,1)}, ...), branch_computations={%region_0.1_spmd, %region_1.3_spmd} | conditional | flops 57344 | bytes 524306 | solution.py:170
  63.8 2.1 %branch_1_fun.3 = bf16[8,64,128]{2,1,0:T(8,128)(2,1)} custom-call(bf16[64,256]{1,0:T(8,128)(2,1)} %slice_bitcast_fusion.pivot, bf16[4,2,32,256]{3,2,1,0:T(8,128)(2,1)S(1)} %get-tuple-element.61.refs_0_, bf16[4,2,32,256]{3,2,1,0:T(8,128)(2,1)} %get-tuple-element.62.refs_1_, bf16[4,2,32,256]{3,2,1,0:T(8,128)(2,1)} %get-tuple-element.63.refs_2_, ...), custom_call_target="tpu_custom_call" | custom-call | tf_op jit(solution)/shard_map/cond/branch_1_fun/pallas_call | solution.py:87
  65.9 11.6 %all_to_all.32 = bf16[8,64,128]{2,1,0:T(8,128)(2,1)S(1)} all-to-all(bf16[8,64,128]{2,1,0:T(8,128)(2,1)} %branch_1_fun.3), channel_id=1, replica_groups=mesh['x'=4,'z'=8,'core'=2,'blk'=8] {'blk'}, dimensions={0} | all-to-all | bytes 262144 | tf_op jit(solution)/shard_map/cond/branch_1_fun/all_to_all | solution.py:16
  78.2 3.3 %all-gather = bf16[128,128]{1,0:T(8,128)(2,1)S(1)} all-gather(bf16[64,128]{1,0:T(8,128)(2,1)} %reduce_sum.38), channel_id=2, replica_groups=mesh['x'=4,'z'=8,'core'=2,'blk'=8] {'core'}, dimensions={0}, use_global_device_ids=true | all-gather | bytes 49152 | tf_op jit(solution)/shard_map/cond/branch_1_fun/all_gather | solution.py:155
  81.5 32.1 %conditional.3 = (bf16[2,64,128]{2,1,0:T(8,128)(2,1)S(1)}) conditional(s32[]{:T(128)} %convert_element_type.37, () %tuple.23, (bf16[64,128]{1,0:T(8,128)(2,1)}, bf16[2,64,256]{2,1,0:T(8,128)(2,1)S(1)}, s32[]{:T(128)}, bf16[2,64,128]{2,1,0:T(8,128)(2,1)S(1)}, bf16[2,256,128]{2,1,0:T(8,128)(2,1)S(1)}, /*index=5*/bf16[8,128,256]{2,1,0:T(8,128)(2,1)}, ...), branch_computations={%region_3.4_spmd, %region_4.7_spmd} | conditional | flops 196608 | bytes 2769022 | solution.py:172
  81.6 2.7 %branch_1_fun.4 = bf16[8,64,128]{2,1,0:T(8,128)(2,1)} custom-call(s32[1]{0:T(128)} %bitcast.4.owner, bf16[2,64,128]{2,1,0:T(8,128)(2,1)S(1)} %get-tuple-element.72.pair, bf16[2,256,128]{2,1,0:T(8,128)(2,1)S(1)} %get-tuple-element.73.order, bf16[8,128,256]{2,1,0:T(8,128)(2,1)} %get-tuple-element.74.own, bf16[8,128,256]{2,1,0:T(8,128)(2,1)} %get-tuple-element.75.refs_0_, ...), custom_call_target="tpu_custom_call" | custom-call | tf_op jit(solution)/shard_map/cond/branch_1_fun/pallas_call | solution.py:87
  84.3 3.4 %all-to-all-start.1 = ((bf16[8,64,128]{2,1,0:T(8,128)(2,1)}), bf16[8,64,128]{2,1,0:T(8,128)(2,1)S(1)}, u32[]{:S(2)}, u32[]{:S(2)}) async-start(bf16[8,64,128]{2,1,0:T(8,128)(2,1)} %branch_1_fun.4), calls=%async_computation.1 | async-start | bytes 262144 | tf_op jit(solution)/shard_map/cond/branch_1_fun/all_to_all | solution.py:16
  88.2 7.6 %all-to-all-done.1 = bf16[8,64,128]{2,1,0:T(8,128)(2,1)S(1)} async-done(((bf16[8,64,128]{2,1,0:T(8,128)(2,1)}), bf16[8,64,128]{2,1,0:T(8,128)(2,1)S(1)}, u32[]{:S(2)}, u32[]{:S(2)}) %all-to-all-start.1) | async-done | bytes 131104 | tf_op jit(solution)/shard_map/cond/branch_1_fun/all_to_all | solution.py:16
  95.9 3.3 %all-gather.1 = f32[128,128]{1,0:T(8,128)} all-gather(f32[64,128]{1,0:T(8,128)S(1)} %convert_reduce_fusion), channel_id=3, replica_groups=mesh['x'=4,'z'=8,'core'=2,'blk'=8] {'core'}, dimensions={0}, use_global_device_ids=true | all-gather | bytes 98304 | tf_op jit(solution)/shard_map/cond/branch_1_fun/all_gather | solution.py:159
  101.2 11.7 %all_to_all.33 = bf16[8,64,128]{2,1,0:T(8,128)(2,1)S(1)} all-to-all(bf16[8,64,128]{2,1,0:T(8,128)(2,1)} %branch_1_fun.5), channel_id=1, replica_groups=mesh['x'=4,'z'=8,'core'=2,'blk'=8] {'blk'}, dimensions={0} | all-to-all | bytes 262144 | tf_op jit(solution)/shard_map/cond/branch_1_fun/all_to_all | solution.py:16
  125.2 3.3 %all-to-all-start.5 = ((bf16[4,2,64,128]{3,2,1,0:T(8,128)(2,1)}), bf16[4,2,64,128]{3,2,1,0:T(8,128)(2,1)S(1)}, u32[]{:S(2)}, u32[]{:S(2)}) async-start(bf16[4,2,64,128]{3,2,1,0:T(8,128)(2,1)} %broadcast_in_dim.12), calls=%async_computation.5 | async-start | bytes 262144 | tf_op jit(solution)/shard_map/all_to_all | solution.py:16
  129.6 3.7 %all-to-all-done.5 = bf16[4,2,64,128]{3,2,1,0:T(8,128)(2,1)S(1)} async-done(((bf16[4,2,64,128]{3,2,1,0:T(8,128)(2,1)}), bf16[4,2,64,128]{3,2,1,0:T(8,128)(2,1)S(1)}, u32[]{:S(2)}, u32[]{:S(2)}) %all-to-all-start.5) | async-done | bytes 131104 | tf_op jit(solution)/shard_map/all_to_all | solution.py:16
  133.3 5.0 %all-gather.2 = bf16[8,2,64,128]{3,2,1,0:T(8,128)(2,1)S(1)} all-gather(bf16[4,2,64,128]{3,2,1,0:T(8,128)(2,1)S(1)} %all-to-all-done.5), channel_id=4, replica_groups=mesh['x'=4,'z'=8,'core'=2,'blk'=8] {'core'}, dimensions={0}, use_global_device_ids=true | all-gather | bytes 393216 | tf_op jit(solution)/shard_map/all_gather | solution.py:140
  139.7 32.4 %all_to_all.34 = bf16[8,544,128]{2,1,0:T(8,128)(2,1)S(1)} all-to-all(bf16[8,544,128]{2,1,0:T(8,128)(2,1)S(1)} %bitcast.75), channel_id=1, replica_groups=mesh['x'=4,'z'=8,'core'=2,'blk'=8] {'blk'}, dimensions={0} | all-to-all | bytes 2228224 | tf_op jit(solution)/shard_map/all_to_all | solution.py:16
  (87 shorter events, 36.1 us)
Async XLA Ops:
  3.5 26.5 %collective-permute-start.7 = (bf16[8,128,256]{2,1,0:T(8,128)(2,1)}, bf16[8,128,256]{2,1,0:T(8,128)(2,1)}, u32[]{:S(2)}, u32[]{:S(2)}) collective-permute-start(bf16[8,128,256]{2,1,0:T(8,128)(2,1)} %slice_bitcast_fusion.2), channel_id=1, source_target_pairs={{8,0},{9,1},{10,2},{11,3},{12,4},{13,5},{14,6},{15,7}} | collective-permute-start | bytes 1572872 | tf_op jit(solution)/shard_map/ppermute | solution.py:123
  13.8 10.1 %all-to-all-start.3 = ((bf16[4,128,256]{2,1,0:T(8,128)(2,1)}), bf16[4,128,256]{2,1,0:T(8,128)(2,1)}, u32[]{:S(2)}, u32[]{:S(2)}) async-start(bf16[4,128,256]{2,1,0:T(8,128)(2,1)} %pad_maximum_fusion.1), calls=%async_computation.3 | async-start | bytes 524288 | tf_op jit(solution)/shard_map/all_to_all | solution.py:16
  24.8 12.9 %collective-permute-start = (bf16[4,2,32,256]{3,2,1,0:T(8,128)(2,1)S(1)}, bf16[4,2,32,256]{3,2,1,0:T(8,128)(2,1)S(1)}, u32[]{:S(2)}, u32[]{:S(2)}) collective-permute-start(bf16[4,2,32,256]{3,2,1,0:T(8,128)(2,1)S(1)} %bitcast.64), channel_id=1, source_target_pairs={{16,0},{17,1},{18,2},{19,3},{20,4},{21,5},{22,6},{23,7},{24,8},{25... | collective-permute-start | bytes 393224 | tf_op jit(solution)/shard_map/ppermute | solution.py:150
  26.1 15.2 %collective-permute-start.1 = (bf16[4,2,32,256]{3,2,1,0:T(8,128)(2,1)S(1)}, bf16[4,2,32,256]{3,2,1,0:T(8,128)(2,1)S(1)}, u32[]{:S(2)}, u32[]{:S(2)}) collective-permute-start(bf16[4,2,32,256]{3,2,1,0:T(8,128)(2,1)S(1)} %bitcast.65), channel_id=1, source_target_pairs={{32,0},{33,1},{34,2},{35,3},{36,4},{37,5},{38,6},{39,7},{40,8},{41... | collective-permute-start | bytes 393224 | tf_op jit(solution)/shard_map/ppermute | solution.py:150
  27.4 16.0 %collective-permute-start.2 = (bf16[4,2,32,256]{3,2,1,0:T(8,128)(2,1)S(1)}, bf16[4,2,32,256]{3,2,1,0:T(8,128)(2,1)S(1)}, u32[]{:S(2)}, u32[]{:S(2)}) collective-permute-start(bf16[4,2,32,256]{3,2,1,0:T(8,128)(2,1)S(1)} %bitcast.66), channel_id=1, source_target_pairs={{48,0},{49,1},{50,2},{51,3},{52,4},{53,5},{54,6},{55,7},{56,8},{57... | collective-permute-start | bytes 393224 | tf_op jit(solution)/shard_map/ppermute | solution.py:150
  28.7 16.9 %collective-permute-start.3 = (bf16[4,2,32,256]{3,2,1,0:T(8,128)(2,1)S(1)}, bf16[4,2,32,256]{3,2,1,0:T(8,128)(2,1)}, u32[]{:S(2)}, u32[]{:S(2)}) collective-permute-start(bf16[4,2,32,256]{3,2,1,0:T(8,128)(2,1)S(1)} %bitcast.67), channel_id=1, source_target_pairs={{64,0},{65,1},{66,2},{67,3},{68,4},{69,5},{70,6},{71,7},{72,8},{73... | collective-permute-start | bytes 393224 | tf_op jit(solution)/shard_map/ppermute | solution.py:150
  30.0 16.9 %collective-permute-start.4 = (bf16[4,2,32,256]{3,2,1,0:T(8,128)(2,1)S(1)}, bf16[4,2,32,256]{3,2,1,0:T(8,128)(2,1)}, u32[]{:S(2)}, u32[]{:S(2)}) collective-permute-start(bf16[4,2,32,256]{3,2,1,0:T(8,128)(2,1)S(1)} %bitcast.68), channel_id=1, source_target_pairs={{80,0},{81,1},{82,2},{83,3},{84,4},{85,5},{86,6},{87,7},{88,8},{89... | collective-permute-start | bytes 393224 | tf_op jit(solution)/shard_map/ppermute | solution.py:150
  37.7 43.8 %collective-permute-start.10 = (bf16[8,128,256]{2,1,0:T(8,128)(2,1)}, bf16[8,128,256]{2,1,0:T(8,128)(2,1)}, u32[]{:S(2)}, u32[]{:S(2)}) collective-permute-start(bf16[8,128,256]{2,1,0:T(8,128)(2,1)} %fusion.6), channel_id=1, source_target_pairs={{0,384},{1,385},{2,386},{3,387},{4,388},{5,389},{6,390},{7,391},{8... | collective-permute-start | bytes 1572872 | tf_op jit(solution)/shard_map/ppermute | solution.py:126
  41.3 40.2 %collective-permute-start.8 = (bf16[8,128,256]{2,1,0:T(8,128)(2,1)}, bf16[8,128,256]{2,1,0:T(8,128)(2,1)}, u32[]{:S(2)}, u32[]{:S(2)}) collective-permute-start(bf16[8,128,256]{2,1,0:T(8,128)(2,1)} %fusion.6), channel_id=1, source_target_pairs={{0,128},{1,129},{2,130},{3,131},{4,132},{5,133},{6,134},{7,135},{8... | collective-permute-start | bytes 1572872 | tf_op jit(solution)/shard_map/ppermute | solution.py:126
  43.4 38.1 %collective-permute-start.9 = (bf16[8,128,256]{2,1,0:T(8,128)(2,1)}, bf16[8,128,256]{2,1,0:T(8,128)(2,1)}, u32[]{:S(2)}, u32[]{:S(2)}) collective-permute-start(bf16[8,128,256]{2,1,0:T(8,128)(2,1)} %fusion.6), channel_id=1, source_target_pairs={{0,256},{1,257},{2,258},{3,259},{4,260},{5,261},{6,262},{7,263},{8... | collective-permute-start | bytes 1572872 | tf_op jit(solution)/shard_map/ppermute | solution.py:126
  45.6 17.6 %collective-permute-start.5 = (bf16[4,2,32,256]{3,2,1,0:T(8,128)(2,1)S(1)}, bf16[4,2,32,256]{3,2,1,0:T(8,128)(2,1)S(1)}, u32[]{:S(2)}, u32[]{:S(2)}) collective-permute-start(bf16[4,2,32,256]{3,2,1,0:T(8,128)(2,1)S(1)} %bitcast.69), channel_id=1, source_target_pairs={{96,0},{97,1},{98,2},{99,3},{100,4},{101,5},{102,6},{103,7},{104,8... | collective-permute-start | bytes 393224 | tf_op jit(solution)/shard_map/ppermute | solution.py:150
  46.9 16.3 %collective-permute-start.6 = (bf16[4,2,32,256]{3,2,1,0:T(8,128)(2,1)S(1)}, bf16[4,2,32,256]{3,2,1,0:T(8,128)(2,1)S(1)}, u32[]{:S(2)}, u32[]{:S(2)}) collective-permute-start(bf16[4,2,32,256]{3,2,1,0:T(8,128)(2,1)S(1)} %bitcast.70), channel_id=1, source_target_pairs={{112,0},{113,1},{114,2},{115,3},{116,4},{117,5},{118,6},{119,7},{1... | collective-permute-start | bytes 393224 | tf_op jit(solution)/shard_map/ppermute | solution.py:150
  49.6 10.1 %all-to-all-start.4 = ((bf16[8,8,256]{2,1,0:T(8,128)(2,1)}), bf16[8,8,256]{2,1,0:T(8,128)(2,1)S(1)}, u32[]{:S(2)}, u32[]{:S(2)}) async-start(bf16[8,8,256]{2,1,0:T(8,128)(2,1)} %slice_bitcast_fusion.4), calls=%async_computation.4 | async-start | bytes 65536 | tf_op jit(solution)/shard_map/all_to_all | solution.py:16
  81.5 17.7 %copy-start.3 = (bf16[4,2,32,256]{3,2,1,0:T(8,128)(2,1)S(1)}, bf16[4,2,32,256]{3,2,1,0:T(8,128)(2,1)}, u32[]{:S(2)}) copy-start(bf16[4,2,32,256]{3,2,1,0:T(8,128)(2,1)} %get-tuple-element.79.refs_1_) | copy-start | bytes 393220 | tf_op jit(solution)/shard_map/cond
  81.6 17.7 %copy-start.5 = (bf16[4,2,32,256]{3,2,1,0:T(8,128)(2,1)S(1)}, bf16[4,2,32,256]{3,2,1,0:T(8,128)(2,1)}, u32[]{:S(2)}) copy-start(bf16[4,2,32,256]{3,2,1,0:T(8,128)(2,1)} %get-tuple-element.80.refs_2_) | copy-start | bytes 393220 | tf_op jit(solution)/shard_map/cond
  84.3 11.6 %all-to-all-start.1 = ((bf16[8,64,128]{2,1,0:T(8,128)(2,1)}), bf16[8,64,128]{2,1,0:T(8,128)(2,1)S(1)}, u32[]{:S(2)}, u32[]{:S(2)}) async-start(bf16[8,64,128]{2,1,0:T(8,128)(2,1)} %branch_1_fun.4), calls=%async_computation.1 | async-start | bytes 262144 | tf_op jit(solution)/shard_map/cond/branch_1_fun/all_to_all | solution.py:16
  113.6 7.2 %collective-permute-start.11 = (bf16[2,64,128]{2,1,0:T(8,128)(2,1)S(1)}, bf16[2,64,128]{2,1,0:T(8,128)(2,1)S(1)}, u32[]{:S(2)}, u32[]{:S(2)}) collective-permute-start(bf16[2,64,128]{2,1,0:T(8,128)(2,1)S(1)} %get-tuple-element.104), channel_id=1, source_target_pairs={{0,16},{1,17},{2,18},{3,19},{4,20},{5,21},{6,22},{7,23},{8,24},{9,... | collective-permute-start | bytes 98312 | tf_op jit(solution)/shard_map/ppermute | solution.py:178
  114.9 7.3 %collective-permute-start.12 = (bf16[2,64,128]{2,1,0:T(8,128)(2,1)S(1)}, bf16[2,64,128]{2,1,0:T(8,128)(2,1)S(1)}, u32[]{:S(2)}, u32[]{:S(2)}) collective-permute-start(bf16[2,64,128]{2,1,0:T(8,128)(2,1)S(1)} %get-tuple-element.104), channel_id=1, source_target_pairs={{0,32},{1,33},{2,34},{3,35},{4,36},{5,37},{6,38},{7,39},{8,40},{9,... | collective-permute-start | bytes 98312 | tf_op jit(solution)/shard_map/ppermute | solution.py:178
  117.0 6.5 %collective-permute-start.13 = (bf16[2,64,128]{2,1,0:T(8,128)(2,1)S(1)}, bf16[2,64,128]{2,1,0:T(8,128)(2,1)S(1)}, u32[]{:S(2)}, u32[]{:S(2)}) collective-permute-start(bf16[2,64,128]{2,1,0:T(8,128)(2,1)S(1)} %get-tuple-element.104), channel_id=1, source_target_pairs={{0,48},{1,49},{2,50},{3,51},{4,52},{5,53},{6,54},{7,55},{8,56},{9,... | collective-permute-start | bytes 98312 | tf_op jit(solution)/shard_map/ppermute | solution.py:178
  118.3 5.3 %collective-permute-start.14 = (bf16[2,64,128]{2,1,0:T(8,128)(2,1)S(1)}, bf16[2,64,128]{2,1,0:T(8,128)(2,1)S(1)}, u32[]{:S(2)}, u32[]{:S(2)}) collective-permute-start(bf16[2,64,128]{2,1,0:T(8,128)(2,1)S(1)} %get-tuple-element.104), channel_id=1, source_target_pairs={{0,64},{1,65},{2,66},{3,67},{4,68},{5,69},{6,70},{7,71},{8,72},{9,... | collective-permute-start | bytes 98312 | tf_op jit(solution)/shard_map/ppermute | solution.py:178
  119.6 4.0 %collective-permute-start.15 = (bf16[2,64,128]{2,1,0:T(8,128)(2,1)S(1)}, bf16[2,64,128]{2,1,0:T(8,128)(2,1)S(1)}, u32[]{:S(2)}, u32[]{:S(2)}) collective-permute-start(bf16[2,64,128]{2,1,0:T(8,128)(2,1)S(1)} %get-tuple-element.104), channel_id=1, source_target_pairs={{0,80},{1,81},{2,82},{3,83},{4,84},{5,85},{6,86},{7,87},{8,88},{9,... | collective-permute-start | bytes 98312 | tf_op jit(solution)/shard_map/ppermute | solution.py:178
  120.9 2.7 %collective-permute-start.16 = (bf16[2,64,128]{2,1,0:T(8,128)(2,1)S(1)}, bf16[2,64,128]{2,1,0:T(8,128)(2,1)S(1)}, u32[]{:S(2)}, u32[]{:S(2)}) collective-permute-start(bf16[2,64,128]{2,1,0:T(8,128)(2,1)S(1)} %get-tuple-element.104), channel_id=1, source_target_pairs={{0,96},{1,97},{2,98},{3,99},{4,100},{5,101},{6,102},{7,103},{8,104... | collective-permute-start | bytes 98312 | tf_op jit(solution)/shard_map/ppermute | solution.py:178
  122.2 2.3 %collective-permute-start.17 = (bf16[2,64,128]{2,1,0:T(8,128)(2,1)S(1)}, bf16[2,64,128]{2,1,0:T(8,128)(2,1)S(1)}, u32[]{:S(2)}, u32[]{:S(2)}) collective-permute-start(bf16[2,64,128]{2,1,0:T(8,128)(2,1)S(1)} %get-tuple-element.104), channel_id=1, source_target_pairs={{0,112},{1,113},{2,114},{3,115},{4,116},{5,117},{6,118},{7,119},{8... | collective-permute-start | bytes 98312 | tf_op jit(solution)/shard_map/ppermute | solution.py:178
  125.2 8.1 %all-to-all-start.5 = ((bf16[4,2,64,128]{3,2,1,0:T(8,128)(2,1)}), bf16[4,2,64,128]{3,2,1,0:T(8,128)(2,1)S(1)}, u32[]{:S(2)}, u32[]{:S(2)}) async-start(bf16[4,2,64,128]{3,2,1,0:T(8,128)(2,1)} %broadcast_in_dim.12), calls=%async_computation.5 | async-start | bytes 262144 | tf_op jit(solution)/shard_map/all_to_all | solution.py:16
  (8 other events, 69.3 us)

commit v7 on v6

--- a/solution.py
+++ b/solution.py
@@ -43,10 +43,23 @@
         out[g] = total[:, g * size : (g + 1) * size]
 
 
+def pack_kernel(inverse, pivot, out):
+    count, _, width = out.shape
+    steps, size, _ = inverse.shape
+    dates = pivot.shape[0] // count
+    for x in range(count):
+        for k in range(steps):
+            out[x, k * size : (k + 1) * size, :] = inverse[k].astype(out.dtype)
+        for g in range(pivot.shape[1] // width):
+            at = steps * size + g * dates
+            part = pivot[x * dates : (x + 1) * dates, g * width : (g + 1) * width]
+            out[x, at : at + dates, :] = part.astype(out.dtype)
+
+
 def first_kernel(pivot, *refs):
     planes, (out, whole) = refs[:NZ], refs[NZ:]
     assemble(planes, 0, whole)
-    write_blocks(pivot[...], whole, out)
+    write_blocks(pivot[0], whole, out)
 
 
 def cross_kernel(owner, pair, order, own, *refs):
@@ -77,7 +90,7 @@
     assemble(planes, 1, whole)
     half = update.shape[2]
     for c in range(NC):
-        part = pivot[:, c * half : (c + 1) * half].astype(WIDE) - update[c]
+        part = pivot[1, :, c * half : (c + 1) * half].astype(WIDE) - update[c]
         value[:, c * half : (c + 1) * half] = part.astype(HALF)
     write_blocks(value[...], whole, out)
 
@@ -107,11 +120,13 @@
     per_blk = width // rows_local
     half = width // NC
 
-    copies = block_inverse.astype(HALF).reshape(1, STEPS * rows_local, width)
-    copies = jnp.broadcast_to(copies, (NX, *copies.shape[1:]))
-    pivot = right_side.astype(HALF).reshape(NX, dates_x, n_blk, width)
-    pivot = pivot.transpose(0, 2, 1, 3).reshape(NX, n_blk * dates_x, width)
-    both = swap_blocks(jnp.concatenate([copies, pivot], axis=1), "x")
+    packed = pl.pallas_call(
+        pack_kernel,
+        out_shape=jax.ShapeDtypeStruct(
+            (NX, STEPS * rows_local + n_blk * dates_x, width), HALF
+        ),
+    )(block_inverse, right_side)
+    both = swap_blocks(packed, "x")
     inverse = both[:, : STEPS * rows_local].reshape(NX, STEPS, rows_local, width)
     mine = both[0, STEPS * rows_local :].reshape(n_blk, dates_x, width)
 
@@ -140,38 +155,40 @@
         pair = lax.all_gather(value, "core", axis=0, tiled=False)
         return jnp.concatenate([pair[0], pair[1]], axis=-1)
 
+    planes = [inverse]
+    for k in range(1, NZ):
+        planes.append(lax.ppermute(inverse, "z", [(k, 0)]))
+
+    def first_half(pivot, planes):
+        partial = run_kernel(first_kernel, *sizes, (), pivot, *planes)
+        first = scatter_sum(partial).astype(HALF)
+        return first, lax.all_gather(first, "core", axis=0, tiled=False)
+
+    def second_half(first, pair, pivot, planes, cross):
+        partial = run_kernel(cross_kernel, *sizes, (), owner, pair, pair_order, *cross)
+        pair = lax.all_gather(scatter_sum(partial), "core", axis=0, tiled=False)
+        scratch = (pltpu.VMEM((t, width), HALF),)
+        partial = run_kernel(second_kernel, *sizes, scratch, pivot, pair, *planes)
+        return jnp.stack([first, scatter_sum(partial).astype(HALF)])
+
+    def none_first(pivot, planes):
+        return jnp.zeros((t, half), HALF), jnp.zeros((NC, t, half), HALF)
+
+    def none_second(first, pair, pivot, planes, cross):
+        return jnp.zeros((STEPS, t, half), HALF)
+
+    first, pair = lax.cond(z == 0, first_half, none_first, pivot, planes)
+    solved = lax.cond(
+        z == 0, second_half, none_second, first, pair, pivot, planes, cross
+    )
+
+    solved, panels, row = lax.optimization_barrier((solved, panels, row))
     extra = 128
     pick = jnp.arange(extra)
     at = pick // rows_local * width + row % per_blk * rows_local + pick % rows_local
     wanted = (pick < STEPS * rows_local) & (row // per_blk == blk)
     select = wanted[:, None] & (at[:, None] == jnp.arange(STEPS * width)[None, :])
     select = select.astype(HALF)
-
-    planes = [inverse] + [lax.ppermute(inverse, "z", [(k, 0)]) for k in range(1, NZ)]
-
-    def first_half(pivot, planes):
-        partial = run_kernel(first_kernel, *sizes, (), pivot, *planes)
-        first = scatter_sum(partial).astype(HALF)
-        return first, lax.all_gather(first, "core", axis=0, tiled=False)
-
-    def second_half(first, pair, pivot, planes, cross):
-        partial = run_kernel(cross_kernel, *sizes, (), owner, pair, pair_order, *cross)
-        pair = lax.all_gather(scatter_sum(partial), "core", axis=0, tiled=False)
-        scratch = (pltpu.VMEM((t, width), HALF),)
-        partial = run_kernel(second_kernel, *sizes, scratch, pivot, pair, *planes)
-        return jnp.stack([first, scatter_sum(partial).astype(HALF)])
-
-    def none_first(pivot, planes):
-        return jnp.zeros((t, half), HALF), jnp.zeros((NC, t, half), HALF)
-
-    def none_second(first, pair, pivot, planes, cross):
-        return jnp.zeros((STEPS, t, half), HALF)
-
-    first, pair = lax.cond(z == 0, first_half, none_first, pivot[0], planes)
-    first, panels = lax.optimization_barrier((first, panels))
-    solved = lax.cond(
-        z == 0, second_half, none_second, first, pair, pivot[1], planes, cross
-    )
 
     spread = solved
     for k in range(1, NZ):

time: 175 us -> 180 us (1.029)
  blocking collectives: 70.7 us -> 83.4 us
  waiting for transfers between devices: 30.6 us -> 23.7 us
  local copies, waits for them, and re-layouts: 8.08 us -> 5.18 us
    all_to_all x3 -> x4, blocking collectives: 55.7 us -> 67.5 us  [swap_blocks(): return lax.all_to_all(array, axis, split_axis=0, concat_axis=0, tiled=True)]
    all_to_all x4 -> x3, waiting for transfers between devices: 24.1 us -> 17.4 us  [swap_blocks(): return lax.all_to_all(array, axis, split_axis=0, concat_axis=0, tiled=True)]
    all_to_all x4 -> x3, starting transfers between devices: 14.1 us -> 15.3 us  [swap_blocks(): return lax.all_to_all(array, axis, split_axis=0, concat_axis=0, tiled=True)]
  transfers between devices with their start and end apart: 22 -> 21, of which waited for: 6 -> 6; matrix products, arithmetic and copies ran while one was open for 4% -> 2% of each run, Pallas kernels for 1% -> 2%
where the time goes in v7:
time: 180 us; the launch traced here: 178 us
  blocking collectives  83.4 us (46%)
  starting transfers between devices  51.1 us (28%)
  waiting for transfers between devices  23.7 us (13%)
  Pallas kernels  8.33 us (5%)
  local copies, waits for them, and re-layouts  5.18 us (3%)
  other arithmetic  4.51 us (3%)
    all_to_all x4, blocking collectives, swap_blocks(): return lax.all_to_all(array, axis, split_axis=0, concat_axis=0, tiled=True)  67.5 us
    all_to_all x3, waiting for transfers between devices, swap_blocks(): return lax.all_to_all(array, axis, split_axis=0, concat_axis=0, tiled=True)  17.4 us
    all_to_all x3, starting transfers between devices, swap_blocks(): return lax.all_to_all(array, axis, split_axis=0, concat_axis=0, tiled=True)  15.3 us
    ppermute x1, starting transfers between devices, local(): sent = lax.ppermute(halves[:, 0], ('x', 'z', 'core'), [(1, 0)])  9.54 us
    ppermute x7, starting transfers between devices, local(): received = lax.ppermute(solved, 'z', [(0, k)])  9.16 us
    ppermute x7, starting transfers between devices, local(): planes.append(lax.ppermute(inverse, 'z', [(k, 0)]))  9.04 us
    ppermute x3, starting transfers between devices, local(): lax.ppermute(lower, ('x', 'z'), [(0, k * NZ)])  8.06 us
    pallas_call x3, Pallas kernels, run_kernel(): pl.pallas_call(kernel, in_specs=[pl.BlockSpec(memory_space=space) for spa...  6.62 us
  transfers between devices with their start and end apart: 21, of which 6 were waited for; matrix products, arithmetic and copies ran while one was open for 2% of the time, Pallas kernels for 2%

profile of v7, /device:TPU:1, one launch (start us, length us, event | category | flops | bytes accessed | tf_op | source)
XLA Modules:
  0.0 178.5 jit_solution(10880207782969299522)
XLA Ops:
  0.6 1.9 %copy.21 = bf16[2048,2,256]{2,0,1:T(8,128)(2,1)S(1)} copy(bf16[2048,2,256]{2,1,0:T(2,128)(2,1)} %param.7) | data formatting | bytes 4194304 | tf_op args[0]
  3.4 9.5 %collective-permute-start.7 = (bf16[8,128,256]{2,1,0:T(8,128)(2,1)}, bf16[8,128,256]{2,1,0:T(8,128)(2,1)}, u32[]{:S(2)}, u32[]{:S(2)}) collective-permute-start(bf16[8,128,256]{2,1,0:T(8,128)(2,1)} %slice_bitcast_fusion), channel_id=1, source_target_pairs={{8,0},{9,1},{10,2},{11,3},{12,4},{13,5},{14,6},{15,7}} | collective-permute-start | bytes 1572872 | tf_op jit(solution)/shard_map/ppermute | solution.py:138
  14.7 3.4 %all-to-all-start.3 = ((bf16[4,128,256]{2,1,0:T(8,128)(2,1)}), bf16[4,128,256]{2,1,0:T(8,128)(2,1)S(1)}, u32[]{:S(2)}, u32[]{:S(2)}) async-start(bf16[4,128,256]{2,1,0:T(8,128)(2,1)} %shard_map.50), calls=%async_computation.3 | async-start | bytes 524288 | tf_op jit(solution)/shard_map/all_to_all | solution.py:16
  18.1 5.9 %all-to-all-done.3 = bf16[4,128,256]{2,1,0:T(8,128)(2,1)S(1)} async-done(((bf16[4,128,256]{2,1,0:T(8,128)(2,1)}), bf16[4,128,256]{2,1,0:T(8,128)(2,1)S(1)}, u32[]{:S(2)}, u32[]{:S(2)}) %all-to-all-start.3) | async-done | bytes 262176 | tf_op jit(solution)/shard_map/all_to_all | solution.py:16
  32.0 3.6 %collective-permute-start.10 = (bf16[8,128,256]{2,1,0:T(8,128)(2,1)}, bf16[8,128,256]{2,1,0:T(8,128)(2,1)}, u32[]{:S(2)}, u32[]{:S(2)}) collective-permute-start(bf16[8,128,256]{2,1,0:T(8,128)(2,1)} %fusion.6), channel_id=1, source_target_pairs={{0,384},{1,385},{2,386},{3,387},{4,388},{5,389},{6,390},{7,391},{8... | collective-permute-start | bytes 1572872 | tf_op jit(solution)/shard_map/ppermute | solution.py:141
  35.6 4.8 %collective-permute-done.5 = bf16[4,2,32,256]{3,2,1,0:T(8,128)(2,1)S(1)} collective-permute-done((bf16[4,2,32,256]{3,2,1,0:T(8,128)(2,1)S(1)}, bf16[4,2,32,256]{3,2,1,0:T(8,128)(2,1)S(1)}, u32[]{:S(2)}, u32[]{:S(2)}) %collective-permute-start.5) | collective-permute-done | bytes 131104 | tf_op jit(solution)/shard_map/ppermute | solution.py:160
  40.3 2.1 %collective-permute-start.9 = (bf16[8,128,256]{2,1,0:T(8,128)(2,1)}, bf16[8,128,256]{2,1,0:T(8,128)(2,1)}, u32[]{:S(2)}, u32[]{:S(2)}) collective-permute-start(bf16[8,128,256]{2,1,0:T(8,128)(2,1)} %fusion.6), channel_id=1, source_target_pairs={{0,256},{1,257},{2,258},{3,259},{4,260},{5,261},{6,262},{7,263},{8... | collective-permute-start | bytes 1572872 | tf_op jit(solution)/shard_map/ppermute | solution.py:141
  42.5 2.4 %collective-permute-start.8 = (bf16[8,128,256]{2,1,0:T(8,128)(2,1)}, bf16[8,128,256]{2,1,0:T(8,128)(2,1)}, u32[]{:S(2)}, u32[]{:S(2)}) collective-permute-start(bf16[8,128,256]{2,1,0:T(8,128)(2,1)} %fusion.6), channel_id=1, source_target_pairs={{0,128},{1,129},{2,130},{3,131},{4,132},{5,133},{6,134},{7,135},{8... | collective-permute-start | bytes 1572872 | tf_op jit(solution)/shard_map/ppermute | solution.py:141
  48.2 8.5 %all-to-all-start.4 = ((bf16[8,8,256]{2,1,0:T(8,128)(2,1)}), bf16[8,8,256]{2,1,0:T(8,128)(2,1)S(1)}, u32[]{:S(2)}, u32[]{:S(2)}) async-start(bf16[8,8,256]{2,1,0:T(8,128)(2,1)} %slice_bitcast_fusion.2), calls=%async_computation.4 | async-start | bytes 65536 | tf_op jit(solution)/shard_map/all_to_all | solution.py:16
  56.7 6.9 %all-to-all-done.4 = bf16[8,8,256]{2,1,0:T(8,128)(2,1)S(1)} async-done(((bf16[8,8,256]{2,1,0:T(8,128)(2,1)}), bf16[8,8,256]{2,1,0:T(8,128)(2,1)S(1)}, u32[]{:S(2)}, u32[]{:S(2)}) %all-to-all-start.4) | async-done | bytes 32800 | tf_op jit(solution)/shard_map/all_to_all | solution.py:16
  63.6 4.4 %all_gather.21 = bf16[2,64,256]{2,1,0:T(8,128)(2,1)S(1)} all-gather(bf16[1,64,256]{2,1,0:T(8,128)(2,1)S(1)} %bitcast.69), channel_id=1, replica_groups=mesh['x'=4,'z'=8,'core'=2,'blk'=8] {'core'}, dimensions={0}, use_global_device_ids=true | all-gather | bytes 98304 | tf_op jit(solution)/shard_map/all_gather | solution.py:134
  68.0 17.7 %conditional.2 = (bf16[64,128]{1,0:T(8,128)(2,1)}, bf16[2,64,128]{2,1,0:T(8,128)(2,1)S(1)}) conditional(s32[]{:T(128)} %convert_element_type.31, () %tuple.24, (bf16[2,64,256]{2,1,0:T(8,128)(2,1)S(1)}, bf16[4,2,32,256]{3,2,1,0:T(8,128)(2,1)S(1)}, bf16[4,2,32,256]{3,2,1,0:T(8,128)(2,1)S(1)}, bf16[4,2,32,256]{3,2,1,0:T(8,128)(2,1)S(1)}, ...), branch_computations={%region_0.1_spmd, %region_1.3_spmd} | conditional | flops 57344 | bytes 458770 | solution.py:180
  68.0 2.1 %branch_1_fun.3 = bf16[8,64,128]{2,1,0:T(8,128)(2,1)} custom-call(bf16[2,64,256]{2,1,0:T(8,128)(2,1)S(1)} %get-tuple-element.56.pivot, bf16[4,2,32,256]{3,2,1,0:T(8,128)(2,1)S(1)} %get-tuple-element.57.refs_0_, bf16[4,2,32,256]{3,2,1,0:T(8,128)(2,1)S(1)} %get-tuple-element.58.refs_1_, bf16[4,2,32,256]{3,2,1,0:T(8,128)(2,1)S(1)} %get-tuple-element.59.refs_2_, ...), custom_call_target="tpu_custom_call" | custom-call | tf_op jit(solution)/shard_map/cond/branch_1_fun/pallas_call | solution.py:100
  70.1 11.6 %all_to_all.32 = bf16[8,64,128]{2,1,0:T(8,128)(2,1)S(1)} all-to-all(bf16[8,64,128]{2,1,0:T(8,128)(2,1)} %branch_1_fun.3), channel_id=1, replica_groups=mesh['x'=4,'z'=8,'core'=2,'blk'=8] {'blk'}, dimensions={0} | all-to-all | bytes 262144 | tf_op jit(solution)/shard_map/cond/branch_1_fun/all_to_all | solution.py:16
  82.3 3.3 %all-gather = bf16[128,128]{1,0:T(8,128)(2,1)S(1)} all-gather(bf16[64,128]{1,0:T(8,128)(2,1)} %reduce_sum.38), channel_id=2, replica_groups=mesh['x'=4,'z'=8,'core'=2,'blk'=8] {'core'}, dimensions={0}, use_global_device_ids=true | all-gather | bytes 49152 | tf_op jit(solution)/shard_map/cond/branch_1_fun/all_gather | solution.py:165
  85.7 32.0 %conditional.3 = (bf16[2,64,128]{2,1,0:T(8,128)(2,1)S(1)}) conditional(s32[]{:T(128)} %convert_element_type.31, () %tuple.23, (bf16[64,128]{1,0:T(8,128)(2,1)}, s32[]{:T(128)}, bf16[2,64,128]{2,1,0:T(8,128)(2,1)S(1)}, bf16[2,256,128]{2,1,0:T(8,128)(2,1)S(1)}, bf16[8,128,256]{2,1,0:T(8,128)(2,1)}, /*index=5*/bf16[8,128,256]{2,1,0:T(8,128)(2,1)}, ...), branch_computations={%region_3.4_spmd, %region_4.7_spmd} | conditional | flops 196608 | bytes 3621014 | solution.py:181
  85.7 2.7 %branch_1_fun.4 = bf16[8,64,128]{2,1,0:T(8,128)(2,1)} custom-call(s32[1]{0:T(128)} %bitcast.2.owner, bf16[2,64,128]{2,1,0:T(8,128)(2,1)S(1)} %get-tuple-element.68.pair, bf16[2,256,128]{2,1,0:T(8,128)(2,1)S(1)} %get-tuple-element.69.order, bf16[8,128,256]{2,1,0:T(8,128)(2,1)} %get-tuple-element.70.own, bf16[8,128,256]{2,1,0:T(8,128)(2,1)} %get-tuple-element.71.refs_0_, ...), custom_call_target="tpu_custom_call" | custom-call | tf_op jit(solution)/shard_map/cond/branch_1_fun/pallas_call | solution.py:100
  88.5 11.6 %all_to_all.33 = bf16[8,64,128]{2,1,0:T(8,128)(2,1)S(1)} all-to-all(bf16[8,64,128]{2,1,0:T(8,128)(2,1)} %branch_1_fun.4), channel_id=1, replica_groups=mesh['x'=4,'z'=8,'core'=2,'blk'=8] {'blk'}, dimensions={0} | all-to-all | bytes 262144 | tf_op jit(solution)/shard_map/cond/branch_1_fun/all_to_all | solution.py:16
  100.1 3.3 %all-gather.1 = f32[128,128]{1,0:T(8,128)} all-gather(f32[64,128]{1,0:T(8,128)S(1)} %convert_reduce_fusion), channel_id=3, replica_groups=mesh['x'=4,'z'=8,'core'=2,'blk'=8] {'core'}, dimensions={0}, use_global_device_ids=true | all-gather | bytes 98304 | tf_op jit(solution)/shard_map/cond/branch_1_fun/all_gather | solution.py:169
  105.2 11.7 %all_to_all.34 = bf16[8,64,128]{2,1,0:T(8,128)(2,1)S(1)} all-to-all(bf16[8,64,128]{2,1,0:T(8,128)(2,1)} %branch_1_fun.5), channel_id=1, replica_groups=mesh['x'=4,'z'=8,'core'=2,'blk'=8] {'blk'}, dimensions={0} | all-to-all | bytes 262144 | tf_op jit(solution)/shard_map/cond/branch_1_fun/all_to_all | solution.py:16
  129.7 3.3 %all-to-all-start.5 = ((bf16[4,2,64,128]{3,2,1,0:T(8,128)(2,1)}), bf16[4,2,64,128]{3,2,1,0:T(8,128)(2,1)S(1)}, u32[]{:S(2)}, u32[]{:S(2)}) async-start(bf16[4,2,64,128]{3,2,1,0:T(8,128)(2,1)} %broadcast_in_dim.6), calls=%async_computation.5 | async-start | bytes 262144 | tf_op jit(solution)/shard_map/all_to_all | solution.py:16
  133.2 4.7 %all-to-all-done.5 = bf16[4,2,64,128]{3,2,1,0:T(8,128)(2,1)S(1)} async-done(((bf16[4,2,64,128]{3,2,1,0:T(8,128)(2,1)}), bf16[4,2,64,128]{3,2,1,0:T(8,128)(2,1)S(1)}, u32[]{:S(2)}, u32[]{:S(2)}) %all-to-all-start.5) | async-done | bytes 131104 | tf_op jit(solution)/shard_map/all_to_all | solution.py:16
  137.9 5.0 %all-gather.2 = bf16[8,2,64,128]{3,2,1,0:T(8,128)(2,1)S(1)} all-gather(bf16[4,2,64,128]{3,2,1,0:T(8,128)(2,1)S(1)} %all-to-all-done.5), channel_id=4, replica_groups=mesh['x'=4,'z'=8,'core'=2,'blk'=8] {'core'}, dimensions={0}, use_global_device_ids=true | all-gather | bytes 393216 | tf_op jit(solution)/shard_map/all_gather | solution.py:155
  144.3 32.6 %all_to_all.35 = bf16[8,544,128]{2,1,0:T(8,128)(2,1)S(1)} all-to-all(bf16[8,544,128]{2,1,0:T(8,128)(2,1)S(1)} %bitcast.65), channel_id=1, replica_groups=mesh['x'=4,'z'=8,'core'=2,'blk'=8] {'blk'}, dimensions={0} | all-to-all | bytes 2228224 | tf_op jit(solution)/shard_map/all_to_all | solution.py:16
  (85 shorter events, 32.2 us)
Async XLA Ops:
  3.4 25.8 %collective-permute-start.7 = (bf16[8,128,256]{2,1,0:T(8,128)(2,1)}, bf16[8,128,256]{2,1,0:T(8,128)(2,1)}, u32[]{:S(2)}, u32[]{:S(2)}) collective-permute-start(bf16[8,128,256]{2,1,0:T(8,128)(2,1)} %slice_bitcast_fusion), channel_id=1, source_target_pairs={{8,0},{9,1},{10,2},{11,3},{12,4},{13,5},{14,6},{15,7}} | collective-permute-start | bytes 1572872 | tf_op jit(solution)/shard_map/ppermute | solution.py:138
  14.7 9.4 %all-to-all-start.3 = ((bf16[4,128,256]{2,1,0:T(8,128)(2,1)}), bf16[4,128,256]{2,1,0:T(8,128)(2,1)S(1)}, u32[]{:S(2)}, u32[]{:S(2)}) async-start(bf16[4,128,256]{2,1,0:T(8,128)(2,1)} %shard_map.50), calls=%async_computation.3 | async-start | bytes 524288 | tf_op jit(solution)/shard_map/all_to_all | solution.py:16
  24.1 7.9 %collective-permute-start.6 = (bf16[4,2,32,256]{3,2,1,0:T(8,128)(2,1)S(1)}, bf16[4,2,32,256]{3,2,1,0:T(8,128)(2,1)S(1)}, u32[]{:S(2)}, u32[]{:S(2)}) collective-permute-start(bf16[4,2,32,256]{3,2,1,0:T(8,128)(2,1)S(1)} %bitcast.54), channel_id=1, source_target_pairs={{112,0},{113,1},{114,2},{115,3},{116,4},{117,5},{118,6},{119,7},{1... | collective-permute-start | bytes 393224 | tf_op jit(solution)/shard_map/ppermute | solution.py:160
  25.4 15.0 %collective-permute-start.5 = (bf16[4,2,32,256]{3,2,1,0:T(8,128)(2,1)S(1)}, bf16[4,2,32,256]{3,2,1,0:T(8,128)(2,1)S(1)}, u32[]{:S(2)}, u32[]{:S(2)}) collective-permute-start(bf16[4,2,32,256]{3,2,1,0:T(8,128)(2,1)S(1)} %bitcast.55), channel_id=1, source_target_pairs={{96,0},{97,1},{98,2},{99,3},{100,4},{101,5},{102,6},{103,7},{104,8... | collective-permute-start | bytes 393224 | tf_op jit(solution)/shard_map/ppermute | solution.py:160
  26.7 15.8 %collective-permute-start.4 = (bf16[4,2,32,256]{3,2,1,0:T(8,128)(2,1)S(1)}, bf16[4,2,32,256]{3,2,1,0:T(8,128)(2,1)S(1)}, u32[]{:S(2)}, u32[]{:S(2)}) collective-permute-start(bf16[4,2,32,256]{3,2,1,0:T(8,128)(2,1)S(1)} %bitcast.56), channel_id=1, source_target_pairs={{80,0},{81,1},{82,2},{83,3},{84,4},{85,5},{86,6},{87,7},{88,8},{89... | collective-permute-start | bytes 393224 | tf_op jit(solution)/shard_map/ppermute | solution.py:160
  28.0 16.9 %collective-permute-start.3 = (bf16[4,2,32,256]{3,2,1,0:T(8,128)(2,1)S(1)}, bf16[4,2,32,256]{3,2,1,0:T(8,128)(2,1)S(1)}, u32[]{:S(2)}, u32[]{:S(2)}) collective-permute-start(bf16[4,2,32,256]{3,2,1,0:T(8,128)(2,1)S(1)} %bitcast.57), channel_id=1, source_target_pairs={{64,0},{65,1},{66,2},{67,3},{68,4},{69,5},{70,6},{71,7},{72,8},{73... | collective-permute-start | bytes 393224 | tf_op jit(solution)/shard_map/ppermute | solution.py:160
  29.3 16.9 %collective-permute-start.2 = (bf16[4,2,32,256]{3,2,1,0:T(8,128)(2,1)S(1)}, bf16[4,2,32,256]{3,2,1,0:T(8,128)(2,1)S(1)}, u32[]{:S(2)}, u32[]{:S(2)}) collective-permute-start(bf16[4,2,32,256]{3,2,1,0:T(8,128)(2,1)S(1)} %bitcast.58), channel_id=1, source_target_pairs={{48,0},{49,1},{50,2},{51,3},{52,4},{53,5},{54,6},{55,7},{56,8},{57... | collective-permute-start | bytes 393224 | tf_op jit(solution)/shard_map/ppermute | solution.py:160
  32.0 53.7 %collective-permute-start.10 = (bf16[8,128,256]{2,1,0:T(8,128)(2,1)}, bf16[8,128,256]{2,1,0:T(8,128)(2,1)}, u32[]{:S(2)}, u32[]{:S(2)}) collective-permute-start(bf16[8,128,256]{2,1,0:T(8,128)(2,1)} %fusion.6), channel_id=1, source_target_pairs={{0,384},{1,385},{2,386},{3,387},{4,388},{5,389},{6,390},{7,391},{8... | collective-permute-start | bytes 1572872 | tf_op jit(solution)/shard_map/ppermute | solution.py:141
  40.3 45.3 %collective-permute-start.9 = (bf16[8,128,256]{2,1,0:T(8,128)(2,1)}, bf16[8,128,256]{2,1,0:T(8,128)(2,1)}, u32[]{:S(2)}, u32[]{:S(2)}) collective-permute-start(bf16[8,128,256]{2,1,0:T(8,128)(2,1)} %fusion.6), channel_id=1, source_target_pairs={{0,256},{1,257},{2,258},{3,259},{4,260},{5,261},{6,262},{7,263},{8... | collective-permute-start | bytes 1572872 | tf_op jit(solution)/shard_map/ppermute | solution.py:141
  42.5 43.2 %collective-permute-start.8 = (bf16[8,128,256]{2,1,0:T(8,128)(2,1)}, bf16[8,128,256]{2,1,0:T(8,128)(2,1)}, u32[]{:S(2)}, u32[]{:S(2)}) collective-permute-start(bf16[8,128,256]{2,1,0:T(8,128)(2,1)} %fusion.6), channel_id=1, source_target_pairs={{0,128},{1,129},{2,130},{3,131},{4,132},{5,133},{6,134},{7,135},{8... | collective-permute-start | bytes 1572872 | tf_op jit(solution)/shard_map/ppermute | solution.py:141
  44.9 23.1 %collective-permute-start.1 = (bf16[4,2,32,256]{3,2,1,0:T(8,128)(2,1)S(1)}, bf16[4,2,32,256]{3,2,1,0:T(8,128)(2,1)S(1)}, u32[]{:S(2)}, u32[]{:S(2)}) collective-permute-start(bf16[4,2,32,256]{3,2,1,0:T(8,128)(2,1)S(1)} %bitcast.59), channel_id=1, source_target_pairs={{32,0},{33,1},{34,2},{35,3},{36,4},{37,5},{38,6},{39,7},{40,8},{41... | collective-permute-start | bytes 393224 | tf_op jit(solution)/shard_map/ppermute | solution.py:160
  46.2 21.7 %collective-permute-start = (bf16[4,2,32,256]{3,2,1,0:T(8,128)(2,1)S(1)}, bf16[4,2,32,256]{3,2,1,0:T(8,128)(2,1)S(1)}, u32[]{:S(2)}, u32[]{:S(2)}) collective-permute-start(bf16[4,2,32,256]{3,2,1,0:T(8,128)(2,1)S(1)} %bitcast.60), channel_id=1, source_target_pairs={{16,0},{17,1},{18,2},{19,3},{20,4},{21,5},{22,6},{23,7},{24,8},{25... | collective-permute-start | bytes 393224 | tf_op jit(solution)/shard_map/ppermute | solution.py:160
  48.2 15.4 %all-to-all-start.4 = ((bf16[8,8,256]{2,1,0:T(8,128)(2,1)}), bf16[8,8,256]{2,1,0:T(8,128)(2,1)S(1)}, u32[]{:S(2)}, u32[]{:S(2)}) async-start(bf16[8,8,256]{2,1,0:T(8,128)(2,1)} %slice_bitcast_fusion.2), calls=%async_computation.4 | async-start | bytes 65536 | tf_op jit(solution)/shard_map/all_to_all | solution.py:16
  85.7 17.7 %copy-start.3 = (bf16[4,2,32,256]{3,2,1,0:T(8,128)(2,1)S(1)}, bf16[4,2,32,256]{3,2,1,0:T(8,128)(2,1)}, u32[]{:S(2)}) copy-start(bf16[4,2,32,256]{3,2,1,0:T(8,128)(2,1)} %get-tuple-element.81.refs_7_) | copy-start | bytes 393220 | tf_op jit(solution)/shard_map/cond
  117.6 7.6 %collective-permute-start.17 = (bf16[2,64,128]{2,1,0:T(8,128)(2,1)S(1)}, bf16[2,64,128]{2,1,0:T(8,128)(2,1)S(1)}, u32[]{:S(2)}, u32[]{:S(2)}) collective-permute-start(bf16[2,64,128]{2,1,0:T(8,128)(2,1)S(1)} %get-tuple-element.102), channel_id=1, source_target_pairs={{0,112},{1,113},{2,114},{3,115},{4,116},{5,117},{6,118},{7,119},{8... | collective-permute-start | bytes 98312 | tf_op jit(solution)/shard_map/ppermute | solution.py:195
  118.9 7.8 %collective-permute-start.16 = (bf16[2,64,128]{2,1,0:T(8,128)(2,1)S(1)}, bf16[2,64,128]{2,1,0:T(8,128)(2,1)S(1)}, u32[]{:S(2)}, u32[]{:S(2)}) collective-permute-start(bf16[2,64,128]{2,1,0:T(8,128)(2,1)S(1)} %get-tuple-element.102), channel_id=1, source_target_pairs={{0,96},{1,97},{2,98},{3,99},{4,100},{5,101},{6,102},{7,103},{8,104... | collective-permute-start | bytes 98312 | tf_op jit(solution)/shard_map/ppermute | solution.py:195
  120.2 7.8 %collective-permute-start.15 = (bf16[2,64,128]{2,1,0:T(8,128)(2,1)S(1)}, bf16[2,64,128]{2,1,0:T(8,128)(2,1)S(1)}, u32[]{:S(2)}, u32[]{:S(2)}) collective-permute-start(bf16[2,64,128]{2,1,0:T(8,128)(2,1)S(1)} %get-tuple-element.102), channel_id=1, source_target_pairs={{0,80},{1,81},{2,82},{3,83},{4,84},{5,85},{6,86},{7,87},{8,88},{9,... | collective-permute-start | bytes 98312 | tf_op jit(solution)/shard_map/ppermute | solution.py:195
  121.5 6.5 %collective-permute-start.14 = (bf16[2,64,128]{2,1,0:T(8,128)(2,1)S(1)}, bf16[2,64,128]{2,1,0:T(8,128)(2,1)S(1)}, u32[]{:S(2)}, u32[]{:S(2)}) collective-permute-start(bf16[2,64,128]{2,1,0:T(8,128)(2,1)S(1)} %get-tuple-element.102), channel_id=1, source_target_pairs={{0,64},{1,65},{2,66},{3,67},{4,68},{5,69},{6,70},{7,71},{8,72},{9,... | collective-permute-start | bytes 98312 | tf_op jit(solution)/shard_map/ppermute | solution.py:195
  122.8 5.2 %collective-permute-start.13 = (bf16[2,64,128]{2,1,0:T(8,128)(2,1)S(1)}, bf16[2,64,128]{2,1,0:T(8,128)(2,1)S(1)}, u32[]{:S(2)}, u32[]{:S(2)}) collective-permute-start(bf16[2,64,128]{2,1,0:T(8,128)(2,1)S(1)} %get-tuple-element.102), channel_id=1, source_target_pairs={{0,48},{1,49},{2,50},{3,51},{4,52},{5,53},{6,54},{7,55},{8,56},{9,... | collective-permute-start | bytes 98312 | tf_op jit(solution)/shard_map/ppermute | solution.py:195
  125.3 18.2 %copy-start = (bf16[2048,256]{1,0:T(8,128)(2,1)S(1)}, bf16[2048,256]{1,0:T(8,128)(2,1)}, u32[]{:S(2)}) copy-start(bf16[2048,256]{1,0:T(8,128)(2,1)} %get-tuple-element.95) | copy-start | bytes 3145732
  125.3 2.8 %collective-permute-start.12 = (bf16[2,64,128]{2,1,0:T(8,128)(2,1)S(1)}, bf16[2,64,128]{2,1,0:T(8,128)(2,1)S(1)}, u32[]{:S(2)}, u32[]{:S(2)}) collective-permute-start(bf16[2,64,128]{2,1,0:T(8,128)(2,1)S(1)} %get-tuple-element.102), channel_id=1, source_target_pairs={{0,32},{1,33},{2,34},{3,35},{4,36},{5,37},{6,38},{7,39},{8,40},{9,... | collective-permute-start | bytes 98312 | tf_op jit(solution)/shard_map/ppermute | solution.py:195
  126.7 2.3 %collective-permute-start.11 = (bf16[2,64,128]{2,1,0:T(8,128)(2,1)S(1)}, bf16[2,64,128]{2,1,0:T(8,128)(2,1)S(1)}, u32[]{:S(2)}, u32[]{:S(2)}) collective-permute-start(bf16[2,64,128]{2,1,0:T(8,128)(2,1)S(1)} %get-tuple-element.102), channel_id=1, source_target_pairs={{0,16},{1,17},{2,18},{3,19},{4,20},{5,21},{6,22},{7,23},{8,24},{9,... | collective-permute-start | bytes 98312 | tf_op jit(solution)/shard_map/ppermute | solution.py:195
  129.7 8.1 %all-to-all-start.5 = ((bf16[4,2,64,128]{3,2,1,0:T(8,128)(2,1)}), bf16[4,2,64,128]{3,2,1,0:T(8,128)(2,1)S(1)}, u32[]{:S(2)}, u32[]{:S(2)}) async-start(bf16[4,2,64,128]{3,2,1,0:T(8,128)(2,1)} %broadcast_in_dim.6), calls=%async_computation.5 | async-start | bytes 262144 | tf_op jit(solution)/shard_map/all_to_all | solution.py:16
  144.3 32.7 %copy-start.1 = (f32[32,2048]{1,0:T(8,128)S(1)}, f32[32,2048]{1,0:T(8,128)}, u32[]{:S(2)}) copy-start(f32[32,2048]{1,0:T(8,128)} %pivot.1) | copy-start | bytes 786436
  (9 other events, 101.3 us)

commit v8 on v7

--- a/solution.py
+++ b/solution.py
@@ -1,3 +1,5 @@
+import functools
+
 import jax
 import jax.numpy as jnp
 from jax import lax
@@ -62,12 +64,16 @@
     write_blocks(pivot[0], whole, out)
 
 
-def cross_kernel(owner, pair, order, own, *refs):
+def cross_kernel(rows_local, owner, pair, own, *refs):
     others, (out, whole) = refs[: NX - 1], refs[NX - 1 :]
-    value = product(pair[0], order[0])
-    for c in range(1, NC):
-        value = value + product(pair[c], order[c])
-    blocks, size, _ = own.shape
+    blocks, size, width = own.shape
+    column = lax.broadcasted_iota(jnp.int32, (width, size), 0)
+    place = lax.broadcasted_iota(jnp.int32, (width, size), 1)
+    natural = place + place // rows_local * (rows_local * (NC - 1))
+    value = jnp.zeros((pair.shape[1], width), WIDE)
+    for c in range(NC):
+        order = jnp.where(column == natural + c * rows_local, 1.0, 0.0).astype(HALF)
+        value = value + product(pair[c], order)
 
     @pl.when(owner[0] == 1)
     def _():
@@ -95,6 +101,24 @@
     write_blocks(value[...], whole, out)
 
 
+def finish_kernel(parts, right, answer, reduced):
+    lanes, rows8 = 128, 8
+    pixels = right.shape[1] // lanes
+    steps, dates, columns = answer.shape
+    deep = parts.shape[1] * rows8 // dates
+    for q in range(dates // rows8):
+        at = slice(q * rows8, (q + 1) * rows8)
+        total = parts[0, q * deep : (q + 1) * deep, :].astype(WIDE)
+        for b in range(1, parts.shape[0]):
+            total = total + parts[b, q * deep : (q + 1) * deep, :].astype(WIDE)
+        for l in range(pixels):
+            lane = slice(l * lanes, (l + 1) * lanes)
+            reduced[at, lane] = right[at, lane] - total[l * rows8 : (l + 1) * rows8, :]
+        last = total[pixels * rows8 : (pixels + 1) * rows8, :]
+        for k in range(steps):
+            answer[k, at, :] = last[:, k * columns : (k + 1) * columns]
+
+
 def run_kernel(kernel, blocks, t, size, width, scratch, *operands):
     spaces = [pltpu.SMEM if item.dtype == jnp.int32 else pltpu.VMEM for item in operands]
     return pl.pallas_call(
@@ -112,7 +136,7 @@
     blk = lax.axis_index("blk")
     row = (x * NZ + z) * NC + core
     n_blk = right_side.shape[1] // factor_panel.shape[2]
-    pixels, _, width = factor_panel.shape
+    _, _, width = factor_panel.shape
     dates_local = right_side.shape[0]
     dates_x = dates_local // NX
     t = dates_x * n_blk
@@ -144,7 +168,6 @@
     c_of, q_of, i_of = place // half, place % half // rows_local, place % rows_local
     natural = (q_of * NC + c_of) * rows_local + i_of
     order = (natural[:, None] == place[None, :]).astype(HALF)
-    pair_order = order.reshape(NC, half, width).transpose(0, 2, 1)
     sizes = (n_blk, t, half, width)
 
 
@@ -165,7 +188,8 @@
         return first, lax.all_gather(first, "core", axis=0, tiled=False)
 
     def second_half(first, pair, pivot, planes, cross):
-        partial = run_kernel(cross_kernel, *sizes, (), owner, pair, pair_order, *cross)
+        kernel = functools.partial(cross_kernel, rows_local)
+        partial = run_kernel(kernel, *sizes, (), owner, pair, *cross)
         pair = lax.all_gather(scatter_sum(partial), "core", axis=0, tiled=False)
         scratch = (pltpu.VMEM((t, width), HALF),)
         partial = run_kernel(second_kernel, *sizes, scratch, pivot, pair, *planes)
@@ -211,12 +235,13 @@
     lanes, rows8 = 128, 8
     total = total.reshape(n_blk * dates_local // rows8, rows8, -1, lanes).transpose(0, 2, 1, 3)
     total = swap_blocks(total.reshape(n_blk, -1, lanes), "blk")
-    total = jnp.sum(total.astype(WIDE), axis=0)
-    total = total.reshape(dates_local // rows8, -1, rows8, lanes).transpose(0, 2, 1, 3)
-    total = total.reshape(dates_local, pixels + extra)
-    answer = total[:, pixels : pixels + STEPS * rows_local]
-    answer = answer.reshape(dates_local, STEPS, rows_local).transpose(1, 0, 2)
-    return (answer, right_side - total[:, :pixels])
+    return pl.pallas_call(
+        finish_kernel,
+        out_shape=(
+            jax.ShapeDtypeStruct((STEPS, dates_local, rows_local), WIDE),
+            jax.ShapeDtypeStruct(right_side.shape, WIDE),
+        ),
+    )(total, right_side)
 
 
 def solution(mesh):

time: 180 us -> 184 us (1.022)
  waiting for transfers between devices: 23.7 us -> 27.3 us
  blocking collectives: 83.4 us -> 85.8 us
  Pallas kernels: 8.33 us -> 10.4 us
  starting transfers between devices: 51.1 us -> 49.1 us
    ppermute x7, waiting for transfers between devices: 5.31 us -> 8.79 us  [local(): planes.append(lax.ppermute(inverse, 'z', [(k, 0)]))]
    pallas_call x0 -> x1, Pallas kernels: none -> 2.13 us  [local(): pl.pallas_call(finish_kernel, out_shape=(jax.ShapeDtypeStruct((STEPS, dat...]
where the time goes in v8:
time: 184 us; the launch traced here: 183 us
  blocking collectives  85.8 us (47%)
  starting transfers between devices  49.1 us (27%)
  waiting for transfers between devices  27.3 us (15%)
  Pallas kernels  10.4 us (6%)
  local copies, waits for them, and re-layouts  4.4 us (2%)
  other arithmetic  3.57 us (2%)
    all_to_all x4, blocking collectives, swap_blocks(): return lax.all_to_all(array, axis, split_axis=0, concat_axis=0, tiled=True)  68.1 us
    all_to_all x3, waiting for transfers between devices, swap_blocks(): return lax.all_to_all(array, axis, split_axis=0, concat_axis=0, tiled=True)  17.5 us
    all_to_all x3, starting transfers between devices, swap_blocks(): return lax.all_to_all(array, axis, split_axis=0, concat_axis=0, tiled=True)  14.4 us
    ppermute x1, starting transfers between devices, local(): sent = lax.ppermute(halves[:, 0], ('x', 'z', 'core'), [(1, 0)])  9.54 us
    ppermute x7, starting transfers between devices, local(): received = lax.ppermute(solved, 'z', [(0, k)])  9.16 us
    ppermute x7, starting transfers between devices, local(): planes.append(lax.ppermute(inverse, 'z', [(k, 0)]))  9.02 us
    ppermute x7, waiting for transfers between devices, local(): planes.append(lax.ppermute(inverse, 'z', [(k, 0)]))  8.79 us
    ppermute x3, starting transfers between devices, local(): lax.ppermute(lower, ('x', 'z'), [(0, k * NZ)])  6.99 us
  transfers between devices with their start and end apart: 21, of which 6 were waited for; matrix products, arithmetic and copies ran while one was open for 2% of the time, Pallas kernels for 2%

profile of v8, /device:TPU:1, one launch (start us, length us, event | category | flops | bytes accessed | tf_op | source)
XLA Modules:
  0.0 182.6 jit_solution(2493040498603220844)
XLA Ops:
  3.4 9.5 %collective-permute-start.7 = (bf16[8,128,256]{2,1,0:T(8,128)(2,1)}, bf16[8,128,256]{2,1,0:T(8,128)(2,1)}, u32[]{:S(2)}, u32[]{:S(2)}) collective-permute-start(bf16[8,128,256]{2,1,0:T(8,128)(2,1)} %slice_bitcast_fusion), channel_id=1, source_target_pairs={{8,0},{9,1},{10,2},{11,3},{12,4},{13,5},{14,6},{15,7}} | collective-permute-start | bytes 1572872 | tf_op jit(solution)/shard_map/ppermute | solution.py:162
  14.7 3.4 %all-to-all-start.3 = ((bf16[4,128,256]{2,1,0:T(8,128)(2,1)}), bf16[4,128,256]{2,1,0:T(8,128)(2,1)S(1)}, u32[]{:S(2)}, u32[]{:S(2)}) async-start(bf16[4,128,256]{2,1,0:T(8,128)(2,1)} %shard_map.50), calls=%async_computation.3 | async-start | bytes 524288 | tf_op jit(solution)/shard_map/all_to_all | solution.py:18
  18.1 5.9 %all-to-all-done.3 = bf16[4,128,256]{2,1,0:T(8,128)(2,1)S(1)} async-done(((bf16[4,128,256]{2,1,0:T(8,128)(2,1)}), bf16[4,128,256]{2,1,0:T(8,128)(2,1)S(1)}, u32[]{:S(2)}, u32[]{:S(2)}) %all-to-all-start.3) | async-done | bytes 262176 | tf_op jit(solution)/shard_map/all_to_all | solution.py:18
  28.8 2.8 %collective-permute-start.10 = (bf16[8,128,256]{2,1,0:T(8,128)(2,1)}, bf16[8,128,256]{2,1,0:T(8,128)(2,1)S(1)}, u32[]{:S(2)}, u32[]{:S(2)}) collective-permute-start(bf16[8,128,256]{2,1,0:T(8,128)(2,1)} %fusion.6), channel_id=1, source_target_pairs={{0,384},{1,385},{2,386},{3,387},{4,388},{5,389},{6,390},{7,391},{8... | collective-permute-start | bytes 1572872 | tf_op jit(solution)/shard_map/ppermute | solution.py:165
  31.6 2.1 %collective-permute-start.9 = (bf16[8,128,256]{2,1,0:T(8,128)(2,1)}, bf16[8,128,256]{2,1,0:T(8,128)(2,1)}, u32[]{:S(2)}, u32[]{:S(2)}) collective-permute-start(bf16[8,128,256]{2,1,0:T(8,128)(2,1)} %fusion.6), channel_id=1, source_target_pairs={{0,256},{1,257},{2,258},{3,259},{4,260},{5,261},{6,262},{7,263},{8... | collective-permute-start | bytes 1572872 | tf_op jit(solution)/shard_map/ppermute | solution.py:165
  33.7 2.1 %collective-permute-start.8 = (bf16[8,128,256]{2,1,0:T(8,128)(2,1)}, bf16[8,128,256]{2,1,0:T(8,128)(2,1)}, u32[]{:S(2)}, u32[]{:S(2)}) collective-permute-start(bf16[8,128,256]{2,1,0:T(8,128)(2,1)} %fusion.6), channel_id=1, source_target_pairs={{0,128},{1,129},{2,130},{3,131},{4,132},{5,133},{6,134},{7,135},{8... | collective-permute-start | bytes 1572872 | tf_op jit(solution)/shard_map/ppermute | solution.py:165
  40.2 7.0 %collective-permute-done.3 = bf16[4,2,32,256]{3,2,1,0:T(8,128)(2,1)S(1)} collective-permute-done((bf16[4,2,32,256]{3,2,1,0:T(8,128)(2,1)S(1)}, bf16[4,2,32,256]{3,2,1,0:T(8,128)(2,1)S(1)}, u32[]{:S(2)}, u32[]{:S(2)}) %collective-permute-start.3) | collective-permute-done | bytes 131104 | tf_op jit(solution)/shard_map/ppermute | solution.py:183
  50.4 7.6 %all-to-all-start.4 = ((bf16[8,8,256]{2,1,0:T(8,128)(2,1)}), bf16[8,8,256]{2,1,0:T(8,128)(2,1)S(1)}, u32[]{:S(2)}, u32[]{:S(2)}) async-start(bf16[8,8,256]{2,1,0:T(8,128)(2,1)} %slice_bitcast_fusion.2), calls=%async_computation.4 | async-start | bytes 65536 | tf_op jit(solution)/shard_map/all_to_all | solution.py:18
  58.1 6.9 %all-to-all-done.4 = bf16[8,8,256]{2,1,0:T(8,128)(2,1)S(1)} async-done(((bf16[8,8,256]{2,1,0:T(8,128)(2,1)}), bf16[8,8,256]{2,1,0:T(8,128)(2,1)S(1)}, u32[]{:S(2)}, u32[]{:S(2)}) %all-to-all-start.4) | async-done | bytes 32800 | tf_op jit(solution)/shard_map/all_to_all | solution.py:18
  65.0 6.1 %all_gather.21 = bf16[2,64,256]{2,1,0:T(8,128)(2,1)S(1)} all-gather(bf16[1,64,256]{2,1,0:T(8,128)(2,1)S(1)} %bitcast.60), channel_id=1, replica_groups=mesh['x'=4,'z'=8,'core'=2,'blk'=8] {'core'}, dimensions={0}, use_global_device_ids=true | all-gather | bytes 98304 | tf_op jit(solution)/shard_map/all_gather | solution.py:158
  71.1 17.6 %conditional.2 = (bf16[64,128]{1,0:T(8,128)(2,1)}, bf16[2,64,128]{2,1,0:T(8,128)(2,1)S(1)}) conditional(s32[]{:T(128)} %convert_element_type.24, () %tuple.23, (bf16[2,64,256]{2,1,0:T(8,128)(2,1)S(1)}, bf16[4,2,32,256]{3,2,1,0:T(8,128)(2,1)S(1)}, bf16[4,2,32,256]{3,2,1,0:T(8,128)(2,1)}, bf16[4,2,32,256]{3,2,1,0:T(8,128)(2,1)S(1)}, ...), branch_computations={%region_0.1_spmd, %region_1.3_spmd} | conditional | flops 57344 | bytes 458770 | solution.py:204
  73.1 11.6 %all_to_all.32 = bf16[8,64,128]{2,1,0:T(8,128)(2,1)S(1)} all-to-all(bf16[8,64,128]{2,1,0:T(8,128)(2,1)} %branch_1_fun.3), channel_id=1, replica_groups=mesh['x'=4,'z'=8,'core'=2,'blk'=8] {'blk'}, dimensions={0} | all-to-all | bytes 262144 | tf_op jit(solution)/shard_map/cond/branch_1_fun/all_to_all | solution.py:18
  85.4 3.3 %all-gather = bf16[128,128]{1,0:T(8,128)(2,1)S(1)} all-gather(bf16[64,128]{1,0:T(8,128)(2,1)} %reduce_sum.30), channel_id=2, replica_groups=mesh['x'=4,'z'=8,'core'=2,'blk'=8] {'core'}, dimensions={0}, use_global_device_ids=true | all-gather | bytes 49152 | tf_op jit(solution)/shard_map/cond/branch_1_fun/all_gather | solution.py:188
  88.7 31.9 %conditional.3 = (bf16[2,64,128]{2,1,0:T(8,128)(2,1)S(1)}) conditional(s32[]{:T(128)} %convert_element_type.24, () %tuple.22, (bf16[64,128]{1,0:T(8,128)(2,1)}, s32[]{:T(128)}, bf16[2,64,128]{2,1,0:T(8,128)(2,1)S(1)}, bf16[8,128,256]{2,1,0:T(8,128)(2,1)}, bf16[8,128,256]{2,1,0:T(8,128)(2,1)}, /*index=5*/bf16[8,128,256]{2,1,0:T(8,128)(2,1)}, ...), branch_computations={%region_3.4_spmd, %region_4.7_spmd} | conditional | flops 196608 | bytes 999434 | solution.py:205
  88.8 2.5 %branch_1_fun.4 = bf16[8,64,128]{2,1,0:T(8,128)(2,1)} custom-call(s32[1]{0:T(128)} %bitcast.2.owner, bf16[2,64,128]{2,1,0:T(8,128)(2,1)S(1)} %get-tuple-element.66.pair, bf16[8,128,256]{2,1,0:T(8,128)(2,1)} %get-tuple-element.67.own, bf16[8,128,256]{2,1,0:T(8,128)(2,1)} %get-tuple-element.68.refs_0_, bf16[8,128,256]{2,1,0:T(8,128)(2,1)} %get-tuple-element.69.refs_1_, ...), custom_call_target="tpu_custom_call" | custom-call | tf_op jit(solution)/shard_map/cond/branch_1_fun/pallas_call | solution.py:124
  91.3 11.7 %all_to_all.33 = bf16[8,64,128]{2,1,0:T(8,128)(2,1)S(1)} all-to-all(bf16[8,64,128]{2,1,0:T(8,128)(2,1)} %branch_1_fun.4), channel_id=1, replica_groups=mesh['x'=4,'z'=8,'core'=2,'blk'=8] {'blk'}, dimensions={0} | all-to-all | bytes 262144 | tf_op jit(solution)/shard_map/cond/branch_1_fun/all_to_all | solution.py:18
  102.9 3.3 %all-gather.1 = f32[128,128]{1,0:T(8,128)} all-gather(f32[64,128]{1,0:T(8,128)S(1)} %convert_reduce_fusion), channel_id=3, replica_groups=mesh['x'=4,'z'=8,'core'=2,'blk'=8] {'core'}, dimensions={0}, use_global_device_ids=true | all-gather | bytes 98304 | tf_op jit(solution)/shard_map/cond/branch_1_fun/all_gather | solution.py:193
  106.2 2.1 %branch_1_fun.5 = bf16[8,64,128]{2,1,0:T(8,128)(2,1)} custom-call(bf16[2,64,256]{2,1,0:T(8,128)(2,1)S(1)} %get-tuple-element.64.pivot, f32[2,64,128]{2,1,0:T(8,128)} %bitcast.57, bf16[4,2,32,256]{3,2,1,0:T(8,128)(2,1)S(1)} %get-tuple-element.71.refs_0_, bf16[4,2,32,256]{3,2,1,0:T(8,128)(2,1)} %get-tuple-element.72.refs_1_, ...), custom_call_target="tpu_custom_call" | custom-call | tf_op jit(solution)/shard_map/cond/branch_1_fun/pallas_call | solution.py:124
  108.3 11.7 %all_to_all.34 = bf16[8,64,128]{2,1,0:T(8,128)(2,1)S(1)} all-to-all(bf16[8,64,128]{2,1,0:T(8,128)(2,1)} %branch_1_fun.5), channel_id=1, replica_groups=mesh['x'=4,'z'=8,'core'=2,'blk'=8] {'blk'}, dimensions={0} | all-to-all | bytes 262144 | tf_op jit(solution)/shard_map/cond/branch_1_fun/all_to_all | solution.py:18
  132.8 3.3 %all-to-all-start.5 = ((bf16[4,2,64,128]{3,2,1,0:T(8,128)(2,1)}), bf16[4,2,64,128]{3,2,1,0:T(8,128)(2,1)S(1)}, u32[]{:S(2)}, u32[]{:S(2)}) async-start(bf16[4,2,64,128]{3,2,1,0:T(8,128)(2,1)} %broadcast_in_dim.6), calls=%async_computation.5 | async-start | bytes 262144 | tf_op jit(solution)/shard_map/all_to_all | solution.py:18
  136.2 4.7 %all-to-all-done.5 = bf16[4,2,64,128]{3,2,1,0:T(8,128)(2,1)S(1)} async-done(((bf16[4,2,64,128]{3,2,1,0:T(8,128)(2,1)}), bf16[4,2,64,128]{3,2,1,0:T(8,128)(2,1)S(1)}, u32[]{:S(2)}, u32[]{:S(2)}) %all-to-all-start.5) | async-done | bytes 131104 | tf_op jit(solution)/shard_map/all_to_all | solution.py:18
  140.9 5.0 %all-gather.2 = bf16[8,2,64,128]{3,2,1,0:T(8,128)(2,1)S(1)} all-gather(bf16[4,2,64,128]{3,2,1,0:T(8,128)(2,1)S(1)} %all-to-all-done.5), channel_id=4, replica_groups=mesh['x'=4,'z'=8,'core'=2,'blk'=8] {'core'}, dimensions={0}, use_global_device_ids=true | all-gather | bytes 393216 | tf_op jit(solution)/shard_map/all_gather | solution.py:178
  147.4 33.1 %all_to_all.35.parts = bf16[8,544,128]{2,1,0:T(8,128)(2,1)} all-to-all(bf16[8,544,128]{2,1,0:T(8,128)(2,1)S(1)} %bitcast.55), channel_id=1, replica_groups=mesh['x'=4,'z'=8,'core'=2,'blk'=8] {'blk'}, dimensions={0} | all-to-all | bytes 2228224 | tf_op jit(solution)/shard_map/all_to_all | solution.py:18
  180.5 2.1 %shard_map.51 = (f32[2,32,32]{2,1,0:T(8,128)}, f32[32,2048]{1,0:T(8,128)}) custom-call(bf16[8,544,128]{2,1,0:T(8,128)(2,1)} %all_to_all.35.parts, f32[32,2048]{1,0:T(8,128)} %right.1), custom_call_target="tpu_custom_call" | custom-call | tf_op jit(solution)/shard_map/pallas_call | solution.py:238
  (57 shorter events, 33.8 us)
Async XLA Ops:
  3.4 24.5 %collective-permute-start.7 = (bf16[8,128,256]{2,1,0:T(8,128)(2,1)}, bf16[8,128,256]{2,1,0:T(8,128)(2,1)}, u32[]{:S(2)}, u32[]{:S(2)}) collective-permute-start(bf16[8,128,256]{2,1,0:T(8,128)(2,1)} %slice_bitcast_fusion), channel_id=1, source_target_pairs={{8,0},{9,1},{10,2},{11,3},{12,4},{13,5},{14,6},{15,7}} | collective-permute-start | bytes 1572872 | tf_op jit(solution)/shard_map/ppermute | solution.py:162
  14.7 9.4 %all-to-all-start.3 = ((bf16[4,128,256]{2,1,0:T(8,128)(2,1)}), bf16[4,128,256]{2,1,0:T(8,128)(2,1)S(1)}, u32[]{:S(2)}, u32[]{:S(2)}) async-start(bf16[4,128,256]{2,1,0:T(8,128)(2,1)} %shard_map.50), calls=%async_computation.3 | async-start | bytes 524288 | tf_op jit(solution)/shard_map/all_to_all | solution.py:18
  24.0 9.7 %collective-permute-start.6 = (bf16[4,2,32,256]{3,2,1,0:T(8,128)(2,1)S(1)}, bf16[4,2,32,256]{3,2,1,0:T(8,128)(2,1)}, u32[]{:S(2)}, u32[]{:S(2)}) collective-permute-start(bf16[4,2,32,256]{3,2,1,0:T(8,128)(2,1)S(1)} %bitcast.46), channel_id=1, source_target_pairs={{112,0},{113,1},{114,2},{115,3},{116,4},{117,5},{118,6},{119,7},{1... | collective-permute-start | bytes 393224 | tf_op jit(solution)/shard_map/ppermute | solution.py:183
  25.3 12.3 %collective-permute-start.5 = (bf16[4,2,32,256]{3,2,1,0:T(8,128)(2,1)S(1)}, bf16[4,2,32,256]{3,2,1,0:T(8,128)(2,1)}, u32[]{:S(2)}, u32[]{:S(2)}) collective-permute-start(bf16[4,2,32,256]{3,2,1,0:T(8,128)(2,1)S(1)} %bitcast.47), channel_id=1, source_target_pairs={{96,0},{97,1},{98,2},{99,3},{100,4},{101,5},{102,6},{103,7},{104,8... | collective-permute-start | bytes 393224 | tf_op jit(solution)/shard_map/ppermute | solution.py:183
  26.6 12.3 %collective-permute-start.4 = (bf16[4,2,32,256]{3,2,1,0:T(8,128)(2,1)S(1)}, bf16[4,2,32,256]{3,2,1,0:T(8,128)(2,1)}, u32[]{:S(2)}, u32[]{:S(2)}) collective-permute-start(bf16[4,2,32,256]{3,2,1,0:T(8,128)(2,1)S(1)} %bitcast.48), channel_id=1, source_target_pairs={{80,0},{81,1},{82,2},{83,3},{84,4},{85,5},{86,6},{87,7},{88,8},{89... | collective-permute-start | bytes 393224 | tf_op jit(solution)/shard_map/ppermute | solution.py:183
  28.8 59.9 %collective-permute-start.10 = (bf16[8,128,256]{2,1,0:T(8,128)(2,1)}, bf16[8,128,256]{2,1,0:T(8,128)(2,1)S(1)}, u32[]{:S(2)}, u32[]{:S(2)}) collective-permute-start(bf16[8,128,256]{2,1,0:T(8,128)(2,1)} %fusion.6), channel_id=1, source_target_pairs={{0,384},{1,385},{2,386},{3,387},{4,388},{5,389},{6,390},{7,391},{8... | collective-permute-start | bytes 1572872 | tf_op jit(solution)/shard_map/ppermute | solution.py:165
  31.6 57.1 %collective-permute-start.9 = (bf16[8,128,256]{2,1,0:T(8,128)(2,1)}, bf16[8,128,256]{2,1,0:T(8,128)(2,1)}, u32[]{:S(2)}, u32[]{:S(2)}) collective-permute-start(bf16[8,128,256]{2,1,0:T(8,128)(2,1)} %fusion.6), channel_id=1, source_target_pairs={{0,256},{1,257},{2,258},{3,259},{4,260},{5,261},{6,262},{7,263},{8... | collective-permute-start | bytes 1572872 | tf_op jit(solution)/shard_map/ppermute | solution.py:165
  33.7 55.0 %collective-permute-start.8 = (bf16[8,128,256]{2,1,0:T(8,128)(2,1)}, bf16[8,128,256]{2,1,0:T(8,128)(2,1)}, u32[]{:S(2)}, u32[]{:S(2)}) collective-permute-start(bf16[8,128,256]{2,1,0:T(8,128)(2,1)} %fusion.6), channel_id=1, source_target_pairs={{0,128},{1,129},{2,130},{3,131},{4,132},{5,133},{6,134},{7,135},{8... | collective-permute-start | bytes 1572872 | tf_op jit(solution)/shard_map/ppermute | solution.py:165
  37.6 9.6 %collective-permute-start.3 = (bf16[4,2,32,256]{3,2,1,0:T(8,128)(2,1)S(1)}, bf16[4,2,32,256]{3,2,1,0:T(8,128)(2,1)S(1)}, u32[]{:S(2)}, u32[]{:S(2)}) collective-permute-start(bf16[4,2,32,256]{3,2,1,0:T(8,128)(2,1)S(1)} %bitcast.49), channel_id=1, source_target_pairs={{64,0},{65,1},{66,2},{67,3},{68,4},{69,5},{70,6},{71,7},{72,8},{73... | collective-permute-start | bytes 393224 | tf_op jit(solution)/shard_map/ppermute | solution.py:183
  38.9 9.6 %collective-permute-start.2 = (bf16[4,2,32,256]{3,2,1,0:T(8,128)(2,1)S(1)}, bf16[4,2,32,256]{3,2,1,0:T(8,128)(2,1)S(1)}, u32[]{:S(2)}, u32[]{:S(2)}) collective-permute-start(bf16[4,2,32,256]{3,2,1,0:T(8,128)(2,1)S(1)} %bitcast.50), channel_id=1, source_target_pairs={{48,0},{49,1},{50,2},{51,3},{52,4},{53,5},{54,6},{55,7},{56,8},{57... | collective-permute-start | bytes 393224 | tf_op jit(solution)/shard_map/ppermute | solution.py:183
  47.2 23.9 %collective-permute-start.1 = (bf16[4,2,32,256]{3,2,1,0:T(8,128)(2,1)S(1)}, bf16[4,2,32,256]{3,2,1,0:T(8,128)(2,1)S(1)}, u32[]{:S(2)}, u32[]{:S(2)}) collective-permute-start(bf16[4,2,32,256]{3,2,1,0:T(8,128)(2,1)S(1)} %bitcast.51), channel_id=1, source_target_pairs={{32,0},{33,1},{34,2},{35,3},{36,4},{37,5},{38,6},{39,7},{40,8},{41... | collective-permute-start | bytes 393224 | tf_op jit(solution)/shard_map/ppermute | solution.py:183
  48.5 22.6 %collective-permute-start = (bf16[4,2,32,256]{3,2,1,0:T(8,128)(2,1)S(1)}, bf16[4,2,32,256]{3,2,1,0:T(8,128)(2,1)}, u32[]{:S(2)}, u32[]{:S(2)}) collective-permute-start(bf16[4,2,32,256]{3,2,1,0:T(8,128)(2,1)S(1)} %bitcast.52), channel_id=1, source_target_pairs={{16,0},{17,1},{18,2},{19,3},{20,4},{21,5},{22,6},{23,7},{24,8},{25... | collective-permute-start | bytes 393224 | tf_op jit(solution)/shard_map/ppermute | solution.py:183
  50.4 14.5 %all-to-all-start.4 = ((bf16[8,8,256]{2,1,0:T(8,128)(2,1)}), bf16[8,8,256]{2,1,0:T(8,128)(2,1)S(1)}, u32[]{:S(2)}, u32[]{:S(2)}) async-start(bf16[8,8,256]{2,1,0:T(8,128)(2,1)} %slice_bitcast_fusion.2), calls=%async_computation.4 | async-start | bytes 65536 | tf_op jit(solution)/shard_map/all_to_all | solution.py:18
  120.7 7.7 %collective-permute-start.17 = (bf16[2,64,128]{2,1,0:T(8,128)(2,1)S(1)}, bf16[2,64,128]{2,1,0:T(8,128)(2,1)S(1)}, u32[]{:S(2)}, u32[]{:S(2)}) collective-permute-start(bf16[2,64,128]{2,1,0:T(8,128)(2,1)S(1)} %get-tuple-element.99), channel_id=1, source_target_pairs={{0,112},{1,113},{2,114},{3,115},{4,116},{5,117},{6,118},{7,119},{8... | collective-permute-start | bytes 98312 | tf_op jit(solution)/shard_map/ppermute | solution.py:219
  122.0 7.8 %collective-permute-start.16 = (bf16[2,64,128]{2,1,0:T(8,128)(2,1)S(1)}, bf16[2,64,128]{2,1,0:T(8,128)(2,1)S(1)}, u32[]{:S(2)}, u32[]{:S(2)}) collective-permute-start(bf16[2,64,128]{2,1,0:T(8,128)(2,1)S(1)} %get-tuple-element.99), channel_id=1, source_target_pairs={{0,96},{1,97},{2,98},{3,99},{4,100},{5,101},{6,102},{7,103},{8,104... | collective-permute-start | bytes 98312 | tf_op jit(solution)/shard_map/ppermute | solution.py:219
  123.3 7.8 %collective-permute-start.15 = (bf16[2,64,128]{2,1,0:T(8,128)(2,1)S(1)}, bf16[2,64,128]{2,1,0:T(8,128)(2,1)S(1)}, u32[]{:S(2)}, u32[]{:S(2)}) collective-permute-start(bf16[2,64,128]{2,1,0:T(8,128)(2,1)S(1)} %get-tuple-element.99), channel_id=1, source_target_pairs={{0,80},{1,81},{2,82},{3,83},{4,84},{5,85},{6,86},{7,87},{8,88},{9,... | collective-permute-start | bytes 98312 | tf_op jit(solution)/shard_map/ppermute | solution.py:219
  124.6 6.5 %collective-permute-start.14 = (bf16[2,64,128]{2,1,0:T(8,128)(2,1)S(1)}, bf16[2,64,128]{2,1,0:T(8,128)(2,1)S(1)}, u32[]{:S(2)}, u32[]{:S(2)}) collective-permute-start(bf16[2,64,128]{2,1,0:T(8,128)(2,1)S(1)} %get-tuple-element.99), channel_id=1, source_target_pairs={{0,64},{1,65},{2,66},{3,67},{4,68},{5,69},{6,70},{7,71},{8,72},{9,... | collective-permute-start | bytes 98312 | tf_op jit(solution)/shard_map/ppermute | solution.py:219
  125.9 5.3 %collective-permute-start.13 = (bf16[2,64,128]{2,1,0:T(8,128)(2,1)S(1)}, bf16[2,64,128]{2,1,0:T(8,128)(2,1)S(1)}, u32[]{:S(2)}, u32[]{:S(2)}) collective-permute-start(bf16[2,64,128]{2,1,0:T(8,128)(2,1)S(1)} %get-tuple-element.99), channel_id=1, source_target_pairs={{0,48},{1,49},{2,50},{3,51},{4,52},{5,53},{6,54},{7,55},{8,56},{9,... | collective-permute-start | bytes 98312 | tf_op jit(solution)/shard_map/ppermute | solution.py:219
  128.3 18.2 %copy-start = (bf16[2048,256]{1,0:T(8,128)(2,1)S(1)}, bf16[2048,256]{1,0:T(8,128)(2,1)}, u32[]{:S(2)}) copy-start(bf16[2048,256]{1,0:T(8,128)(2,1)} %get-tuple-element.92) | copy-start | bytes 3145732
  128.4 2.8 %collective-permute-start.12 = (bf16[2,64,128]{2,1,0:T(8,128)(2,1)S(1)}, bf16[2,64,128]{2,1,0:T(8,128)(2,1)S(1)}, u32[]{:S(2)}, u32[]{:S(2)}) collective-permute-start(bf16[2,64,128]{2,1,0:T(8,128)(2,1)S(1)} %get-tuple-element.99), channel_id=1, source_target_pairs={{0,32},{1,33},{2,34},{3,35},{4,36},{5,37},{6,38},{7,39},{8,40},{9,... | collective-permute-start | bytes 98312 | tf_op jit(solution)/shard_map/ppermute | solution.py:219
  129.8 2.3 %collective-permute-start.11 = (bf16[2,64,128]{2,1,0:T(8,128)(2,1)S(1)}, bf16[2,64,128]{2,1,0:T(8,128)(2,1)S(1)}, u32[]{:S(2)}, u32[]{:S(2)}) collective-permute-start(bf16[2,64,128]{2,1,0:T(8,128)(2,1)S(1)} %get-tuple-element.99), channel_id=1, source_target_pairs={{0,16},{1,17},{2,18},{3,19},{4,20},{5,21},{6,22},{7,23},{8,24},{9,... | collective-permute-start | bytes 98312 | tf_op jit(solution)/shard_map/ppermute | solution.py:219
  132.8 8.1 %all-to-all-start.5 = ((bf16[4,2,64,128]{3,2,1,0:T(8,128)(2,1)}), bf16[4,2,64,128]{3,2,1,0:T(8,128)(2,1)S(1)}, u32[]{:S(2)}, u32[]{:S(2)}) async-start(bf16[4,2,64,128]{3,2,1,0:T(8,128)(2,1)} %broadcast_in_dim.6), calls=%async_computation.5 | async-start | bytes 262144 | tf_op jit(solution)/shard_map/all_to_all | solution.py:18
